TPU v7x, 256 devices: a whole 4x4x8 slice. The times are simulated.
256 devices in a mesh: sample: 4 (over z_lo, core), space: 64 (over y, z_hi, x).
Axes of the slice: x: 4, y: 4, z: 8 (z_hi: 4, z_lo: 2; z = z_hi * 2 + z_lo), core: 2. Of those that a mesh axis runs over, the one named last changes fastest.
Arguments:
- acts: bfloat16 [8, 64, 16, 8, 8, 128], P('sample', 'space'), may hold values from -6 to 6
- weight: float32 [3456, 128], P('space'), may hold values from -0.109375 to 0.109375
- moment: float32 [3456, 128], P('space'), may hold values from -3 to 3
- second: float32 [3456, 128], P('space'), may hold values from 0.05 to 2
- cotangent: bfloat16 [8, 64, 16, 8, 8, 128], P('sample', 'space'), may hold values from -6 to 6
Outputs:
- output: bfloat16 [8, 64, 16, 8, 8, 128], P('sample', 'space')
- input_grad: bfloat16 [8, 64, 16, 8, 8, 128], P('sample', 'space')
- weight_grad: float32 [3456, 128], P('space')
- new_weight: float32 [3456, 128], P('space')
- new_moment: float32 [3456, 128], P('space')
- new_second: float32 [3456, 128], P('space')
All inputs are finite; a program needn't handle non-finite values.
Results may differ from a plain program's by a relative error of at most 0.0062.
Values may be sent and summed in bfloat16 or wider, within the bound.
No kernel may reach another device: no remote copies, remote signals or barrier semaphores. Data moves between devices by JAX's collectives and lax.ppermute only.
A program may use at most 64 MiB of HBM per device.

v0:
```python
import jax
import jax.numpy as jnp
from jax import lax
from jax.sharding import PartitionSpec as P

GY = 2
GZ = 4


root_coef = 0.7978845608
cubic_coef = 0.044715


def shifted(value, axis, by):
    devices = lax.axis_size(axis)
    pairs = [(i, i + by) for i in range(devices) if 0 <= i + by < devices]
    return lax.ppermute(value, axis, pairs)


def joined_along(parts, dim):
    shape = list(parts.shape[1:])
    shape[dim] *= parts.shape[0]
    return jnp.moveaxis(parts, 0, dim).reshape(shape)


def copy_for_each(value, axis):
    copies = jnp.broadcast_to(value, (lax.axis_size(axis), *value.shape))
    return lax.all_to_all(copies, axis, split_axis=0, concat_axis=0, tiled=True)


def gathered_copies(value, axis, dim):
    return joined_along(copy_for_each(value, axis), dim)


def cut_along(value, dim, devices):
    shape = value.shape
    parts = value.reshape(*shape[:dim], devices, shape[dim] // devices, *shape[dim + 1 :])
    return jnp.moveaxis(parts, dim, 0)


def summed_on_arrival(value, axis, dim):
    parts = cut_along(value, dim, lax.axis_size(axis))
    arrived = lax.all_to_all(parts, axis, split_axis=0, concat_axis=0, tiled=True)
    return arrived.sum(axis=0)


def of_everyone(value, axis):
    return copy_for_each(value, axis).sum(axis=0)


def convolve(field, kernel):
    return lax.conv_general_dilated(
        field,
        kernel,
        (1, 1, 1),
        "VALID",
        dimension_numbers=("NDHWC", "DHWIO", "NDHWC"),
        preferred_element_type=jnp.float32,
    )


def activate(pre):
    inner = root_coef * (pre + cubic_coef * pre * pre * pre)
    tval = jnp.tanh(inner)
    value = 0.5 * pre * (1.0 + tval)
    slope = 0.5 * (1.0 + tval) + 0.5 * pre * (1.0 - tval * tval) * root_coef * (
        1.0 + 3.0 * cubic_coef * pre * pre
    )
    return (value, slope)


def extend(field):
    place = lax.axis_index("space")
    groups = lax.axis_size("space") // (GY * GZ)
    coord_z = place % GZ
    coord_y = place // GZ % GY
    coord_x = place // (GZ * GY)
    for dim, stride, coord, count in (
        (3, 1, coord_z, GZ),
        (2, GZ, coord_y, GY),
        (1, GY * GZ, coord_x, groups),
    ):
        length = field.shape[dim]
        first_layer = lax.slice_in_dim(field, 0, 1, 1, dim)
        last_layer = lax.slice_in_dim(field, length - 1, length, 1, dim)
        below = shifted(last_layer, "space", stride)
        above = shifted(first_layer, "space", -stride)
        below = jnp.where(coord > 0, below, jnp.zeros_like(below))
        above = jnp.where(coord < count - 1, above, jnp.zeros_like(above))
        field = jnp.concatenate([below, field, above], dim)
    return field


def kernel_terms(padded, grad_pre):
    nx, ny, nz = (grad_pre.shape[1], grad_pre.shape[2], grad_pre.shape[3])
    terms = []
    for kx in range(3):
        for ky in range(3):
            for kz in range(3):
                window = padded[:, kx : kx + nx, ky : ky + ny, kz : kz + nz, :]
                terms.append(
                    lax.dot_general(
                        window,
                        grad_pre,
                        (((0, 1, 2, 3), (0, 1, 2, 3)), ((), ())),
                        preferred_element_type=jnp.float32,
                    )
                )
    stacked = jnp.stack(terms, 0)
    return stacked.reshape(27 * stacked.shape[1], stacked.shape[2])


def local(acts, weight, moment, second, cotangent):
    field = acts[:, 0]
    grad_out = cotangent[:, 0]
    channels = weight.shape[1]
    rows_bf = weight.astype(jnp.bfloat16)
    whole = gathered_copies(rows_bf, "space", 0)
    kernel = whole.reshape(3, 3, 3, channels, channels)
    padded = extend(field)
    pre = convolve(padded, kernel)
    value, slope = activate(pre)
    output = value.astype(jnp.bfloat16)
    grad_pre = (grad_out.astype(jnp.float32) * slope).astype(jnp.bfloat16)
    flipped = jnp.flip(kernel, (0, 1, 2)).transpose(0, 1, 2, 4, 3)
    grad_padded = extend(grad_pre)
    input_grad = convolve(grad_padded, flipped).astype(jnp.bfloat16)
    total = (
        field.shape[0]
        * lax.axis_size("sample")
        * lax.axis_size("space")
        * field.shape[1]
        * field.shape[2]
        * field.shape[3]
    )
    local_terms = kernel_terms(padded, grad_pre) * float(total) ** (-0.5)
    owned = summed_on_arrival(local_terms, "space", 0)
    weight_grad = of_everyone(owned, "sample")
    new_moment = 0.9 * moment + 0.1 * weight_grad
    new_second = 0.999 * second + 0.001 * weight_grad * weight_grad
    first_fix = 1.0 - 0.9**10
    second_fix = 1.0 - 0.999**10
    new_weight = weight - 0.001 * (new_moment / first_fix) / (
        jnp.sqrt(new_second / second_fix) + 1e-08
    )
    return (output[:, None], input_grad[:, None], weight_grad, new_weight, new_moment, new_second)


def solution(mesh):
    in_specs = (
        P("sample", "space", None, None, None, None),
        P("space", None),
        P("space", None),
        P("space", None),
        P("sample", "space", None, None, None, None),
    )
    out_specs = (
        P("sample", "space", None, None, None, None),
        P("sample", "space", None, None, None, None),
        P("space", None),
        P("space", None),
        P("space", None),
        P("space", None),
    )
    return jax.shard_map(local, mesh=mesh, in_specs=in_specs, out_specs=out_specs, check_vma=False)
```

profile of v0, /device:TPU:25, one launch (start us, length us, event | category | flops | bytes accessed | tf_op | source)
XLA Modules:
  0.0 212.3 jit_solution(5376992157897566695)
XLA Ops:
  2.1 10.3 %collective-permute-start.1 = (bf16[2,16,8,1,128]{4,3,2,1,0:T(2,128)(2,1)S(1)}, bf16[2,16,8,1,128]{4,3,2,1,0:T(2,128)(2,1)S(1)}, u32[]{:S(2)}, u32[]{:S(2)}) collective-permute-start(bf16[2,16,8,1,128]{4,3,2,1,0:T(2,128)(2,1)S(1)} %get-tuple-element.56), channel_id=1, source_target_pairs={{1,0},{2,1},{3,2},{4,3},{5,4},{6,5},{7,6},{8,7},{9,8},{10,9},{11,1... | collective-permute-start | bytes 196616 | tf_op jit(solution)/shard_map/ppermute | solution.py:17
  12.4 1.9 collective-permute-start
  14.7 12.4 %collective-permute-done = bf16[2,16,8,1,128]{4,3,2,1,0:T(2,128)(2,1)S(1)} collective-permute-done((bf16[2,16,8,1,128]{4,3,2,1,0:T(2,128)(2,1)S(1)}, bf16[2,16,8,1,128]{4,3,2,1,0:T(2,128)(2,1)S(1)}, u32[]{:S(2)}, u32[]{:S(2)}) %collective-permute-start) | collective-permute-done | bytes 65568 | tf_op jit(solution)/shard_map/ppermute | solution.py:17
  28.3 2.1 collective-permute-start.3
  31.4 6.8 %all-to-all-start = ((bf16[64,54,128]{2,1,0:T(8,128)(2,1)}), bf16[64,54,128]{2,1,0:T(8,128)(2,1)S(1)}, u32[]{:S(2)}, u32[]{:S(2)}) async-start(bf16[64,54,128]{2,1,0:T(8,128)(2,1)} %broadcast_in_dim.12), calls=%async_computation | async-start | bytes 1835008 | tf_op jit(solution)/shard_map/all_to_all | solution.py:28
  38.2 4.0 %collective-permute-start.2 = (bf16[2,16,1,10,128]{4,3,2,1,0:T(8,128)(2,1)S(1)}, bf16[2,16,1,10,128]{4,3,2,1,0:T(8,128)(2,1)S(1)}, u32[]{:S(2)}, u32[]{:S(2)}) collective-permute-start(bf16[2,16,1,10,128]{4,3,2,1,0:T(8,128)(2,1)S(1)} %get-tuple-element.51), channel_id=1, source_target_pairs={{0,4},{1,5},{2,6},{3,7},{4,8},{5,9},{6,10},{7,11},{8,12},{9,13},{1... | collective-permute-start | bytes 245768 | tf_op jit(solution)/shard_map/ppermute | solution.py:17
  42.3 23.5 %collective-permute-done.2 = bf16[2,16,1,10,128]{4,3,2,1,0:T(8,128)(2,1)S(1)} collective-permute-done((bf16[2,16,1,10,128]{4,3,2,1,0:T(8,128)(2,1)S(1)}, bf16[2,16,1,10,128]{4,3,2,1,0:T(8,128)(2,1)S(1)}, u32[]{:S(2)}, u32[]{:S(2)}) %collective-permute-start.2) | collective-permute-done | bytes 81952 | tf_op jit(solution)/shard_map/ppermute | solution.py:17
  65.9 2.6 %collective-permute-start.5 = (bf16[2,1,10,10,128]{4,3,2,1,0:T(8,128)(2,1)S(1)}, bf16[2,1,10,10,128]{4,3,2,1,0:T(8,128)(2,1)S(1)}, u32[]{:S(2)}, u32[]{:S(2)}) collective-permute-start(bf16[2,1,10,10,128]{4,3,2,1,0:T(8,128)(2,1)S(1)} %get-tuple-element.46), channel_id=1, source_target_pairs={{8,0},{9,1},{10,2},{11,3},{12,4},{13,5},{14,6},{15,7},{16,8},{17,9... | collective-permute-start | bytes 153608 | tf_op jit(solution)/shard_map/ppermute | solution.py:17
  68.6 2.8 %pad_maximum_fusion.3 = (bf16[2,16,9,10,128]{4,3,2,1,0:T(8,128)(2,1)}, bf16[2,16,9,10,128]{4,3,2,1,0:T(8,128)(2,1)}) fusion(bf16[2,16,1,10,128]{4,3,2,1,0:T(8,128)(2,1)S(1)} %broadcast_select_fusion.5, bf16[2,16,8,1,128]{4,3,2,1,0:T(2,128)(2,1)S(1)} %broadcast_select_fusion.1, bf16[2,16,8,8,128]{4,3,2,1,0:T(8,128)(2,1)S(1)} %bitcast.264, ...), kind=kLoop, calls=%fused_computation.9 | loop fusion | flops 5898240 | bytes 2293760 | tf_op jit(solution)/shard_map/concatenate | solution.py:90
  71.3 6.5 %collective-permute-start.4 = (bf16[2,1,10,10,128]{4,3,2,1,0:T(8,128)(2,1)S(1)}, bf16[2,1,10,10,128]{4,3,2,1,0:T(8,128)(2,1)S(1)}, u32[]{:S(2)}, u32[]{:S(2)}) collective-permute-start(bf16[2,1,10,10,128]{4,3,2,1,0:T(8,128)(2,1)S(1)} %get-tuple-element.45), channel_id=1, source_target_pairs={{0,8},{1,9},{2,10},{3,11},{4,12},{5,13},{6,14},{7,15},{8,16},{9,17... | collective-permute-start | bytes 153608 | tf_op jit(solution)/shard_map/ppermute | solution.py:17
  77.9 3.5 %collective-permute-done.4 = bf16[2,1,10,10,128]{4,3,2,1,0:T(8,128)(2,1)S(1)} collective-permute-done((bf16[2,1,10,10,128]{4,3,2,1,0:T(8,128)(2,1)S(1)}, bf16[2,1,10,10,128]{4,3,2,1,0:T(8,128)(2,1)S(1)}, u32[]{:S(2)}, u32[]{:S(2)}) %collective-permute-start.4) | collective-permute-done | bytes 51232 | tf_op jit(solution)/shard_map/ppermute | solution.py:17
  82.2 2.6 %pad_maximum_fusion.2 = (bf16[2,17,10,10,128]{4,3,2,1,0:T(8,128)(2,1)}, bf16[2,17,10,10,128]{4,3,2,1,0:T(8,128)(2,1)}) fusion(bf16[2,1,10,10,128]{4,3,2,1,0:T(8,128)(2,1)S(1)} %broadcast_select_fusion.9, bf16[2,16,1,10,128]{4,3,2,1,0:T(8,128)(2,1)S(1)} %broadcast_select_fusion.5, bf16[2,16,8,1,128]{4,3,2,1,0:T(2,128)(2,1)S(1)} %broadcast_select_fusion.1, ...), kind=kLoop, calls=%fused_computation.5 | loop fusion | flops 10444800 | bytes 2662400 | tf_op jit(solution)/shard_map/concatenate | solution.py:90
  86.0 7.3 %fusion.36 = f32[2,16,8,8,128]{4,0,3,2,1:T(2,128)S(1)} fusion(bf16[3,3,3,128,128]{4,3,2,1,0:T(8,128)(2,1)} %reshape_reshape.3, bf16[2,18,10,10,128]{4,3,2,1,0:T(8,128)(2,1)S(1)} %pad_maximum_fusion), kind=kOutput, calls=%fused_computation.73 | convolution fusion | flops 1811939328 | bytes 2854912 | tf_op jit(solution)/shard_map/conv_general_dilated | solution.py:52
  109.2 9.8 %all-to-all-start.1 = ((f32[64,54,128]{2,1,0:T(8,128)}), f32[64,54,128]{2,1,0:T(8,128)S(1)}, u32[]{:S(2)}, u32[]{:S(2)}) async-start(f32[64,54,128]{2,1,0:T(8,128)} %mul.106), calls=%async_computation.1 | async-start | bytes 3670016 | tf_op jit(solution)/shard_map/all_to_all | solution.py:43
  119.2 7.6 %collective-permute-start.7 = (bf16[2,16,8,1,128]{4,3,2,1,0:T(2,128)(2,1)S(1)}, bf16[2,16,8,1,128]{4,3,2,1,0:T(2,128)(2,1)S(1)}, u32[]{:S(2)}, u32[]{:S(2)}) collective-permute-start(bf16[2,16,8,1,128]{4,3,2,1,0:T(2,128)(2,1)S(1)} %get-tuple-element.54), channel_id=1, source_target_pairs={{1,0},{2,1},{3,2},{4,3},{5,4},{6,5},{7,6},{8,7},{9,8},{10,9},{11,1... | collective-permute-start | bytes 196616 | tf_op jit(solution)/shard_map/ppermute | solution.py:17
  126.8 1.9 collective-permute-start.6
  128.7 5.0 %collective-permute-done.7 = bf16[2,16,8,1,128]{4,3,2,1,0:T(2,128)(2,1)S(1)} collective-permute-done((bf16[2,16,8,1,128]{4,3,2,1,0:T(2,128)(2,1)S(1)}, bf16[2,16,8,1,128]{4,3,2,1,0:T(2,128)(2,1)S(1)}, u32[]{:S(2)}, u32[]{:S(2)}) %collective-permute-start.7) | collective-permute-done | bytes 65568 | tf_op jit(solution)/shard_map/ppermute | solution.py:17
  133.9 20.7 %collective-permute-done.6 = bf16[2,16,8,1,128]{4,3,2,1,0:T(2,128)(2,1)S(1)} collective-permute-done((bf16[2,16,8,1,128]{4,3,2,1,0:T(2,128)(2,1)S(1)}, bf16[2,16,8,1,128]{4,3,2,1,0:T(2,128)(2,1)S(1)}, u32[]{:S(2)}, u32[]{:S(2)}) %collective-permute-start.6) | collective-permute-done | bytes 65568 | tf_op jit(solution)/shard_map/ppermute | solution.py:17
  154.8 5.1 %collective-permute-start.9 = (bf16[2,16,1,10,128]{4,3,2,1,0:T(8,128)(2,1)S(1)}, bf16[2,16,1,10,128]{4,3,2,1,0:T(8,128)(2,1)S(1)}, u32[]{:S(2)}, u32[]{:S(2)}) collective-permute-start(bf16[2,16,1,10,128]{4,3,2,1,0:T(8,128)(2,1)S(1)} %get-tuple-element.50), channel_id=1, source_target_pairs={{4,0},{5,1},{6,2},{7,3},{8,4},{9,5},{10,6},{11,7},{12,8},{13,9},{1... | collective-permute-start | bytes 245768 | tf_op jit(solution)/shard_map/ppermute | solution.py:17
  162.7 5.9 %collective-permute-done.8 = bf16[2,16,1,10,128]{4,3,2,1,0:T(8,128)(2,1)S(1)} collective-permute-done((bf16[2,16,1,10,128]{4,3,2,1,0:T(8,128)(2,1)S(1)}, bf16[2,16,1,10,128]{4,3,2,1,0:T(8,128)(2,1)S(1)}, u32[]{:S(2)}, u32[]{:S(2)}) %collective-permute-start.8) | collective-permute-done | bytes 81952 | tf_op jit(solution)/shard_map/ppermute | solution.py:17
  170.7 7.3 %collective-permute-start.10 = (bf16[2,1,10,10,128]{4,3,2,1,0:T(8,128)(2,1)S(1)}, bf16[2,1,10,10,128]{4,3,2,1,0:T(8,128)(2,1)S(1)}, u32[]{:S(2)}, u32[]{:S(2)}) collective-permute-start(bf16[2,1,10,10,128]{4,3,2,1,0:T(8,128)(2,1)S(1)} %get-tuple-element.41), channel_id=1, source_target_pairs={{0,8},{1,9},{2,10},{3,11},{4,12},{5,13},{6,14},{7,15},{8,16},{9,17... | collective-permute-start | bytes 153608 | tf_op jit(solution)/shard_map/ppermute | solution.py:17
  178.2 3.5 %collective-permute-done.10 = bf16[2,1,10,10,128]{4,3,2,1,0:T(8,128)(2,1)S(1)} collective-permute-done((bf16[2,1,10,10,128]{4,3,2,1,0:T(8,128)(2,1)S(1)}, bf16[2,1,10,10,128]{4,3,2,1,0:T(8,128)(2,1)S(1)}, u32[]{:S(2)}, u32[]{:S(2)}) %collective-permute-start.10) | collective-permute-done | bytes 51232 | tf_op jit(solution)/shard_map/ppermute | solution.py:17
  184.5 18.6 %all-to-all-start.2 = ((f32[4,54,128]{2,1,0:T(8,128)}), f32[4,54,128]{2,1,0:T(8,128)S(1)}, u32[]{:S(2)}, u32[]{:S(2)}) async-start(f32[4,54,128]{2,1,0:T(8,128)} %broadcast_in_dim.15), calls=%async_computation.2 | async-start | bytes 229376 | tf_op jit(solution)/shard_map/all_to_all | solution.py:28
  203.2 7.5 %fusion = bf16[2,1,16,8,8,128]{5,0,4,3,2,1:T(2,128)(2,1)S(1)} fusion(bf16[3,3,3,128,128]{4,3,2,1,0:T(8,128)(2,1)S(1)} %copy-done.5, bf16[2,18,10,10,128]{4,3,2,1,0:T(8,128)(2,1)} %pad_maximum_fusion.1), kind=kOutput, calls=%fused_computation.7 | convolution fusion | flops 1812201472 | bytes 2330624 | tf_op jit(solution)/shard_map/conv_general_dilated | solution.py:52
  (90 shorter events, 31.7 us)
Async XLA Ops:
  0.6 29.7 %copy-start.7 = (f32[54,128]{1,0:T(8,128)S(1)}, f32[54,128]{1,0:T(8,128)}, u32[]{:S(2)}) copy-start(f32[54,128]{1,0:T(8,128)} %param.6) | copy-start | bytes 82948
  2.1 12.5 %collective-permute-start.1 = (bf16[2,16,8,1,128]{4,3,2,1,0:T(2,128)(2,1)S(1)}, bf16[2,16,8,1,128]{4,3,2,1,0:T(2,128)(2,1)S(1)}, u32[]{:S(2)}, u32[]{:S(2)}) collective-permute-start(bf16[2,16,8,1,128]{4,3,2,1,0:T(2,128)(2,1)S(1)} %get-tuple-element.56), channel_id=1, source_target_pairs={{1,0},{2,1},{3,2},{4,3},{5,4},{6,5},{7,6},{8,7},{9,8},{10,9},{11,1... | collective-permute-start | bytes 196616 | tf_op jit(solution)/shard_map/ppermute | solution.py:17
  12.4 14.7 %collective-permute-start = (bf16[2,16,8,1,128]{4,3,2,1,0:T(2,128)(2,1)S(1)}, bf16[2,16,8,1,128]{4,3,2,1,0:T(2,128)(2,1)S(1)}, u32[]{:S(2)}, u32[]{:S(2)}) collective-permute-start(bf16[2,16,8,1,128]{4,3,2,1,0:T(2,128)(2,1)S(1)} %get-tuple-element.55), channel_id=1, source_target_pairs={{0,1},{1,2},{2,3},{3,4},{4,5},{5,6},{6,7},{7,8},{8,9},{9,10},{10,1... | collective-permute-start | bytes 196616 | tf_op jit(solution)/shard_map/ppermute | solution.py:17
  28.2 37.6 %copy-start = (bf16[2,1,16,8,8,128]{5,4,3,2,1,0:T(8,128)(2,1)S(1)}, bf16[2,1,16,8,8,128]{5,4,3,2,1,0:T(8,128)(2,1)}, u32[]{:S(2)}) copy-start(bf16[2,1,16,8,8,128]{5,4,3,2,1,0:T(8,128)(2,1)} %param.5) | copy-start | bytes 1572868
  28.3 14.0 %collective-permute-start.3 = (bf16[2,16,1,10,128]{4,3,2,1,0:T(8,128)(2,1)S(1)}, bf16[2,16,1,10,128]{4,3,2,1,0:T(8,128)(2,1)S(1)}, u32[]{:S(2)}, u32[]{:S(2)}) collective-permute-start(bf16[2,16,1,10,128]{4,3,2,1,0:T(8,128)(2,1)S(1)} %get-tuple-element.52), channel_id=1, source_target_pairs={{4,0},{5,1},{6,2},{7,3},{8,4},{9,5},{10,6},{11,7},{12,8},{13,9},{1... | collective-permute-start | bytes 245768 | tf_op jit(solution)/shard_map/ppermute | solution.py:17
  31.4 53.4 %all-to-all-start = ((bf16[64,54,128]{2,1,0:T(8,128)(2,1)}), bf16[64,54,128]{2,1,0:T(8,128)(2,1)S(1)}, u32[]{:S(2)}, u32[]{:S(2)}) async-start(bf16[64,54,128]{2,1,0:T(8,128)(2,1)} %broadcast_in_dim.12), calls=%async_computation | async-start | bytes 1835008 | tf_op jit(solution)/shard_map/all_to_all | solution.py:28
  38.2 27.5 %collective-permute-start.2 = (bf16[2,16,1,10,128]{4,3,2,1,0:T(8,128)(2,1)S(1)}, bf16[2,16,1,10,128]{4,3,2,1,0:T(8,128)(2,1)S(1)}, u32[]{:S(2)}, u32[]{:S(2)}) collective-permute-start(bf16[2,16,1,10,128]{4,3,2,1,0:T(8,128)(2,1)S(1)} %get-tuple-element.51), channel_id=1, source_target_pairs={{0,4},{1,5},{2,6},{3,7},{4,8},{5,9},{6,10},{7,11},{8,12},{9,13},{1... | collective-permute-start | bytes 245768 | tf_op jit(solution)/shard_map/ppermute | solution.py:17
  65.9 12.0 %collective-permute-start.5 = (bf16[2,1,10,10,128]{4,3,2,1,0:T(8,128)(2,1)S(1)}, bf16[2,1,10,10,128]{4,3,2,1,0:T(8,128)(2,1)S(1)}, u32[]{:S(2)}, u32[]{:S(2)}) collective-permute-start(bf16[2,1,10,10,128]{4,3,2,1,0:T(8,128)(2,1)S(1)} %get-tuple-element.46), channel_id=1, source_target_pairs={{8,0},{9,1},{10,2},{11,3},{12,4},{13,5},{14,6},{15,7},{16,8},{17,9... | collective-permute-start | bytes 153608 | tf_op jit(solution)/shard_map/ppermute | solution.py:17
  71.3 10.1 %collective-permute-start.4 = (bf16[2,1,10,10,128]{4,3,2,1,0:T(8,128)(2,1)S(1)}, bf16[2,1,10,10,128]{4,3,2,1,0:T(8,128)(2,1)S(1)}, u32[]{:S(2)}, u32[]{:S(2)}) collective-permute-start(bf16[2,1,10,10,128]{4,3,2,1,0:T(8,128)(2,1)S(1)} %get-tuple-element.45), channel_id=1, source_target_pairs={{0,8},{1,9},{2,10},{3,11},{4,12},{5,13},{6,14},{7,15},{8,16},{9,17... | collective-permute-start | bytes 153608 | tf_op jit(solution)/shard_map/ppermute | solution.py:17
  86.0 7.4 %copy-start.6 = (bf16[2,1,16,8,8,128]{5,4,3,2,1,0:T(8,128)(2,1)S(1)}, bf16[2,1,16,8,8,128]{5,4,3,2,1,0:T(8,128)(2,1)}, u32[]{:S(2)}) copy-start(bf16[2,1,16,8,8,128]{5,4,3,2,1,0:T(8,128)(2,1)} %param.9) | copy-start | bytes 1572868
  93.3 1.6 copy-start.2
  97.8 1.3 copy-start.4
  103.0 1.3 copy-start.1
  109.2 74.5 %all-to-all-start.1 = ((f32[64,54,128]{2,1,0:T(8,128)}), f32[64,54,128]{2,1,0:T(8,128)S(1)}, u32[]{:S(2)}, u32[]{:S(2)}) async-start(f32[64,54,128]{2,1,0:T(8,128)} %mul.106), calls=%async_computation.1 | async-start | bytes 3670016 | tf_op jit(solution)/shard_map/all_to_all | solution.py:43
  119.2 14.5 %collective-permute-start.7 = (bf16[2,16,8,1,128]{4,3,2,1,0:T(2,128)(2,1)S(1)}, bf16[2,16,8,1,128]{4,3,2,1,0:T(2,128)(2,1)S(1)}, u32[]{:S(2)}, u32[]{:S(2)}) collective-permute-start(bf16[2,16,8,1,128]{4,3,2,1,0:T(2,128)(2,1)S(1)} %get-tuple-element.54), channel_id=1, source_target_pairs={{1,0},{2,1},{3,2},{4,3},{5,4},{6,5},{7,6},{8,7},{9,8},{10,9},{11,1... | collective-permute-start | bytes 196616 | tf_op jit(solution)/shard_map/ppermute | solution.py:17
  126.8 27.7 %collective-permute-start.6 = (bf16[2,16,8,1,128]{4,3,2,1,0:T(2,128)(2,1)S(1)}, bf16[2,16,8,1,128]{4,3,2,1,0:T(2,128)(2,1)S(1)}, u32[]{:S(2)}, u32[]{:S(2)}) collective-permute-start(bf16[2,16,8,1,128]{4,3,2,1,0:T(2,128)(2,1)S(1)} %get-tuple-element.53), channel_id=1, source_target_pairs={{0,1},{1,2},{2,3},{3,4},{4,5},{5,6},{6,7},{7,8},{8,9},{9,10},{10,1... | collective-permute-start | bytes 196616 | tf_op jit(solution)/shard_map/ppermute | solution.py:17
  154.8 7.9 %collective-permute-start.9 = (bf16[2,16,1,10,128]{4,3,2,1,0:T(8,128)(2,1)S(1)}, bf16[2,16,1,10,128]{4,3,2,1,0:T(8,128)(2,1)S(1)}, u32[]{:S(2)}, u32[]{:S(2)}) collective-permute-start(bf16[2,16,1,10,128]{4,3,2,1,0:T(8,128)(2,1)S(1)} %get-tuple-element.50), channel_id=1, source_target_pairs={{4,0},{5,1},{6,2},{7,3},{8,4},{9,5},{10,6},{11,7},{12,8},{13,9},{1... | collective-permute-start | bytes 245768 | tf_op jit(solution)/shard_map/ppermute | solution.py:17
  159.9 8.7 %collective-permute-start.8 = (bf16[2,16,1,10,128]{4,3,2,1,0:T(8,128)(2,1)S(1)}, bf16[2,16,1,10,128]{4,3,2,1,0:T(8,128)(2,1)S(1)}, u32[]{:S(2)}, u32[]{:S(2)}) collective-permute-start(bf16[2,16,1,10,128]{4,3,2,1,0:T(8,128)(2,1)S(1)} %get-tuple-element.49), channel_id=1, source_target_pairs={{0,4},{1,5},{2,6},{3,7},{4,8},{5,9},{6,10},{7,11},{8,12},{9,13},{1... | collective-permute-start | bytes 245768 | tf_op jit(solution)/shard_map/ppermute | solution.py:17
  168.8 9.5 %collective-permute-start.11 = (bf16[2,1,10,10,128]{4,3,2,1,0:T(8,128)(2,1)S(1)}, bf16[2,1,10,10,128]{4,3,2,1,0:T(8,128)(2,1)S(1)}, u32[]{:S(2)}, u32[]{:S(2)}) collective-permute-start(bf16[2,1,10,10,128]{4,3,2,1,0:T(8,128)(2,1)S(1)} %get-tuple-element.42), channel_id=1, source_target_pairs={{8,0},{9,1},{10,2},{11,3},{12,4},{13,5},{14,6},{15,7},{16,8},{17,9... | collective-permute-start | bytes 153608 | tf_op jit(solution)/shard_map/ppermute | solution.py:17
  170.7 11.1 %collective-permute-start.10 = (bf16[2,1,10,10,128]{4,3,2,1,0:T(8,128)(2,1)S(1)}, bf16[2,1,10,10,128]{4,3,2,1,0:T(8,128)(2,1)S(1)}, u32[]{:S(2)}, u32[]{:S(2)}) collective-permute-start(bf16[2,1,10,10,128]{4,3,2,1,0:T(8,128)(2,1)S(1)} %get-tuple-element.41), channel_id=1, source_target_pairs={{0,8},{1,9},{2,10},{3,11},{4,12},{5,13},{6,14},{7,15},{8,16},{9,17... | collective-permute-start | bytes 153608 | tf_op jit(solution)/shard_map/ppermute | solution.py:17
  183.7 19.4 %copy-start.5 = (bf16[3,3,3,128,128]{4,3,2,1,0:T(8,128)(2,1)S(1)}, bf16[3,3,3,128,128]{4,3,2,1,0:T(8,128)(2,1)}, u32[]{:S(2)}) copy-start(bf16[3,3,3,128,128]{4,3,2,1,0:T(8,128)(2,1)} %reshape_reshape.3) | copy-start | bytes 2654212
  184.5 27.1 %all-to-all-start.2 = ((f32[4,54,128]{2,1,0:T(8,128)}), f32[4,54,128]{2,1,0:T(8,128)S(1)}, u32[]{:S(2)}, u32[]{:S(2)}) async-start(f32[4,54,128]{2,1,0:T(8,128)} %broadcast_in_dim.15), calls=%async_computation.2 | async-start | bytes 229376 | tf_op jit(solution)/shard_map/all_to_all | solution.py:28
  203.2 8.4 %copy-start.9 = (f32[54,128]{1,0:T(8,128)S(1)}, f32[54,128]{1,0:T(8,128)}, u32[]{:S(2)}) copy-start(f32[54,128]{1,0:T(8,128)} %param.7) | copy-start | bytes 82948
  203.2 8.4 %copy-start.10 = (f32[54,128]{1,0:T(8,128)S(1)}, f32[54,128]{1,0:T(8,128)}, u32[]{:S(2)}) copy-start(f32[54,128]{1,0:T(8,128)} %param.8) | copy-start | bytes 82948
  (2 other events, 1.9 us)
where the time goes:
time: 213 us; the launch traced here: 212 us
  starting transfers between devices  88.5 us (42%)
  waiting for transfers between devices  75.8 us (36%)
  matrix products  24.8 us (12%)
  other arithmetic  12.6 us (6%)
  local copies, waits for them, and re-layouts  9.44 us (4%)
    ppermute x12, waiting for transfers between devices, shifted(): return lax.ppermute(value, axis, pairs)  75.8 us
    ppermute x12, starting transfers between devices, shifted(): return lax.ppermute(value, axis, pairs)  53.2 us
    all_to_all x2, starting transfers between devices, copy_for_each(): return lax.all_to_all(copies, axis, split_axis=0, concat_axis=0, tiled=True)  25.4 us
    conv_general_dilated x2, matrix products, convolve(): lax.conv_general_dilated(field, kernel, (1, 1, 1), 'VALID', dimension_num...  14.8 us
    dot_general x27, matrix products, kernel_terms(): lax.dot_general(window, grad_pre, (((0, 1, 2, 3), (0, 1, 2, 3)), ((), ())...  9.92 us
    all_to_all x1, starting transfers between devices, summed_on_arrival(): lax.all_to_all(parts, axis, split_axis=0, concat_axis=0, tiled=True)  9.84 us
    concatenate x4, other arithmetic, extend(): field = jnp.concatenate([below, field, above], dim)  8.07 us
  transfers between devices with their start and end apart: 15, of which 10 were waited for; matrix products, arithmetic and copies ran while one was open for 9% of the time, Pallas kernels for 0%

commit v1 on v0

v1 whole, which is shorter than its diff:
```python
import jax
import jax.numpy as jnp
from jax import lax
from jax.sharding import PartitionSpec as P

GY = 2
GZ = 4


root_coef = 0.7978845608
cubic_coef = 0.044715


def flip_pairs(count, bit):
    return [(i, i ^ bit) for i in range(count)]


def odd_pairs(count, stride, length):
    pairs = []
    for i in range(count):
        coord = i // stride % length
        other = coord + 1 if coord % 2 == 1 else coord - 1
        if 0 <= other < length:
            pairs.append((i, i + (other - coord) * stride))
    return pairs


def swap_layers(first, last, coord, stride, length):
    devices = lax.axis_size("space")
    even = coord % 2 == 0
    inner = lax.ppermute(jnp.where(even, last, first), "space", flip_pairs(devices, stride))
    if length == 2:
        outer = jnp.zeros_like(inner)
    else:
        outer = lax.ppermute(
            jnp.where(even, first, last), "space", odd_pairs(devices, stride, length)
        )
    return jnp.where(even, outer, inner), jnp.where(even, inner, outer)


def extend(field):
    place = lax.axis_index("space")
    groups = lax.axis_size("space") // (GY * GZ)
    coord_z = place % GZ
    coord_y = place // GZ % GY
    coord_x = place // (GZ * GY)
    for dim, stride, coord, count in (
        (3, 1, coord_z, GZ),
        (2, GZ, coord_y, GY),
        (1, GY * GZ, coord_x, groups),
    ):
        length = field.shape[dim]
        first_layer = lax.slice_in_dim(field, 0, 1, 1, dim)
        last_layer = lax.slice_in_dim(field, length - 1, length, 1, dim)
        below, above = swap_layers(first_layer, last_layer, coord, stride, count)
        field = jnp.concatenate([below, field, above], dim)
    return field


def convolve(field, kernel):
    return lax.conv_general_dilated(
        field,
        kernel,
        (1, 1, 1),
        "VALID",
        dimension_numbers=("NDHWC", "DHWIO", "NDHWC"),
        preferred_element_type=jnp.float32,
    )


def activate(pre):
    inner = root_coef * (pre + cubic_coef * pre * pre * pre)
    tval = jnp.tanh(inner)
    value = 0.5 * pre * (1.0 + tval)
    slope = 0.5 * (1.0 + tval) + 0.5 * pre * (1.0 - tval * tval) * root_coef * (
        1.0 + 3.0 * cubic_coef * pre * pre
    )
    return (value, slope)


def kernel_terms(padded, grad_pre):
    nx, ny, nz = (grad_pre.shape[1], grad_pre.shape[2], grad_pre.shape[3])
    terms = []
    for kx in range(3):
        for ky in range(3):
            for kz in range(3):
                window = padded[:, kx : kx + nx, ky : ky + ny, kz : kz + nz, :]
                terms.append(
                    lax.dot_general(
                        window,
                        grad_pre,
                        (((0, 1, 2, 3), (0, 1, 2, 3)), ((), ())),
                        preferred_element_type=jnp.float32,
                    )
                )
    stacked = jnp.stack(terms, 0)
    return stacked.reshape(27 * stacked.shape[1], stacked.shape[2])


def core_swap(value):
    return lax.ppermute(value, "sample", flip_pairs(lax.axis_size("sample"), 1))


def chip_swap(value):
    return lax.ppermute(value, "sample", flip_pairs(lax.axis_size("sample"), 2))


def halves_joined(mine, other, core, dim):
    low = jnp.where(core == 0, mine, other)
    high = jnp.where(core == 0, other, mine)
    return jnp.concatenate([low, high], dim)


def whole_kernel(rows, core):
    devices = lax.axis_size("space")
    half = rows.shape[0] // 2
    mine = lax.dynamic_slice_in_dim(rows, core * half, half, 0)
    copies = jnp.broadcast_to(mine, (devices, *mine.shape))
    got = lax.all_to_all(copies, "space", split_axis=0, concat_axis=0, tiled=True)
    other = core_swap(got)
    return halves_joined(got, other, core, 1)


def own_rows_sum(terms, core):
    devices = lax.axis_size("space")
    parts = terms.reshape(devices, -1, terms.shape[1])
    half = parts.shape[1] // 2
    mine = lax.dynamic_slice_in_dim(parts, core * half, half, 1)
    away = lax.dynamic_slice_in_dim(parts, (1 - core) * half, half, 1)
    chip = mine + core_swap(away.astype(jnp.bfloat16)).astype(jnp.float32)
    arrived = lax.all_to_all(
        chip.astype(jnp.bfloat16), "space", split_axis=0, concat_axis=0, tiled=True
    )
    owned = arrived.astype(jnp.float32).sum(axis=0)
    owned = owned + chip_swap(owned)
    return halves_joined(owned, core_swap(owned), core, 0)


def local(acts, weight, moment, second, cotangent):
    field = acts[:, 0]
    grad_out = cotangent[:, 0]
    channels = weight.shape[1]
    core = lax.axis_index("sample") % 2
    rows_bf = weight.astype(jnp.bfloat16)
    kernel = whole_kernel(rows_bf, core).reshape(3, 3, 3, channels, channels)
    padded = extend(field)
    pre = convolve(padded, kernel)
    value, slope = activate(pre)
    output = value.astype(jnp.bfloat16)
    grad_pre = (grad_out.astype(jnp.float32) * slope).astype(jnp.bfloat16)
    flipped = jnp.flip(kernel, (0, 1, 2)).transpose(0, 1, 2, 4, 3)
    grad_padded = extend(grad_pre)
    input_grad = convolve(grad_padded, flipped).astype(jnp.bfloat16)
    total = (
        field.shape[0]
        * lax.axis_size("sample")
        * lax.axis_size("space")
        * field.shape[1]
        * field.shape[2]
        * field.shape[3]
    )
    local_terms = kernel_terms(padded, grad_pre) * float(total) ** (-0.5)
    weight_grad = own_rows_sum(local_terms, core)
    new_moment = 0.9 * moment + 0.1 * weight_grad
    new_second = 0.999 * second + 0.001 * weight_grad * weight_grad
    first_fix = 1.0 - 0.9**10
    second_fix = 1.0 - 0.999**10
    new_weight = weight - 0.001 * (new_moment / first_fix) / (
        jnp.sqrt(new_second / second_fix) + 1e-08
    )
    return (output[:, None], input_grad[:, None], weight_grad, new_weight, new_moment, new_second)


def solution(mesh):
    in_specs = (
        P("sample", "space", None, None, None, None),
        P("space", None),
        P("space", None),
        P("space", None),
        P("sample", "space", None, None, None, None),
    )
    out_specs = (
        P("sample", "space", None, None, None, None),
        P("sample", "space", None, None, None, None),
        P("space", None),
        P("space", None),
        P("space", None),
        P("space", None),
    )
    return jax.shard_map(local, mesh=mesh, in_specs=in_specs, out_specs=out_specs, check_vma=False)
```

time: 213 us -> 139 us (0.65)
  the two profiles are of different devices: /device:TPU:25 before, /device:TPU:1 now
where the time goes in v1:
time: 139 us
  starting transfers between devices  64.4 us (46%)
  waiting for transfers between devices  26.3 us (19%)
  matrix products  23.4 us (17%)
  other arithmetic  14.6 us (11%)
  local copies, waits for them, and re-layouts  8.56 us (6%)
    ppermute x6, starting transfers between devices, swap_layers(): lax.ppermute(jnp.where(even, last, first), 'space', flip_pairs(devices, s...  28.7 us
    ppermute x6, waiting for transfers between devices, swap_layers(): lax.ppermute(jnp.where(even, last, first), 'space', flip_pairs(devices, s...  25.9 us
    conv_general_dilated x2, matrix products, convolve(): lax.conv_general_dilated(field, kernel, (1, 1, 1), 'VALID', dimension_num...  13.5 us
    all_to_all x1, starting transfers between devices, whole_kernel(): lax.all_to_all(copies, 'space', split_axis=0, concat_axis=0, tiled=True)  11.5 us
    dot_general x27, matrix products, kernel_terms(): lax.dot_general(window, grad_pre, (((0, 1, 2, 3), (0, 1, 2, 3)), ((), ())...  9.92 us
    ppermute x1, starting transfers between devices, chip_swap(): return lax.ppermute(value, 'sample', flip_pairs(lax.axis_size('sample'), 2))  8.49 us
    all_to_all x1, starting transfers between devices, own_rows_sum(): lax.all_to_all(chip.astype(jnp.bfloat16), 'space', split_axis=0, concat_a...  7.88 us
    concatenate x4, other arithmetic, extend(): field = jnp.concatenate([below, field, above], dim)  6.92 us
  transfers between devices with their start and end apart: 16, of which 5 were waited for; matrix products, arithmetic and copies ran while one was open for 12% of the time, Pallas kernels for 0%

profile of v1, /device:TPU:1, one launch (start us, length us, event | category | flops | bytes accessed | tf_op | source)
XLA Modules:
  0.0 138.5 jit_solution(7919757445262440831)
XLA Ops:
  0.7 1.5 %broadcast_select_fusion.9 = (bf16[2,16,8,1,128]{4,3,2,1,0:T(2,128)(2,1)S(1)}, bf16[2,16,8,1,128]{4,3,2,1,0:T(2,128)(2,1)S(1)}) fusion(pred[]{:T(512)S(6)} %eq.32, bf16[2,16,8,8,128]{4,3,2,1,0:T(8,128)(2,1)} %bitcast.261), kind=kLoop, calls=%fused_computation.118 | loop fusion | flops 65536 | bytes 262145 | tf_op jit(solution)/shard_map/jit(_where)/select_n | solution.py:36
  2.9 4.6 %collective-permute-start.1 = (bf16[2,16,8,1,128]{4,3,2,1,0:T(2,128)(2,1)S(1)}, bf16[2,16,8,1,128]{4,3,2,1,0:T(2,128)(2,1)S(1)}, u32[]{:S(2)}, u32[]{:S(2)}) collective-permute-start(bf16[2,16,8,1,128]{4,3,2,1,0:T(2,128)(2,1)S(1)} %get-tuple-element.45), channel_id=1, source_target_pairs={{0,1},{1,0},{2,3},{3,2},{4,5},{5,4},{6,7},{7,6},{8,9},{9,8},{10,11... | collective-permute-start | bytes 196616 | tf_op jit(solution)/shard_map/ppermute | solution.py:31
  7.5 2.9 %collective-permute-done.1 = bf16[2,16,8,1,128]{4,3,2,1,0:T(2,128)(2,1)S(1)} collective-permute-done((bf16[2,16,8,1,128]{4,3,2,1,0:T(2,128)(2,1)S(1)}, bf16[2,16,8,1,128]{4,3,2,1,0:T(2,128)(2,1)S(1)}, u32[]{:S(2)}, u32[]{:S(2)}) %collective-permute-start.1) | collective-permute-done | bytes 65568 | tf_op jit(solution)/shard_map/ppermute | solution.py:31
  11.7 3.1 %collective-permute-start.2 = (bf16[2,16,1,10,128]{4,3,2,1,0:T(8,128)(2,1)S(1)}, bf16[2,16,1,10,128]{4,3,2,1,0:T(8,128)(2,1)S(1)}, u32[]{:S(2)}, u32[]{:S(2)}) collective-permute-start(bf16[2,16,1,10,128]{4,3,2,1,0:T(8,128)(2,1)S(1)} %fusion.66), channel_id=1, source_target_pairs={{0,4},{1,5},{2,6},{3,7},{4,0},{5,1},{6,2},{7,3},{8,12},{9,13},{10,... | collective-permute-start | bytes 245768 | tf_op jit(solution)/shard_map/ppermute | solution.py:31
  15.6 11.5 %all-to-all-start = ((bf16[64,27,128]{2,1,0:T(8,128)(2,1)}), bf16[64,27,128]{2,1,0:T(8,128)(2,1)S(1)}, u32[]{:S(2)}, u32[]{:S(2)}) async-start(bf16[64,27,128]{2,1,0:T(8,128)(2,1)} %broadcast_in_dim.9), calls=%async_computation | async-start | bytes 1048576 | tf_op jit(solution)/shard_map/all_to_all | solution.py:119
  28.0 7.4 %collective-permute-start.4 = (bf16[2,1,10,10,128]{4,3,2,1,0:T(8,128)(2,1)S(1)}, bf16[2,1,10,10,128]{4,3,2,1,0:T(8,128)(2,1)S(1)}, u32[]{:S(2)}, u32[]{:S(2)}) collective-permute-start(bf16[2,1,10,10,128]{4,3,2,1,0:T(8,128)(2,1)S(1)} %broadcast_select_fusion.20), channel_id=1, source_target_pairs={{0,8},{1,9},{2,10},{3,11},{4,12},{5,13},{6,14},{7,15},{8,0},{9,1},... | collective-permute-start | bytes 153608 | tf_op jit(solution)/shard_map/ppermute | solution.py:31
  35.5 2.8 %pad_maximum_fusion.3 = (bf16[2,16,9,10,128]{4,3,2,1,0:T(8,128)(2,1)}, bf16[2,16,9,10,128]{4,3,2,1,0:T(8,128)(2,1)}) fusion(bf16[2,16,1,10,128]{4,3,2,1,0:T(8,128)(2,1)S(1)} %get-tuple-element.57, bf16[2,16,8,1,128]{4,3,2,1,0:T(2,128)(2,1)S(1)} %get-tuple-element.49, bf16[2,16,8,8,128]{4,3,2,1,0:T(8,128)(2,1)S(1)} %bitcast.264, ...), kind=kLoop, calls=%fused_computation.9 | loop fusion | flops 5898240 | bytes 2293760 | tf_op jit(solution)/shard_map/concatenate | solution.py:56
  38.3 8.7 %collective-permute-done.4 = bf16[2,1,10,10,128]{4,3,2,1,0:T(8,128)(2,1)S(1)} collective-permute-done((bf16[2,1,10,10,128]{4,3,2,1,0:T(8,128)(2,1)S(1)}, bf16[2,1,10,10,128]{4,3,2,1,0:T(8,128)(2,1)S(1)}, u32[]{:S(2)}, u32[]{:S(2)}) %collective-permute-start.4) | collective-permute-done | bytes 51232 | tf_op jit(solution)/shard_map/ppermute | solution.py:31
  46.9 3.2 %collective-permute-start.5 = (bf16[64,27,128]{2,1,0:T(8,128)(2,1)S(1)}, bf16[64,27,128]{2,1,0:T(8,128)(2,1)S(1)}, u32[]{:S(2)}, u32[]{:S(2)}) collective-permute-start(bf16[64,27,128]{2,1,0:T(8,128)(2,1)S(1)} %all-to-all-done), channel_id=1, source_target_pairs={{0,64},{64,0},{128,192},{192,128},{1,65},{65,1},{129,193},{193,129... | collective-permute-start | bytes 1327112 | tf_op jit(solution)/shard_map/ppermute | solution.py:101
  50.8 2.7 %pad_maximum_fusion.2 = (bf16[2,17,10,10,128]{4,3,2,1,0:T(8,128)(2,1)}, bf16[2,17,10,10,128]{4,3,2,1,0:T(8,128)(2,1)}) fusion(bf16[2,1,10,10,128]{4,3,2,1,0:T(8,128)(2,1)S(1)} %get-tuple-element.53, bf16[2,16,1,10,128]{4,3,2,1,0:T(8,128)(2,1)S(1)} %get-tuple-element.57, bf16[2,16,8,1,128]{4,3,2,1,0:T(2,128)(2,1)S(1)} %get-tuple-element.49, ...), kind=kLoop, calls=%fused_computation.5 | loop fusion | flops 10444800 | bytes 2662400 | tf_op jit(solution)/shard_map/concatenate | solution.py:56
  53.9 1.2 reshape.22
  55.0 7.3 %fusion.36 = f32[2,16,8,8,128]{4,0,3,2,1:T(2,128)S(1)} fusion(bf16[3,3,3,128,128]{4,3,2,1,0:T(8,128)(2,1)} %reshape.22, bf16[2,18,10,10,128]{4,3,2,1,0:T(8,128)(2,1)S(1)} %pad_maximum_fusion), kind=kOutput, calls=%fused_computation.76 | convolution fusion | flops 1811939328 | bytes 2854912 | tf_op jit(solution)/shard_map/conv_general_dilated | solution.py:61
  62.4 1.6 %fusion.34 = (bf16[2,16,8,8,128]{4,3,2,1,0:T(8,128)(2,1)S(1)}, bf16[2,1,16,8,8,128]{5,4,3,2,1,0:T(8,128)(2,1)}) fusion(f32[2,16,8,8,128]{4,0,3,2,1:T(2,128)S(1)} %fusion.36, bf16[2,1,16,8,8,128]{5,4,3,2,1,0:T(8,128)(2,1)S(1)} %copy-done.7), kind=kLoop, calls=%fused_computation.70 | loop fusion | flops 5767168 | bytes 2621440 | tf_op jit(solution)/shard_map/convert_element_type | solution.py:150
  76.9 1.4 mul.114
  78.2 1.6 %dynamic-slice_convert_fusion = bf16[64,27,128]{2,1,0:T(8,128)(2,1)S(1)} fusion(f32[64,54,128]{2,1,0:T(8,128)} %mul.114, s32[]{:T(128)S(6)} %select_n.215), kind=kLoop, calls=%fused_computation.73 | loop fusion | bytes 884740 | tf_op jit(solution)/shard_map/convert_element_type | solution.py:130
  80.9 3.6 %collective-permute-start.7 = (bf16[2,16,8,1,128]{4,3,2,1,0:T(2,128)(2,1)S(1)}, bf16[2,16,8,1,128]{4,3,2,1,0:T(2,128)(2,1)S(1)}, u32[]{:S(2)}, u32[]{:S(2)}) collective-permute-start(bf16[2,16,8,1,128]{4,3,2,1,0:T(2,128)(2,1)S(1)} %get-tuple-element.43), channel_id=1, source_target_pairs={{0,1},{1,0},{2,3},{3,2},{4,5},{5,4},{6,7},{7,6},{8,9},{9,8},{10,11... | collective-permute-start | bytes 196616 | tf_op jit(solution)/shard_map/ppermute | solution.py:31
  84.5 3.1 %collective-permute-done.7 = bf16[2,16,8,1,128]{4,3,2,1,0:T(2,128)(2,1)S(1)} collective-permute-done((bf16[2,16,8,1,128]{4,3,2,1,0:T(2,128)(2,1)S(1)}, bf16[2,16,8,1,128]{4,3,2,1,0:T(2,128)(2,1)S(1)}, u32[]{:S(2)}, u32[]{:S(2)}) %collective-permute-start.7) | collective-permute-done | bytes 65568 | tf_op jit(solution)/shard_map/ppermute | solution.py:31
  88.0 2.6 %collective-permute-start.8 = (bf16[2,16,1,10,128]{4,3,2,1,0:T(8,128)(2,1)S(1)}, bf16[2,16,1,10,128]{4,3,2,1,0:T(8,128)(2,1)S(1)}, u32[]{:S(2)}, u32[]{:S(2)}) collective-permute-start(bf16[2,16,1,10,128]{4,3,2,1,0:T(8,128)(2,1)S(1)} %fusion.65), channel_id=1, source_target_pairs={{0,4},{1,5},{2,6},{3,7},{4,0},{5,1},{6,2},{7,3},{8,12},{9,13},{10,... | collective-permute-start | bytes 245768 | tf_op jit(solution)/shard_map/ppermute | solution.py:31
  91.6 7.9 %all-to-all-start.1 = ((bf16[64,27,128]{2,1,0:T(8,128)(2,1)}), bf16[64,27,128]{2,1,0:T(8,128)(2,1)S(1)}, u32[]{:S(2)}, u32[]{:S(2)}) async-start(bf16[64,27,128]{2,1,0:T(8,128)(2,1)} %add_convert_fusion), calls=%async_computation.1 | async-start | bytes 1048576 | tf_op jit(solution)/shard_map/all_to_all | solution.py:131
  100.4 7.4 %collective-permute-start.10 = (bf16[2,1,10,10,128]{4,3,2,1,0:T(8,128)(2,1)S(1)}, bf16[2,1,10,10,128]{4,3,2,1,0:T(8,128)(2,1)S(1)}, u32[]{:S(2)}, u32[]{:S(2)}) collective-permute-start(bf16[2,1,10,10,128]{4,3,2,1,0:T(8,128)(2,1)S(1)} %broadcast_select_fusion.16), channel_id=1, source_target_pairs={{0,8},{1,9},{2,10},{3,11},{4,12},{5,13},{6,14},{7,15},{8,0},{9,1},... | collective-permute-start | bytes 153608 | tf_op jit(solution)/shard_map/ppermute | solution.py:31
  107.8 11.3 %collective-permute-done.10 = bf16[2,1,10,10,128]{4,3,2,1,0:T(8,128)(2,1)S(1)} collective-permute-done((bf16[2,1,10,10,128]{4,3,2,1,0:T(8,128)(2,1)S(1)}, bf16[2,1,10,10,128]{4,3,2,1,0:T(8,128)(2,1)S(1)}, u32[]{:S(2)}, u32[]{:S(2)}) %collective-permute-start.10) | collective-permute-done | bytes 51232 | tf_op jit(solution)/shard_map/ppermute | solution.py:31
  119.2 8.5 %collective-permute-start.12 = (f32[27,128]{1,0:T(8,128)S(1)}, f32[27,128]{1,0:T(8,128)S(1)}, u32[]{:S(2)}, u32[]{:S(2)}) collective-permute-start(f32[27,128]{1,0:T(8,128)S(1)} %convert_reduce_fusion), channel_id=1, source_target_pairs={{0,128},{64,192},{128,0},{192,64},{1,129},{65,193},{129,1},{193,65... | collective-permute-start | bytes 41480 | tf_op jit(solution)/shard_map/ppermute | solution.py:105
  128.9 1.9 %collective-permute-start.13 = (f32[27,128]{1,0:T(8,128)S(1)}, f32[27,128]{1,0:T(8,128)S(1)}, u32[]{:S(2)}, u32[]{:S(2)}) collective-permute-start(f32[27,128]{1,0:T(8,128)S(1)} %add.77), channel_id=1, source_target_pairs={{0,64},{64,0},{128,192},{192,128},{1,65},{65,1},{129,193},{193,129... | collective-permute-start | bytes 41480 | tf_op jit(solution)/shard_map/ppermute | solution.py:101
  130.7 6.2 %fusion = bf16[2,1,16,8,8,128]{5,0,4,3,2,1:T(2,128)(2,1)S(1)} fusion(bf16[3,3,3,128,128]{4,3,2,1,0:T(8,128)(2,1)S(1)} %copy-done.6, bf16[2,18,10,10,128]{4,3,2,1,0:T(8,128)(2,1)S(1)} %pad_maximum_fusion.1), kind=kOutput, calls=%fused_computation.7 | convolution fusion | flops 1812201472 | bytes 2330624 | tf_op jit(solution)/shard_map/conv_general_dilated | solution.py:61
  (92 shorter events, 23.6 us)
Async XLA Ops:
  0.6 14.1 %copy-start.8 = (f32[54,128]{1,0:T(8,128)S(1)}, f32[54,128]{1,0:T(8,128)}, u32[]{:S(2)}) copy-start(f32[54,128]{1,0:T(8,128)} %param.6) | copy-start | bytes 82948
  2.2 5.3 %collective-permute-start = (bf16[2,16,8,1,128]{4,3,2,1,0:T(2,128)(2,1)S(1)}, bf16[2,16,8,1,128]{4,3,2,1,0:T(2,128)(2,1)S(1)}, u32[]{:S(2)}, u32[]{:S(2)}) collective-permute-start(bf16[2,16,8,1,128]{4,3,2,1,0:T(2,128)(2,1)S(1)} %get-tuple-element.44), channel_id=1, source_target_pairs={{1,2},{2,1},{5,6},{6,5},{9,10},{10,9},{13,14},{14,13},{17,18},{18,... | collective-permute-start | bytes 196616 | tf_op jit(solution)/shard_map/ppermute | solution.py:35
  2.9 7.5 %collective-permute-start.1 = (bf16[2,16,8,1,128]{4,3,2,1,0:T(2,128)(2,1)S(1)}, bf16[2,16,8,1,128]{4,3,2,1,0:T(2,128)(2,1)S(1)}, u32[]{:S(2)}, u32[]{:S(2)}) collective-permute-start(bf16[2,16,8,1,128]{4,3,2,1,0:T(2,128)(2,1)S(1)} %get-tuple-element.45), channel_id=1, source_target_pairs={{0,1},{1,0},{2,3},{3,2},{4,5},{5,4},{6,7},{7,6},{8,9},{9,8},{10,11... | collective-permute-start | bytes 196616 | tf_op jit(solution)/shard_map/ppermute | solution.py:31
  7.5 19.8 %copy-start = (bf16[2,1,16,8,8,128]{5,4,3,2,1,0:T(8,128)(2,1)S(1)}, bf16[2,1,16,8,8,128]{5,4,3,2,1,0:T(8,128)(2,1)}, u32[]{:S(2)}) copy-start(bf16[2,1,16,8,8,128]{5,4,3,2,1,0:T(8,128)(2,1)} %param.5) | copy-start | bytes 1572868
  11.7 15.5 %collective-permute-start.2 = (bf16[2,16,1,10,128]{4,3,2,1,0:T(8,128)(2,1)S(1)}, bf16[2,16,1,10,128]{4,3,2,1,0:T(8,128)(2,1)S(1)}, u32[]{:S(2)}, u32[]{:S(2)}) collective-permute-start(bf16[2,16,1,10,128]{4,3,2,1,0:T(8,128)(2,1)S(1)} %fusion.66), channel_id=1, source_target_pairs={{0,4},{1,5},{2,6},{3,7},{4,0},{5,1},{6,2},{7,3},{8,12},{9,13},{10,... | collective-permute-start | bytes 245768 | tf_op jit(solution)/shard_map/ppermute | solution.py:31
  15.6 31.3 %all-to-all-start = ((bf16[64,27,128]{2,1,0:T(8,128)(2,1)}), bf16[64,27,128]{2,1,0:T(8,128)(2,1)S(1)}, u32[]{:S(2)}, u32[]{:S(2)}) async-start(bf16[64,27,128]{2,1,0:T(8,128)(2,1)} %broadcast_in_dim.9), calls=%async_computation | async-start | bytes 1048576 | tf_op jit(solution)/shard_map/all_to_all | solution.py:119
  27.4 10.9 %collective-permute-start.3 = (bf16[2,1,10,10,128]{4,3,2,1,0:T(8,128)(2,1)S(1)}, bf16[2,1,10,10,128]{4,3,2,1,0:T(8,128)(2,1)S(1)}, u32[]{:S(2)}, u32[]{:S(2)}) collective-permute-start(bf16[2,1,10,10,128]{4,3,2,1,0:T(8,128)(2,1)S(1)} %get-tuple-element.31), channel_id=1, source_target_pairs={{8,16},{9,17},{10,18},{11,19},{12,20},{13,21},{14,22},{15,23},{16,... | collective-permute-start | bytes 153608 | tf_op jit(solution)/shard_map/ppermute | solution.py:35
  28.0 18.9 %collective-permute-start.4 = (bf16[2,1,10,10,128]{4,3,2,1,0:T(8,128)(2,1)S(1)}, bf16[2,1,10,10,128]{4,3,2,1,0:T(8,128)(2,1)S(1)}, u32[]{:S(2)}, u32[]{:S(2)}) collective-permute-start(bf16[2,1,10,10,128]{4,3,2,1,0:T(8,128)(2,1)S(1)} %broadcast_select_fusion.20), channel_id=1, source_target_pairs={{0,8},{1,9},{2,10},{3,11},{4,12},{5,13},{6,14},{7,15},{8,0},{9,1},... | collective-permute-start | bytes 153608 | tf_op jit(solution)/shard_map/ppermute | solution.py:31
  46.9 6.6 %collective-permute-start.5 = (bf16[64,27,128]{2,1,0:T(8,128)(2,1)S(1)}, bf16[64,27,128]{2,1,0:T(8,128)(2,1)S(1)}, u32[]{:S(2)}, u32[]{:S(2)}) collective-permute-start(bf16[64,27,128]{2,1,0:T(8,128)(2,1)S(1)} %all-to-all-done), channel_id=1, source_target_pairs={{0,64},{64,0},{128,192},{192,128},{1,65},{65,1},{129,193},{193,129... | collective-permute-start | bytes 1327112 | tf_op jit(solution)/shard_map/ppermute | solution.py:101
  55.0 7.4 %copy-start.7 = (bf16[2,1,16,8,8,128]{5,4,3,2,1,0:T(8,128)(2,1)S(1)}, bf16[2,1,16,8,8,128]{5,4,3,2,1,0:T(8,128)(2,1)}, u32[]{:S(2)}) copy-start(bf16[2,1,16,8,8,128]{5,4,3,2,1,0:T(8,128)(2,1)} %param.9) | copy-start | bytes 1572868
  62.4 1.6 %copy-start.3 = (bf16[2,17,10,10,128]{4,3,2,1,0:T(8,128)(2,1)S(1)}, bf16[2,17,10,10,128]{4,3,2,1,0:T(8,128)(2,1)}, u32[]{:S(2)}) copy-start(bf16[2,17,10,10,128]{4,3,2,1,0:T(8,128)(2,1)} %get-tuple-element.35) | copy-start | bytes 2611204
  78.2 12.4 %copy-start.1 = (f32[64,54,128]{2,1,0:T(8,128)S(1)}, f32[64,54,128]{2,1,0:T(8,128)}, u32[]{:S(2)}) copy-start(f32[64,54,128]{2,1,0:T(8,128)} %mul.114) | copy-start | bytes 5308420
  79.8 10.8 %collective-permute-start.11 = (bf16[64,27,128]{2,1,0:T(8,128)(2,1)S(1)}, bf16[64,27,128]{2,1,0:T(8,128)(2,1)S(1)}, u32[]{:S(2)}, u32[]{:S(2)}) collective-permute-start(bf16[64,27,128]{2,1,0:T(8,128)(2,1)S(1)} %dynamic-slice_convert_fusion), channel_id=1, source_target_pairs={{0,64},{64,0},{128,192},{192,128},{1,65},{65,1},{129,193},{193,129... | collective-permute-start | bytes 1327112 | tf_op jit(solution)/shard_map/ppermute | solution.py:101
  80.2 4.2 %collective-permute-start.6 = (bf16[2,16,8,1,128]{4,3,2,1,0:T(2,128)(2,1)S(1)}, bf16[2,16,8,1,128]{4,3,2,1,0:T(2,128)(2,1)S(1)}, u32[]{:S(2)}, u32[]{:S(2)}) collective-permute-start(bf16[2,16,8,1,128]{4,3,2,1,0:T(2,128)(2,1)S(1)} %get-tuple-element.42), channel_id=1, source_target_pairs={{1,2},{2,1},{5,6},{6,5},{9,10},{10,9},{13,14},{14,13},{17,18},{18,... | collective-permute-start | bytes 196616 | tf_op jit(solution)/shard_map/ppermute | solution.py:35
  80.9 6.7 %collective-permute-start.7 = (bf16[2,16,8,1,128]{4,3,2,1,0:T(2,128)(2,1)S(1)}, bf16[2,16,8,1,128]{4,3,2,1,0:T(2,128)(2,1)S(1)}, u32[]{:S(2)}, u32[]{:S(2)}) collective-permute-start(bf16[2,16,8,1,128]{4,3,2,1,0:T(2,128)(2,1)S(1)} %get-tuple-element.43), channel_id=1, source_target_pairs={{0,1},{1,0},{2,3},{3,2},{4,5},{5,4},{6,7},{7,6},{8,9},{9,8},{10,11... | collective-permute-start | bytes 196616 | tf_op jit(solution)/shard_map/ppermute | solution.py:31
  88.0 11.5 %collective-permute-start.8 = (bf16[2,16,1,10,128]{4,3,2,1,0:T(8,128)(2,1)S(1)}, bf16[2,16,1,10,128]{4,3,2,1,0:T(8,128)(2,1)S(1)}, u32[]{:S(2)}, u32[]{:S(2)}) collective-permute-start(bf16[2,16,1,10,128]{4,3,2,1,0:T(8,128)(2,1)S(1)} %fusion.65), channel_id=1, source_target_pairs={{0,4},{1,5},{2,6},{3,7},{4,0},{5,1},{6,2},{7,3},{8,12},{9,13},{10,... | collective-permute-start | bytes 245768 | tf_op jit(solution)/shard_map/ppermute | solution.py:31
  91.6 27.5 %all-to-all-start.1 = ((bf16[64,27,128]{2,1,0:T(8,128)(2,1)}), bf16[64,27,128]{2,1,0:T(8,128)(2,1)S(1)}, u32[]{:S(2)}, u32[]{:S(2)}) async-start(bf16[64,27,128]{2,1,0:T(8,128)(2,1)} %add_convert_fusion), calls=%async_computation.1 | async-start | bytes 1048576 | tf_op jit(solution)/shard_map/all_to_all | solution.py:131
  99.7 8.1 %collective-permute-start.9 = (bf16[2,1,10,10,128]{4,3,2,1,0:T(8,128)(2,1)S(1)}, bf16[2,1,10,10,128]{4,3,2,1,0:T(8,128)(2,1)S(1)}, u32[]{:S(2)}, u32[]{:S(2)}) collective-permute-start(bf16[2,1,10,10,128]{4,3,2,1,0:T(8,128)(2,1)S(1)} %get-tuple-element.28), channel_id=1, source_target_pairs={{8,16},{9,17},{10,18},{11,19},{12,20},{13,21},{14,22},{15,23},{16,... | collective-permute-start | bytes 153608 | tf_op jit(solution)/shard_map/ppermute | solution.py:35
  100.4 30.4 %copy-start.6 = (bf16[3,3,3,128,128]{4,3,2,1,0:T(8,128)(2,1)S(1)}, bf16[3,3,3,128,128]{4,3,2,1,0:T(8,128)(2,1)}, u32[]{:S(2)}) copy-start(bf16[3,3,3,128,128]{4,3,2,1,0:T(8,128)(2,1)} %reshape.22) | copy-start | bytes 2654212
  100.4 18.7 %collective-permute-start.10 = (bf16[2,1,10,10,128]{4,3,2,1,0:T(8,128)(2,1)S(1)}, bf16[2,1,10,10,128]{4,3,2,1,0:T(8,128)(2,1)S(1)}, u32[]{:S(2)}, u32[]{:S(2)}) collective-permute-start(bf16[2,1,10,10,128]{4,3,2,1,0:T(8,128)(2,1)S(1)} %broadcast_select_fusion.16), channel_id=1, source_target_pairs={{0,8},{1,9},{2,10},{3,11},{4,12},{5,13},{6,14},{7,15},{8,0},{9,1},... | collective-permute-start | bytes 153608 | tf_op jit(solution)/shard_map/ppermute | solution.py:31
  119.2 9.6 %collective-permute-start.12 = (f32[27,128]{1,0:T(8,128)S(1)}, f32[27,128]{1,0:T(8,128)S(1)}, u32[]{:S(2)}, u32[]{:S(2)}) collective-permute-start(f32[27,128]{1,0:T(8,128)S(1)} %convert_reduce_fusion), channel_id=1, source_target_pairs={{0,128},{64,192},{128,0},{192,64},{1,129},{65,193},{129,1},{193,65... | collective-permute-start | bytes 41480 | tf_op jit(solution)/shard_map/ppermute | solution.py:105
  128.9 9.0 %copy-start.9 = (f32[54,128]{1,0:T(8,128)S(1)}, f32[54,128]{1,0:T(8,128)}, u32[]{:S(2)}) copy-start(f32[54,128]{1,0:T(8,128)} %param.7) | copy-start | bytes 82948
  128.9 9.0 %copy-start.10 = (f32[54,128]{1,0:T(8,128)S(1)}, f32[54,128]{1,0:T(8,128)}, u32[]{:S(2)}) copy-start(f32[54,128]{1,0:T(8,128)} %param.8) | copy-start | bytes 82948
  128.9 9.0 %collective-permute-start.13 = (f32[27,128]{1,0:T(8,128)S(1)}, f32[27,128]{1,0:T(8,128)S(1)}, u32[]{:S(2)}, u32[]{:S(2)}) collective-permute-start(f32[27,128]{1,0:T(8,128)S(1)} %add.77), channel_id=1, source_target_pairs={{0,64},{64,0},{128,192},{192,128},{1,65},{65,1},{129,193},{193,129... | collective-permute-start | bytes 41480 | tf_op jit(solution)/shard_map/ppermute | solution.py:101
  (3 other events, 3.9 us)

commit v2 on v1

v2 whole, which is shorter than its diff:
```python
import functools

import jax
import jax.numpy as jnp
from jax import lax
from jax.experimental import pallas as pl
from jax.experimental.pallas import tpu as pltpu
from jax.sharding import PartitionSpec as P

GY = 2
GZ = 4

root_coef = 0.7978845608
cubic_coef = 0.044715
bf16, f32 = jnp.bfloat16, jnp.float32


def activate(pre):
    square = pre * pre
    inner = root_coef * (pre + cubic_coef * pre * square)
    tval = jnp.tanh(inner)
    value = 0.5 * pre * (1.0 + tval)
    slope = 0.5 * (1.0 + tval) + 0.5 * pre * (1.0 - tval * tval) * root_coef * (
        1.0 + 3.0 * cubic_coef * square
    )
    return (value, slope)


def fill_windows(center, ylo, yhi, zlo, zhi, windows, layers):
    place = lax.broadcasted_iota(jnp.int32, (8, 128), 0)

    def one(x, _):
        rows = [ylo[0, x].astype(f32)] + [center[0, x, y].astype(f32) for y in range(8)] + [yhi[0, x].astype(f32)]
        low, high = zlo[0, x].astype(f32), zhi[0, x].astype(f32)
        shifted = [[], [], []]
        for yy in range(10):
            row = rows[yy]
            lo = jnp.broadcast_to(low[yy : yy + 1], (8, 128))
            hi = jnp.broadcast_to(high[yy : yy + 1], (8, 128))
            shifted[0].append(jnp.where(place == 0, lo, pltpu.roll(row, 1, 0)))
            shifted[1].append(row)
            shifted[2].append(jnp.where(place == 7, hi, pltpu.roll(row, 7, 0)))
        for ky in range(3):
            for kz in range(3):
                col = (ky * 3 + kz) * 128
                tile = jnp.concatenate(shifted[kz][ky : ky + 8], axis=0).astype(bf16)
                windows[x, :, col : col + 128] = tile
        return 0

    lax.fori_loop(0, layers, one, 0)


def forward_kernel(scale, core_ref, center, ylo, yhi, zlo, zhi, dy, mine, other,
                   out, dz, parts, kern_out, windows, rows, kern, dzs, total, values):
    step = pl.program_id(0)
    core = core_ref[0]

    @pl.when(step == 0)
    def _():
        def piece(s, _):
            a, b = mine[s].astype(f32), other[s].astype(f32)
            rows[pl.ds(54 * s, 27), :] = jnp.where(core == 0, a, b)
            rows[pl.ds(54 * s + 27, 27), :] = jnp.where(core == 0, b, a)
            return 0
        lax.fori_loop(0, 64, piece, 0)
        for kx in range(3):
            kern[kx] = rows[1152 * kx : 1152 * (kx + 1), :].astype(bf16)
            kern_out[kx] = kern[kx]

    fill_windows(center, ylo, yhi, zlo, zhi, windows, 20)

    def layer(i, _):
        x = 3 * i
        pre = jnp.zeros((192, 128), f32)
        for kx in range(3):
            lhs = windows[pl.ds(x + kx, 3)].reshape(192, 1152)
            pre += jnp.dot(lhs, kern[kx], preferred_element_type=f32)
        value, slope = activate(pre)
        grad = (dy[0, pl.ds(x, 3)].reshape(192, 128).astype(f32) * slope).astype(bf16)
        dz[0, pl.ds(x, 3)] = grad.reshape(3, 64, 128)
        values[pl.ds(x, 3)] = value.astype(bf16).reshape(3, 64, 128)
        return 0

    lax.fori_loop(0, 6, layer, 0)
    out[0] = values[1:17]
    own = dz[0, 1:17].reshape(1024, 128)
    dzs[...] = jnp.zeros_like(dzs)
    for kx in range(3):
        dzs[64 * kx : 64 * kx + 1024, 128 * kx : 128 * (kx + 1)] = own
    both = windows[1:19].reshape(1152, 1152)
    term = lax.dot_general(dzs[...], both, (((0,), (0,)), ((), ())), preferred_element_type=f32)

    @pl.when(step == 0)
    def _():
        total[...] = term

    @pl.when(step == 1)
    def _():
        whole = (total[...] + term) * scale
        for kx in range(3):
            for t in range(9):
                block = whole[128 * kx : 128 * (kx + 1), 128 * t : 128 * (t + 1)]
                row = (kx * 9 + t) * 128
                rows[row : row + 128, :] = block.T
        def piece(s, _):
            parts[0, s] = rows[pl.ds(54 * s, 27), :].astype(bf16)
            parts[1, s] = rows[pl.ds(54 * s + 27, 27), :].astype(bf16)
            return 0
        lax.fori_loop(0, 64, piece, 0)


def forward(core, center, ylo, yhi, zlo, zhi, dy, mine, other, scale):
    def crop(shape):
        return pl.BlockSpec((1, *shape[1:]), lambda b: (b,) + (0,) * (len(shape) - 1))
    def whole(shape):
        return pl.BlockSpec(shape, lambda b: (0,) * len(shape), pipeline_mode=pl.Buffered(1))
    ins = (center, ylo, yhi, zlo, zhi, dy)
    outs = [jax.ShapeDtypeStruct((2, 16, 64, 128), bf16), jax.ShapeDtypeStruct((2, 18, 64, 128), bf16),
            jax.ShapeDtypeStruct((2, 64, 27, 128), bf16), jax.ShapeDtypeStruct((3, 1152, 128), bf16)]
    return pl.pallas_call(
        functools.partial(forward_kernel, scale),
        grid=(2,),
        in_specs=[pl.BlockSpec(memory_space=pltpu.SMEM)] + [crop(a.shape) for a in ins] + [whole(mine.shape), whole(other.shape)],
        out_specs=[crop(outs[0].shape), crop(outs[1].shape), whole(outs[2].shape), whole(outs[3].shape)],
        out_shape=outs,
        scratch_shapes=[pltpu.VMEM((20, 64, 1152), bf16), pltpu.VMEM((3488, 128), f32), pltpu.VMEM((3, 1152, 128), bf16),
                        pltpu.VMEM((1152, 384), bf16), pltpu.VMEM((384, 1152), f32),
                        pltpu.VMEM((18, 64, 128), bf16)],
        compiler_params=pltpu.CompilerParams(vmem_limit_bytes=40 * 2**20),
        cost_estimate=pl.CostEstimate(flops=8 * 10**9, bytes_accessed=8 * 10**6, transcendentals=300000),
        name="forward",
    )(core, *ins, mine, other)


def backward_kernel(center, ylo, yhi, zlo, zhi, kern, out, windows):
    fill_windows(center, ylo, yhi, zlo, zhi, windows, 18)

    def layer(i, _):
        x = 4 * i
        grad = jnp.zeros((256, 128), f32)
        for kx in range(3):
            lhs = windows[pl.ds(x + kx, 4)].reshape(256, 1152)
            grad += jnp.dot(lhs, kern[kx], preferred_element_type=f32)
        out[0, pl.ds(x, 4)] = grad.astype(bf16).reshape(4, 64, 128)
        return 0

    lax.fori_loop(0, 4, layer, 0)


def backward(center, ylo, yhi, zlo, zhi, kern):
    def crop(shape):
        return pl.BlockSpec((1, *shape[1:]), lambda b: (b,) + (0,) * (len(shape) - 1))
    ins = (center, ylo, yhi, zlo, zhi)
    out = jax.ShapeDtypeStruct((2, 16, 64, 128), bf16)
    return pl.pallas_call(
        backward_kernel,
        grid=(2,),
        in_specs=[crop(a.shape) for a in ins] + [pl.BlockSpec(kern.shape, lambda b: (0, 0, 0), pipeline_mode=pl.Buffered(1))],
        out_specs=crop(out.shape),
        out_shape=out,
        scratch_shapes=[pltpu.VMEM((18, 64, 1152), bf16)],
        compiler_params=pltpu.CompilerParams(vmem_limit_bytes=30 * 2**20),
        cost_estimate=pl.CostEstimate(flops=4 * 10**9, bytes_accessed=3 * 10**6, transcendentals=0),
        name="backward",
    )(*ins, kern)


def flip_pairs(count, bit):
    return [(i, i ^ bit) for i in range(count)]


def odd_pairs(count, stride, length):
    pairs = []
    for i in range(count):
        coord = i // stride % length
        other = coord + 1 if coord % 2 == 1 else coord - 1
        if 0 <= other < length:
            pairs.append((i, i + (other - coord) * stride))
    return pairs


def swap_layers(first, last, coord, stride, length):
    devices = lax.axis_size("space")
    even = coord % 2 == 0
    inner = lax.ppermute(jnp.where(even, last, first), "space", flip_pairs(devices, stride))
    if length == 2:
        outer = jnp.zeros_like(inner)
    else:
        outer = lax.ppermute(
            jnp.where(even, first, last), "space", odd_pairs(devices, stride, length)
        )
    return jnp.where(even, outer, inner), jnp.where(even, inner, outer)


def core_swap(value):
    return lax.ppermute(value, "sample", flip_pairs(lax.axis_size("sample"), 1))


def chip_swap(value):
    return lax.ppermute(value, "sample", flip_pairs(lax.axis_size("sample"), 2))


def halves_joined(mine, other, core, dim):
    low = jnp.where(core == 0, mine, other)
    high = jnp.where(core == 0, other, mine)
    return jnp.concatenate([low, high], dim)


def coords():
    place = lax.axis_index("space")
    return place // (GZ * GY), place // GZ % GY, place % GZ


def side_halo(center):
    _, coord_y, coord_z = coords()
    devices = lax.axis_size("space")
    face = jnp.where(coord_y == 0, center[:, :, -1], center[:, :, 0])
    got = lax.ppermute(face, "space", flip_pairs(devices, GZ))
    none = jnp.zeros_like(got)
    ylo, yhi = jnp.where(coord_y == 0, none, got), jnp.where(coord_y == 0, got, none)
    first, last = (
        jnp.concatenate([ylo[:, :, None, at], center[:, :, :, at], yhi[:, :, None, at]], 2)
        for at in (0, center.shape[3] - 1)
    )
    zlo, zhi = swap_layers(first, last, coord_z, 1, GZ)
    return ylo, yhi, zlo, zhi


def half_kernels(rows, core):
    devices = lax.axis_size("space")
    half = rows.shape[0] // 2
    mine = lax.dynamic_slice_in_dim(rows, core * half, half, 0)
    copies = jnp.broadcast_to(mine, (devices, *mine.shape))
    got = lax.all_to_all(copies, "space", split_axis=0, concat_axis=0, tiled=True)
    return got, core_swap(got)


def own_rows_sum(parts, core):
    mine = lax.dynamic_index_in_dim(parts, core, 0, False)
    away = lax.dynamic_index_in_dim(parts, 1 - core, 0, False)
    chip = mine.astype(f32) + core_swap(away).astype(f32)
    arrived = lax.all_to_all(chip.astype(bf16), "space", split_axis=0, concat_axis=0, tiled=True)
    owned = arrived.astype(f32).sum(axis=0)
    owned = owned + chip_swap(owned)
    return halves_joined(owned, core_swap(owned), core, 0)


def local(acts, weight, moment, second, cotangent):
    field = acts[:, 0]
    grad_out = cotangent[:, 0]
    crops, nx, ny, nz, channels = field.shape
    core = lax.axis_index("sample") % 2
    coord_x = coords()[0]
    mine, other = half_kernels(weight.astype(bf16), core)
    first = jnp.concatenate([field[:, :2], grad_out[:, :1]], 1)
    last = jnp.concatenate([field[:, -2:], grad_out[:, -1:]], 1)
    groups = lax.axis_size("space") // (GY * GZ)
    below, above = swap_layers(first, last, coord_x, GY * GZ, groups)
    center = jnp.concatenate([below[:, :2], field, above[:, :2]], 1)
    dy = jnp.concatenate([below[:, 2:], grad_out, above[:, 2:]], 1)
    total = crops * lax.axis_size("sample") * lax.axis_size("space") * nx * ny * nz
    output, dz, parts, kernel = forward(
        jnp.full((1,), core, jnp.int32),
        center,
        *side_halo(center),
        dy.reshape(crops, nx + 2, ny * nz, channels),
        mine,
        other,
        float(total) ** (-0.5),
    )
    dz = dz.reshape(crops, nx + 2, ny, nz, channels)
    taps = kernel.reshape(3, 3, 3, channels, channels)
    flipped = jnp.flip(taps, (0, 1, 2)).transpose(0, 1, 2, 4, 3).reshape(kernel.shape)
    input_grad = backward(dz, *side_halo(dz), flipped)
    weight_grad = own_rows_sum(parts, core)
    new_moment = 0.9 * moment + 0.1 * weight_grad
    new_second = 0.999 * second + 0.001 * weight_grad * weight_grad
    first_fix = 1.0 - 0.9**10
    second_fix = 1.0 - 0.999**10
    new_weight = weight - 0.001 * (new_moment / first_fix) / (
        jnp.sqrt(new_second / second_fix) + 1e-08
    )
    return (
        output.reshape(acts.shape),
        input_grad.reshape(acts.shape),
        weight_grad,
        new_weight,
        new_moment,
        new_second,
    )


def solution(mesh):
    in_specs = (
        P("sample", "space", None, None, None, None),
        P("space", None),
        P("space", None),
        P("space", None),
        P("sample", "space", None, None, None, None),
    )
    out_specs = (
        P("sample", "space", None, None, None, None),
        P("sample", "space", None, None, None, None),
        P("space", None),
        P("space", None),
        P("space", None),
        P("space", None),
    )
    return jax.shard_map(local, mesh=mesh, in_specs=in_specs, out_specs=out_specs, check_vma=False)
```

time: 139 us -> 117 us (0.84)
  matrix products: 23.4 us -> 0 us
  Pallas kernels: 0 us -> 19.8 us
  starting transfers between devices: 64.4 us -> 51.9 us
  other arithmetic: 14.6 us -> 5.02 us
  waiting for transfers between devices: 26.3 us -> 30.9 us
    ppermute x6 -> x3, waiting for transfers between devices: 25.9 us -> 4.38 us  [swap_layers(): lax.ppermute(jnp.where(even, last, first), 'space', flip_pairs(devices, s...]
    pallas_call x0 -> x2, Pallas kernels: none -> 19.8 us  [the longest x1 13.3 us: forward(): pl.pallas_call(functools.partial(forward_kernel, scale), grid=(2,), in_sp...]
    ppermute x6 -> x3, starting transfers between devices: 28.7 us -> 14.2 us  [swap_layers(): lax.ppermute(jnp.where(even, last, first), 'space', flip_pairs(devices, s...]
    ppermute x0 -> x2, waiting for transfers between devices: none -> 14.3 us  [side_halo(): got = lax.ppermute(face, 'space', flip_pairs(devices, GZ))]
    conv_general_dilated x2 -> x0, matrix products: 13.5 us -> none  [convolve(): lax.conv_general_dilated(field, kernel, (1, 1, 1), 'VALID', dimension_num...]
    all_to_all x2, waiting for transfers between devices: 0.01 us -> 9.99 us  [the longest x1 9.83 us: own_rows_sum(): lax.all_to_all(chip.astype(bf16), 'space', split_axis=0, concat_axis=0, t...]
    dot_general x27 -> x0, matrix products: 9.92 us -> none  [kernel_terms(): lax.dot_general(window, grad_pre, (((0, 1, 2, 3), (0, 1, 2, 3)), ((), ())...]
    concatenate x5 -> x2, other arithmetic: 7.18 us -> 0.16 us  [the longest x1 0.08 us: local(): center = jnp.concatenate([below[:, :2], field, above[:, :2]], 1)]
  transfers between devices with their start and end apart: 16 -> 14, of which waited for: 5 -> 6; matrix products, arithmetic and copies ran while one was open for 12% -> 7% of each run, Pallas kernels for 0% -> 6%
where the time goes in v2:
time: 117 us; the launch traced here: 116 us
  starting transfers between devices  51.9 us (44%)
  waiting for transfers between devices  30.9 us (26%)
  Pallas kernels  19.8 us (17%)
  local copies, waits for them, and re-layouts  7.65 us (7%)
  other arithmetic  5.02 us (4%)
    ppermute x2, waiting for transfers between devices, side_halo(): got = lax.ppermute(face, 'space', flip_pairs(devices, GZ))  14.3 us
    ppermute x3, starting transfers between devices, swap_layers(): lax.ppermute(jnp.where(even, last, first), 'space', flip_pairs(devices, s...  14.2 us
    pallas_call x1, Pallas kernels, forward(): pl.pallas_call(functools.partial(forward_kernel, scale), grid=(2,), in_sp...  13.3 us
    all_to_all x1, starting transfers between devices, half_kernels(): lax.all_to_all(copies, 'space', split_axis=0, concat_axis=0, tiled=True)  12.7 us
    all_to_all x1, waiting for transfers between devices, own_rows_sum(): lax.all_to_all(chip.astype(bf16), 'space', split_axis=0, concat_axis=0, t...  9.83 us
    ppermute x3, starting transfers between devices, core_swap(): return lax.ppermute(value, 'sample', flip_pairs(lax.axis_size('sample'), 1))  8.77 us
    all_to_all x1, starting transfers between devices, own_rows_sum(): lax.all_to_all(chip.astype(bf16), 'space', split_axis=0, concat_axis=0, t...  8.22 us
    pallas_call x1, Pallas kernels, backward(): pl.pallas_call(backward_kernel, grid=(2,), in_specs=[crop(a.shape) for a...  6.55 us
  transfers between devices with their start and end apart: 14, of which 6 were waited for; matrix products, arithmetic and copies ran while one was open for 7% of the time, Pallas kernels for 6%

profile of v2, /device:TPU:1, one launch (start us, length us, event | category | flops | bytes accessed | tf_op | source)
XLA Modules:
  0.0 116.3 jit_solution(3595004057762096868)
XLA Ops:
  0.7 1.2 %copy.49 = bf16[2,1,16,8,8,128]{5,4,2,0,3,1:T(8,128)(2,1)S(1)} copy(bf16[2,1,16,8,8,128]{5,4,3,2,1,0:T(8,128)(2,1)} %param.5) | data formatting | bytes 1048576 | tf_op args[0]
  2.8 9.1 %collective-permute-start.1 = (bf16[2,3,8,8,128]{4,3,1,0,2:T(8,128)(2,1)S(1)}, bf16[2,3,8,8,128]{4,3,1,0,2:T(8,128)(2,1)S(1)}, u32[]{:S(2)}, u32[]{:S(2)}) collective-permute-start(bf16[2,3,8,8,128]{4,3,1,0,2:T(8,128)(2,1)S(1)} %get-tuple-element.49), channel_id=1, source_target_pairs={{0,8},{1,9},{2,10},{3,11},{4,12},{5,13},{6,14},{7,15},{8,0},{9,1},... | collective-permute-start | bytes 294920 | tf_op jit(solution)/shard_map/ppermute | solution.py:185
  12.6 0.9 broadcast_in_dim.14
  13.5 12.7 %all-to-all-start = ((bf16[64,27,128]{2,1,0:T(8,128)(2,1)}), bf16[64,27,128]{2,1,0:T(8,128)(2,1)S(1)}, u32[]{:S(2)}, u32[]{:S(2)}) async-start(bf16[64,27,128]{2,1,0:T(8,128)(2,1)} %broadcast_in_dim.14), calls=%async_computation | async-start | bytes 1048576 | tf_op jit(solution)/shard_map/all_to_all | solution.py:234
  26.7 2.0 %collective-permute-start.2 = (bf16[2,20,8,128]{3,2,1,0:T(8,128)(2,1)S(1)}, bf16[2,20,8,128]{3,2,1,0:T(8,128)(2,1)S(1)}, u32[]{:S(2)}, u32[]{:S(2)}) collective-permute-start(bf16[2,20,8,128]{3,2,1,0:T(8,128)(2,1)S(1)} %fusion.1), channel_id=1, source_target_pairs={{0,4},{1,5},{2,6},{3,7},{4,0},{5,1},{6,2},{7,3},{8,12},{9,13},{10,... | collective-permute-start | bytes 245768 | tf_op jit(solution)/shard_map/ppermute | solution.py:218
  29.0 14.3 %collective-permute-done.2 = bf16[2,20,8,128]{3,2,1,0:T(8,128)(2,1)S(1)} collective-permute-done((bf16[2,20,8,128]{3,2,1,0:T(8,128)(2,1)S(1)}, bf16[2,20,8,128]{3,2,1,0:T(8,128)(2,1)S(1)}, u32[]{:S(2)}, u32[]{:S(2)}) %collective-permute-start.2) | collective-permute-done | bytes 81952 | tf_op jit(solution)/shard_map/ppermute | solution.py:218
  43.5 5.4 %collective-permute-start.5 = (bf16[64,27,128]{2,1,0:T(8,128)(2,1)S(1)}, bf16[64,27,128]{2,1,0:T(8,128)(2,1)S(1)}, u32[]{:S(2)}, u32[]{:S(2)}) collective-permute-start(bf16[64,27,128]{2,1,0:T(8,128)(2,1)S(1)} %all-to-all-done.mine), channel_id=1, source_target_pairs={{0,64},{64,0},{128,192},{192,128},{1,65},{65,1},{129,193},{193,129... | collective-permute-start | bytes 1327112 | tf_op jit(solution)/shard_map/ppermute | solution.py:196
  49.8 1.7 %collective-permute-start.4 = (bf16[2,20,10,128]{3,2,1,0:T(8,128)(2,1)S(1)}, bf16[2,20,10,128]{3,2,1,0:T(8,128)(2,1)S(1)}, u32[]{:S(2)}, u32[]{:S(2)}) collective-permute-start(bf16[2,20,10,128]{3,2,1,0:T(8,128)(2,1)S(1)} %get-tuple-element.42), channel_id=1, source_target_pairs={{0,1},{1,0},{2,3},{3,2},{4,5},{5,4},{6,7},{7,6},{8,9},{9,8},{10,11... | collective-permute-start | bytes 307208 | tf_op jit(solution)/shard_map/ppermute | solution.py:185
  51.6 4.4 %collective-permute-done.4 = bf16[2,20,10,128]{3,2,1,0:T(8,128)(2,1)S(1)} collective-permute-done((bf16[2,20,10,128]{3,2,1,0:T(8,128)(2,1)S(1)}, bf16[2,20,10,128]{3,2,1,0:T(8,128)(2,1)S(1)}, u32[]{:S(2)}, u32[]{:S(2)}) %collective-permute-start.4) | collective-permute-done | bytes 102432 | tf_op jit(solution)/shard_map/ppermute | solution.py:185
  56.0 13.3 %forward.1 = (bf16[2,16,64,128]{3,2,1,0:T(8,128)(2,1)}, bf16[2,18,64,128]{3,2,1,0:T(8,128)(2,1)S(1)}, bf16[2,64,27,128]{3,2,1,0:T(8,128)(2,1)S(1)}, bf16[3,1152,128]{2,1,0:T(8,128)(2,1)S(1)}) custom-call(s32[1]{0:T(128)} %bitcast.core_ref, bf16[2,20,8,8,128]{4,3,2,1,0:T(8,128)(2,1)S(1)} %copy.30.center, bf16[2,20,8,128]{3,2,1,0:T(8,128)(2,1)S(1)} %get-tuple-element.55.ylo, ...), custom_call_target="tpu_custom_call" | custom-call | flops 8000000000 | bytes 8000000 | tf_op jit(solution)/shard_map/forward/pallas_call | solution.py:120
  69.3 0.8 copy-done
  70.1 0.8 dynamic-slice_bitcast_fusion
  72.3 1.1 collective-permute-done.9
  73.4 0.9 fusion
  74.3 8.2 %all-to-all-start.1 = ((bf16[64,27,128]{2,1,0:T(8,128)(2,1)}), bf16[64,27,128]{2,1,0:T(8,128)(2,1)}, u32[]{:S(2)}, u32[]{:S(2)}) async-start(bf16[64,27,128]{2,1,0:T(8,128)(2,1)} %fusion), calls=%async_computation.1 | async-start | bytes 1048576 | tf_op jit(solution)/shard_map/all_to_all | solution.py:242
  82.8 1.4 %copy.33 = bf16[3,3,3,128,128]{3,4,2,1,0:T(8,128)(2,1)S(1)} copy(bf16[3,3,3,128,128]{4,3,2,1,0:T(8,128)(2,1)S(1)} %bitcast.53) | data formatting | bytes 1769472 | tf_op jit(solution)/shard_map/reshape | solution.py:272
  84.3 0.9 broadcast_select_fusion.14
  86.2 3.4 %collective-permute-start.8 = (bf16[2,18,10,128]{3,2,1,0:T(8,128)(2,1)S(1)}, bf16[2,18,10,128]{3,2,1,0:T(8,128)(2,1)S(1)}, u32[]{:S(2)}, u32[]{:S(2)}) collective-permute-start(bf16[2,18,10,128]{3,2,1,0:T(8,128)(2,1)S(1)} %get-tuple-element.44), channel_id=1, source_target_pairs={{0,1},{1,0},{2,3},{3,2},{4,5},{5,4},{6,7},{7,6},{8,9},{9,8},{10,11... | collective-permute-start | bytes 276488 | tf_op jit(solution)/shard_map/ppermute | solution.py:185
  89.6 9.8 %all-to-all-done.1 = bf16[64,27,128]{2,1,0:T(8,128)(2,1)} async-done(((bf16[64,27,128]{2,1,0:T(8,128)(2,1)}), bf16[64,27,128]{2,1,0:T(8,128)(2,1)}, u32[]{:S(2)}, u32[]{:S(2)}) %all-to-all-start.1) | async-done | bytes 442400 | tf_op jit(solution)/shard_map/all_to_all | solution.py:242
  99.4 1.1 convert_reduce_fusion
  100.6 3.9 %collective-permute-start.10 = (f32[27,128]{1,0:T(8,128)S(1)}, f32[27,128]{1,0:T(8,128)S(1)}, u32[]{:S(2)}, u32[]{:S(2)}) collective-permute-start(f32[27,128]{1,0:T(8,128)S(1)} %convert_reduce_fusion), channel_id=1, source_target_pairs={{0,128},{64,192},{128,0},{192,64},{1,129},{65,193},{129,1},{193,65... | collective-permute-start | bytes 41480 | tf_op jit(solution)/shard_map/ppermute | solution.py:200
  104.6 1.1 collective-permute-done.10
  105.7 2.7 %collective-permute-start.11 = (f32[27,128]{1,0:T(8,128)S(1)}, f32[27,128]{1,0:T(8,128)S(1)}, u32[]{:S(2)}, u32[]{:S(2)}) collective-permute-start(f32[27,128]{1,0:T(8,128)S(1)} %add.59), channel_id=1, source_target_pairs={{0,64},{64,0},{128,192},{192,128},{1,65},{65,1},{129,193},{193,129... | collective-permute-start | bytes 41480 | tf_op jit(solution)/shard_map/ppermute | solution.py:196
  108.4 6.5 %backward.1 = bf16[2,16,64,128]{3,2,1,0:T(8,128)(2,1)} custom-call(bf16[2,18,8,8,128]{4,3,2,1,0:T(8,128)(2,1)S(1)} %bitcast.56, bf16[2,18,8,128]{3,2,1,0:T(8,128)(2,1)S(1)} %get-tuple-element.61.ylo, bf16[2,18,8,128]{3,2,1,0:T(8,128)(2,1)S(1)} %get-tuple-element.60.yhi, bf16[2,18,10,128]{3,2,1,0:T(8,128)(2,1)S(1)} %get-tuple-element.41.zlo, ...), custom_call_target="tpu_custom_call" | custom-call | flops 4000000000 | bytes 3000000 | tf_op jit(solution)/shard_map/backward/pallas_call | solution.py:155
  (56 shorter events, 7.4 us)
Async XLA Ops:
  0.7 1.3 %copy-start.2 = (bf16[2,1,16,8,8,128]{5,4,3,2,1,0:T(8,128)(2,1)S(1)}, bf16[2,1,16,8,8,128]{5,4,3,2,1,0:T(8,128)(2,1)}, u32[]{:S(2)}) copy-start(bf16[2,1,16,8,8,128]{5,4,3,2,1,0:T(8,128)(2,1)} %param.9) | copy-start | bytes 1572868
  2.1 24.2 %collective-permute-start = (bf16[2,3,8,8,128]{4,3,1,0,2:T(8,128)(2,1)S(1)}, bf16[2,3,8,8,128]{4,3,1,0,2:T(8,128)(2,1)S(1)}, u32[]{:S(2)}, u32[]{:S(2)}) collective-permute-start(bf16[2,3,8,8,128]{4,3,1,0,2:T(8,128)(2,1)S(1)} %get-tuple-element.48), channel_id=1, source_target_pairs={{8,16},{9,17},{10,18},{11,19},{12,20},{13,21},{14,22},{15,23},{16,... | collective-permute-start | bytes 294920 | tf_op jit(solution)/shard_map/ppermute | solution.py:189
  2.8 23.5 %collective-permute-start.1 = (bf16[2,3,8,8,128]{4,3,1,0,2:T(8,128)(2,1)S(1)}, bf16[2,3,8,8,128]{4,3,1,0,2:T(8,128)(2,1)S(1)}, u32[]{:S(2)}, u32[]{:S(2)}) collective-permute-start(bf16[2,3,8,8,128]{4,3,1,0,2:T(8,128)(2,1)S(1)} %get-tuple-element.49), channel_id=1, source_target_pairs={{0,8},{1,9},{2,10},{3,11},{4,12},{5,13},{6,14},{7,15},{8,0},{9,1},... | collective-permute-start | bytes 294920 | tf_op jit(solution)/shard_map/ppermute | solution.py:185
  13.5 30.0 %all-to-all-start = ((bf16[64,27,128]{2,1,0:T(8,128)(2,1)}), bf16[64,27,128]{2,1,0:T(8,128)(2,1)S(1)}, u32[]{:S(2)}, u32[]{:S(2)}) async-start(bf16[64,27,128]{2,1,0:T(8,128)(2,1)} %broadcast_in_dim.14), calls=%async_computation | async-start | bytes 1048576 | tf_op jit(solution)/shard_map/all_to_all | solution.py:234
  26.7 16.6 %collective-permute-start.2 = (bf16[2,20,8,128]{3,2,1,0:T(8,128)(2,1)S(1)}, bf16[2,20,8,128]{3,2,1,0:T(8,128)(2,1)S(1)}, u32[]{:S(2)}, u32[]{:S(2)}) collective-permute-start(bf16[2,20,8,128]{3,2,1,0:T(8,128)(2,1)S(1)} %fusion.1), channel_id=1, source_target_pairs={{0,4},{1,5},{2,6},{3,7},{4,0},{5,1},{6,2},{7,3},{8,12},{9,13},{10,... | collective-permute-start | bytes 245768 | tf_op jit(solution)/shard_map/ppermute | solution.py:218
  43.5 12.5 %collective-permute-start.5 = (bf16[64,27,128]{2,1,0:T(8,128)(2,1)S(1)}, bf16[64,27,128]{2,1,0:T(8,128)(2,1)S(1)}, u32[]{:S(2)}, u32[]{:S(2)}) collective-permute-start(bf16[64,27,128]{2,1,0:T(8,128)(2,1)S(1)} %all-to-all-done.mine), channel_id=1, source_target_pairs={{0,64},{64,0},{128,192},{192,128},{1,65},{65,1},{129,193},{193,129... | collective-permute-start | bytes 1327112 | tf_op jit(solution)/shard_map/ppermute | solution.py:196
  49.1 2.5 %collective-permute-start.3 = (bf16[2,20,10,128]{3,2,1,0:T(8,128)(2,1)S(1)}, bf16[2,20,10,128]{3,2,1,0:T(8,128)(2,1)S(1)}, u32[]{:S(2)}, u32[]{:S(2)}) collective-permute-start(bf16[2,20,10,128]{3,2,1,0:T(8,128)(2,1)S(1)} %get-tuple-element.43), channel_id=1, source_target_pairs={{1,2},{2,1},{5,6},{6,5},{9,10},{10,9},{13,14},{14,13},{17,18},{18,... | collective-permute-start | bytes 307208 | tf_op jit(solution)/shard_map/ppermute | solution.py:189
  49.8 6.2 %collective-permute-start.4 = (bf16[2,20,10,128]{3,2,1,0:T(8,128)(2,1)S(1)}, bf16[2,20,10,128]{3,2,1,0:T(8,128)(2,1)S(1)}, u32[]{:S(2)}, u32[]{:S(2)}) collective-permute-start(bf16[2,20,10,128]{3,2,1,0:T(8,128)(2,1)S(1)} %get-tuple-element.42), channel_id=1, source_target_pairs={{0,1},{1,0},{2,3},{3,2},{4,5},{5,4},{6,7},{7,6},{8,9},{9,8},{10,11... | collective-permute-start | bytes 307208 | tf_op jit(solution)/shard_map/ppermute | solution.py:185
  69.3 0.8 copy-start
  70.1 1.5 %copy-start.1 = (bf16[2,18,64,128]{3,2,1,0:T(8,128)(2,1)S(1)}, bf16[2,18,64,128]{3,2,1,0:T(8,128)(2,1)}, u32[]{:S(2)}) copy-start(bf16[2,18,64,128]{3,2,1,0:T(8,128)(2,1)} %copy-done) | copy-start | bytes 1769476
  71.0 2.4 %collective-permute-start.9 = (bf16[64,27,128]{2,1,0:T(8,128)(2,1)}, bf16[64,27,128]{2,1,0:T(8,128)(2,1)S(1)}, u32[]{:S(2)}, u32[]{:S(2)}) collective-permute-start(bf16[64,27,128]{2,1,0:T(8,128)(2,1)} %dynamic-slice_bitcast_fusion), channel_id=1, source_target_pairs={{0,64},{64,0},{128,192},{192,128},{1,65},{65,1},{129,193},{193,129... | collective-permute-start | bytes 1327112 | tf_op jit(solution)/shard_map/ppermute | solution.py:196
  72.3 12.0 %collective-permute-start.6 = (bf16[2,18,8,128]{3,2,1,0:T(8,128)(2,1)}, bf16[2,18,8,128]{3,2,1,0:T(8,128)(2,1)}, u32[]{:S(2)}, u32[]{:S(2)}) collective-permute-start(bf16[2,18,8,128]{3,2,1,0:T(8,128)(2,1)} %fusion.3), channel_id=1, source_target_pairs={{0,4},{1,5},{2,6},{3,7},{4,0},{5,1},{6,2},{7,3},{8,12},{9,13},{10,... | collective-permute-start | bytes 221192 | tf_op jit(solution)/shard_map/ppermute | solution.py:218
  74.3 25.1 %all-to-all-start.1 = ((bf16[64,27,128]{2,1,0:T(8,128)(2,1)}), bf16[64,27,128]{2,1,0:T(8,128)(2,1)}, u32[]{:S(2)}, u32[]{:S(2)}) async-start(bf16[64,27,128]{2,1,0:T(8,128)(2,1)} %fusion), calls=%async_computation.1 | async-start | bytes 1048576 | tf_op jit(solution)/shard_map/all_to_all | solution.py:242
  85.5 19.1 %collective-permute-start.7 = (bf16[2,18,10,128]{3,2,1,0:T(8,128)(2,1)S(1)}, bf16[2,18,10,128]{3,2,1,0:T(8,128)(2,1)S(1)}, u32[]{:S(2)}, u32[]{:S(2)}) collective-permute-start(bf16[2,18,10,128]{3,2,1,0:T(8,128)(2,1)S(1)} %get-tuple-element.45), channel_id=1, source_target_pairs={{1,2},{2,1},{5,6},{6,5},{9,10},{10,9},{13,14},{14,13},{17,18},{18,... | collective-permute-start | bytes 276488 | tf_op jit(solution)/shard_map/ppermute | solution.py:189
  86.2 18.4 %collective-permute-start.8 = (bf16[2,18,10,128]{3,2,1,0:T(8,128)(2,1)S(1)}, bf16[2,18,10,128]{3,2,1,0:T(8,128)(2,1)S(1)}, u32[]{:S(2)}, u32[]{:S(2)}) collective-permute-start(bf16[2,18,10,128]{3,2,1,0:T(8,128)(2,1)S(1)} %get-tuple-element.44), channel_id=1, source_target_pairs={{0,1},{1,0},{2,3},{3,2},{4,5},{5,4},{6,7},{7,6},{8,9},{9,8},{10,11... | collective-permute-start | bytes 276488 | tf_op jit(solution)/shard_map/ppermute | solution.py:185
  100.6 5.1 %collective-permute-start.10 = (f32[27,128]{1,0:T(8,128)S(1)}, f32[27,128]{1,0:T(8,128)S(1)}, u32[]{:S(2)}, u32[]{:S(2)}) collective-permute-start(f32[27,128]{1,0:T(8,128)S(1)} %convert_reduce_fusion), channel_id=1, source_target_pairs={{0,128},{64,192},{128,0},{192,64},{1,129},{65,193},{129,1},{193,65... | collective-permute-start | bytes 41480 | tf_op jit(solution)/shard_map/ppermute | solution.py:200
  105.7 9.2 %collective-permute-start.11 = (f32[27,128]{1,0:T(8,128)S(1)}, f32[27,128]{1,0:T(8,128)S(1)}, u32[]{:S(2)}, u32[]{:S(2)}) collective-permute-start(f32[27,128]{1,0:T(8,128)S(1)} %add.59), channel_id=1, source_target_pairs={{0,64},{64,0},{128,192},{192,128},{1,65},{65,1},{129,193},{193,129... | collective-permute-start | bytes 41480 | tf_op jit(solution)/shard_map/ppermute | solution.py:196
  108.4 6.6 %copy-start.5 = (f32[54,128]{1,0:T(8,128)S(1)}, f32[54,128]{1,0:T(8,128)}, u32[]{:S(2)}) copy-start(f32[54,128]{1,0:T(8,128)} %param.8) | copy-start | bytes 82948
  114.9 0.7 copy-start.3
  114.9 0.8 copy-start.4

commit v3 on v2

v3 whole, which is shorter than its diff:
```python
import functools

import jax
import jax.numpy as jnp
from jax import lax
from jax.experimental import pallas as pl
from jax.experimental.pallas import tpu as pltpu
from jax.sharding import PartitionSpec as P

GY = 2
GZ = 4

root_coef = 0.7978845608
cubic_coef = 0.044715
bf16, f32 = jnp.bfloat16, jnp.float32


def activate(pre):
    square = pre * pre
    inner = root_coef * (pre + cubic_coef * pre * square)
    tval = jnp.tanh(inner)
    value = 0.5 * pre * (1.0 + tval)
    slope = 0.5 * (1.0 + tval) + 0.5 * pre * (1.0 - tval * tval) * root_coef * (
        1.0 + 3.0 * cubic_coef * square
    )
    return (value, slope)


def fill_windows(windows, start, layers, source):
    place = lax.broadcasted_iota(jnp.int32, (8, 128), 0)

    def one(x, _):
        shifted = [[], [], []]
        for row, low, high in source(x):
            lo, hi = jnp.broadcast_to(low, (8, 128)), jnp.broadcast_to(high, (8, 128))
            shifted[0].append(jnp.where(place == 0, lo, pltpu.roll(row, 1, 0)))
            shifted[1].append(row)
            shifted[2].append(jnp.where(place == 7, hi, pltpu.roll(row, 7, 0)))
        for ky in range(3):
            for kz in range(3):
                col = (ky * 3 + kz) * 128
                tile = jnp.concatenate(shifted[kz][ky : ky + 8], axis=0).astype(bf16)
                windows[start + x, :, col : col + 128] = tile
        return 0

    lax.fori_loop(0, layers, one, 0)


def z_first_source(center, zlo, zhi, ylo, yhi, ahead=0):
    def source(x):
        at = x + ahead
        wide, low, high = (ref.astype(f32) for ref in (center[0, x], zlo[0, at], zhi[0, at]))
        below, above = ylo[0, at].astype(f32), yhi[0, at].astype(f32)
        rows = [(below[0:8], below[8:9], below[9:10])]
        rows += [(wide[8 * y : 8 * y + 8], low[y : y + 1], high[y : y + 1]) for y in range(8)]
        return rows + [(above[0:8], above[8:9], above[9:10])]

    return source


def y_first_source(center, ylo, yhi, zlo, zhi):
    def source(x):
        wide, low, high = (ref.astype(f32) for ref in (center[0, x], zlo[0, x], zhi[0, x]))
        rows = [ylo[0, x].astype(f32)] + [wide[8 * y : 8 * y + 8] for y in range(8)]
        rows += [yhi[0, x].astype(f32)]
        return [(rows[y], low[y : y + 1], high[y : y + 1]) for y in range(10)]

    return source


def forward_kernel(core_ref, center, zlo, zhi, ylo, yhi, dy, below, above, mine, other,
                   out, dz, windows_out, kern, rows, values, dys):
    step = pl.program_id(0)
    core = core_ref[0]
    windows = windows_out.at[0]

    @pl.when(step == 0)
    def _():
        def piece(s, _):
            a, b = mine[s].astype(f32), other[s].astype(f32)
            rows[pl.ds(54 * s, 27), :] = jnp.where(core == 0, a, b)
            rows[pl.ds(54 * s + 27, 27), :] = jnp.where(core == 0, b, a)
            return 0
        lax.fori_loop(0, 64, piece, 0)
        for kx in range(3):
            kern[kx] = rows[1152 * kx : 1152 * (kx + 1), :].astype(bf16)

    side = (zlo, zhi, ylo, yhi)
    fill_windows(windows, 0, 2, z_first_source(below, *side))
    fill_windows(windows, 2, 16, z_first_source(center, *side, 2))
    fill_windows(windows, 18, 2, z_first_source(above, *side, 18))
    dys[0] = below[0, 2]
    dys[1:17] = dy[0]
    dys[17] = above[0, 2]

    def layer(i, _):
        x = 3 * i
        pre = jnp.zeros((192, 128), f32)
        for kx in range(3):
            lhs = windows[pl.ds(x + kx, 3)].reshape(192, 1152)
            pre += jnp.dot(lhs, kern[kx], preferred_element_type=f32)
        value, slope = activate(pre)
        grad = (dys[pl.ds(x, 3)].reshape(192, 128).astype(f32) * slope).astype(bf16)
        dz[0, pl.ds(x, 3)] = grad.reshape(3, 64, 128)
        values[pl.ds(x, 3)] = value.astype(bf16).reshape(3, 64, 128)
        return 0

    lax.fori_loop(0, 6, layer, 0)
    out[0] = values[1:17]


def crop_block(shape):
    return pl.BlockSpec((1, *shape[1:]), lambda b: (b,) + (0,) * (len(shape) - 1))


def whole_block(shape):
    return pl.BlockSpec(shape, lambda b: (0,) * len(shape), pipeline_mode=pl.Buffered(1))


def forward(core, center, zlo, zhi, ylo, yhi, dy, below, above, mine, other):
    ins = (center, zlo, zhi, ylo, yhi, dy, below, above)
    outs = [
        jax.ShapeDtypeStruct((2, 16, 64, 128), bf16),
        jax.ShapeDtypeStruct((2, 18, 64, 128), bf16),
        jax.ShapeDtypeStruct((2, 20, 64, 1152), bf16),
        jax.ShapeDtypeStruct((3, 1152, 128), bf16),
    ]
    return pl.pallas_call(
        forward_kernel,
        grid=(2,),
        in_specs=[pl.BlockSpec(memory_space=pltpu.SMEM)]
        + [crop_block(a.shape) for a in ins]
        + [whole_block(mine.shape), whole_block(other.shape)],
        out_specs=[crop_block(o.shape) for o in outs[:3]] + [whole_block(outs[3].shape)],
        out_shape=outs,
        scratch_shapes=[
            pltpu.VMEM((3488, 128), f32),
            pltpu.VMEM((18, 64, 128), bf16),
            pltpu.VMEM((18, 64, 128), bf16),
        ],
        compiler_params=pltpu.CompilerParams(vmem_limit_bytes=24 * 2**20),
        cost_estimate=pl.CostEstimate(flops=4 * 10**9, bytes_accessed=8 * 10**6, transcendentals=300000),
        name="forward",
    )(core, *ins, mine, other)


def weight_grad_kernel(scale, core_ref, windows, dz, stays, leaves, rows, dzs, total):
    step = pl.program_id(0)
    core = core_ref[0]
    own = dz[0, 1:17].reshape(1024, 128)
    dzs[...] = jnp.zeros_like(dzs)
    for kx in range(3):
        dzs[64 * kx : 64 * kx + 1024, 128 * kx : 128 * (kx + 1)] = own
    both = windows[0, 1:19].reshape(1152, 1152)
    term = lax.dot_general(dzs[...], both, (((0,), (0,)), ((), ())), preferred_element_type=f32)

    @pl.when(step == 0)
    def _():
        total[...] = term

    @pl.when(step == 1)
    def _():
        whole = (total[...] + term) * scale
        for kx in range(3):
            for t in range(9):
                block = whole[128 * kx : 128 * (kx + 1), 128 * t : 128 * (t + 1)]
                row = (kx * 9 + t) * 128
                rows[row : row + 128, :] = block.T
        def piece(s, _):
            low, high = rows[pl.ds(54 * s, 27), :], rows[pl.ds(54 * s + 27, 27), :]
            stays[s] = jnp.where(core == 0, low, high).astype(bf16)
            leaves[s] = jnp.where(core == 0, high, low).astype(bf16)
            return 0
        lax.fori_loop(0, 64, piece, 0)


def weight_grad_halves(core, windows, dz, scale):
    half = jax.ShapeDtypeStruct((64, 27, 128), bf16)
    return pl.pallas_call(
        functools.partial(weight_grad_kernel, scale),
        grid=(2,),
        in_specs=[pl.BlockSpec(memory_space=pltpu.SMEM), crop_block(windows.shape), crop_block(dz.shape)],
        out_specs=[whole_block(half.shape)] * 2,
        out_shape=[half] * 2,
        scratch_shapes=[
            pltpu.VMEM((3488, 128), f32),
            pltpu.VMEM((1152, 384), bf16),
            pltpu.VMEM((384, 1152), f32),
        ],
        compiler_params=pltpu.CompilerParams(vmem_limit_bytes=24 * 2**20),
        cost_estimate=pl.CostEstimate(flops=4 * 10**9, bytes_accessed=7 * 10**6, transcendentals=0),
        name="weight_grad_halves",
    )(core, windows, dz)


def chip_kernel(stays, got, chip):
    chip[...] = (stays[...].astype(f32) + got[...].astype(f32)).astype(bf16)


def chip_sum(stays, got):
    vmem = pl.BlockSpec(memory_space=pltpu.VMEM)
    return pl.pallas_call(
        chip_kernel,
        in_specs=[vmem, vmem],
        out_specs=vmem,
        out_shape=jax.ShapeDtypeStruct(stays.shape, bf16),
        compiler_params=pltpu.CompilerParams(vmem_limit_bytes=4 * 2**20),
        name="chip_sum",
    )(stays, got)


def backward_kernel(center, ylo, yhi, zlo, zhi, kern, out, windows):
    fill_windows(windows, 0, 18, y_first_source(center, ylo, yhi, zlo, zhi))

    def layer(i, _):
        x = 4 * i
        grad = jnp.zeros((256, 128), f32)
        for kx in range(3):
            lhs = windows[pl.ds(x + kx, 4)].reshape(256, 1152)
            grad += jnp.dot(lhs, kern[kx], preferred_element_type=f32)
        out[0, pl.ds(x, 4)] = grad.astype(bf16).reshape(4, 64, 128)
        return 0

    lax.fori_loop(0, 4, layer, 0)


def backward(center, ylo, yhi, zlo, zhi, kern):
    def crop(shape):
        return pl.BlockSpec((1, *shape[1:]), lambda b: (b,) + (0,) * (len(shape) - 1))
    ins = (center, ylo, yhi, zlo, zhi)
    out = jax.ShapeDtypeStruct((2, 16, 64, 128), bf16)
    return pl.pallas_call(
        backward_kernel,
        grid=(2,),
        in_specs=[crop(a.shape) for a in ins] + [pl.BlockSpec(kern.shape, lambda b: (0, 0, 0), pipeline_mode=pl.Buffered(1))],
        out_specs=crop(out.shape),
        out_shape=out,
        scratch_shapes=[pltpu.VMEM((18, 64, 1152), bf16)],
        compiler_params=pltpu.CompilerParams(vmem_limit_bytes=20 * 2**20),
        cost_estimate=pl.CostEstimate(flops=4 * 10**9, bytes_accessed=3 * 10**6, transcendentals=0),
        name="backward",
    )(*ins, kern)


def flip_pairs(count, bit):
    return [(i, i ^ bit) for i in range(count)]


def odd_pairs(count, stride, length):
    pairs = []
    for i in range(count):
        coord = i // stride % length
        other = coord + 1 if coord % 2 == 1 else coord - 1
        if 0 <= other < length:
            pairs.append((i, i + (other - coord) * stride))
    return pairs


def swap_layers(first, last, coord, stride, length):
    devices = lax.axis_size("space")
    even = coord % 2 == 0
    inner = lax.ppermute(jnp.where(even, last, first), "space", flip_pairs(devices, stride))
    if length == 2:
        outer = jnp.zeros_like(inner)
    else:
        outer = lax.ppermute(
            jnp.where(even, first, last), "space", odd_pairs(devices, stride, length)
        )
    return jnp.where(even, outer, inner), jnp.where(even, inner, outer)


def core_swap(value):
    return lax.ppermute(value, "sample", flip_pairs(lax.axis_size("sample"), 1))


def chip_swap(value):
    return lax.ppermute(value, "sample", flip_pairs(lax.axis_size("sample"), 2))


def halves_joined(mine, other, core, dim):
    low = jnp.where(core == 0, mine, other)
    high = jnp.where(core == 0, other, mine)
    return jnp.concatenate([low, high], dim)


def coords():
    place = lax.axis_index("space")
    return place // (GZ * GY), place // GZ % GY, place % GZ


def y_halo(first, last, after=None):
    coord_y = coords()[1]
    face = jnp.where(coord_y == 0, last, first)
    got = lax.ppermute(face, "space", flip_pairs(lax.axis_size("space"), GZ))
    got = got if after is None else gate(got, after)
    none = jnp.zeros_like(got)
    return jnp.where(coord_y == 0, none, got), jnp.where(coord_y == 0, got, none)


def y_layers(field):
    return field[:, :, :8], field[:, :, -8:]


def z_halo(first, last):
    return swap_layers(first, last, coords()[2], 1, GZ)


def z_layers(field):
    tall = field.reshape(*field.shape[:2], 8, 8, field.shape[3])
    return tall[:, :, :, 0], tall[:, :, :, 7]


def x_halo(field, dy):
    groups = lax.axis_size("space") // (GY * GZ)
    first = jnp.concatenate([field[:, :2], dy[:, :1]], 1)
    last = jnp.concatenate([field[:, -2:], dy[:, -1:]], 1)
    return swap_layers(first, last, coords()[0], GY * GZ, groups)


def gate_kernel(value, after, same):
    pass


def gate(value, after):
    space = pl.BlockSpec(memory_space=pl.ANY)
    return pl.pallas_call(
        gate_kernel,
        in_specs=[space, space],
        out_specs=space,
        out_shape=jax.ShapeDtypeStruct(value.shape, value.dtype),
        input_output_aliases={0: 0},
        compiler_params=pltpu.CompilerParams(vmem_limit_bytes=2**20),
        name="gate",
    )(value, after)


def sum_kernel(arrived, after, total):
    total[...] = arrived[...].astype(f32).sum(axis=0)


def sum_of_arrived(arrived, after):
    return pl.pallas_call(
        sum_kernel,
        in_specs=[pl.BlockSpec(memory_space=pltpu.VMEM), pl.BlockSpec(memory_space=pl.ANY)],
        out_shape=jax.ShapeDtypeStruct(arrived.shape[1:], f32),
        compiler_params=pltpu.CompilerParams(vmem_limit_bytes=4 * 2**20),
        cost_estimate=pl.CostEstimate(flops=10**6, bytes_accessed=5 * 10**5, transcendentals=0),
        name="sum_of_arrived",
    )(arrived, after)


def half_kernels(rows, core):
    devices = lax.axis_size("space")
    half = rows.shape[0] // 2
    mine = lax.dynamic_slice_in_dim(rows, core * half, half, 0)
    copies = jnp.broadcast_to(mine, (devices, *mine.shape))
    return lax.all_to_all(copies, "space", split_axis=0, concat_axis=0, tiled=True)


def local(acts, weight, moment, second, cotangent):
    crops, _, nx, ny, nz, channels = acts.shape
    field = acts.reshape(crops, nx, ny * nz, channels)
    grad_out = cotangent.reshape(field.shape)
    core = lax.axis_index("sample") % 2
    mine = half_kernels(weight.astype(bf16), core)
    below, above = x_halo(field, grad_out)

    def along(layers):
        pairs = zip(layers(below[:, :2]), layers(field), layers(above[:, :2]))
        return [jnp.concatenate(three, 1) for three in pairs]

    zlo, zhi = z_halo(*along(z_layers))
    ylo, yhi = y_halo(
        *(
            jnp.concatenate([face, zlo[:, :, at : at + 1], zhi[:, :, at : at + 1]], 2)
            for at, face in zip((0, 7), along(y_layers))
        )
    )
    total = crops * lax.axis_size("sample") * lax.axis_size("space") * nx * ny * nz
    which = jnp.full((1,), core, jnp.int32)
    mine = gate(mine, yhi)
    other = core_swap(mine)
    output, dz, windows, kernel = forward(
        which, field, zlo, zhi, ylo, yhi, grad_out, below, above, mine, other
    )
    stays, leaves = weight_grad_halves(which, windows, dz, float(total) ** (-0.5))
    chip = chip_sum(stays, core_swap(leaves))
    ylo, yhi = y_halo(*y_layers(dz), chip)
    zlo, zhi = z_halo(
        *(
            jnp.concatenate([ylo[:, :, at : at + 1], face, yhi[:, :, at : at + 1]], 2)
            for at, face in zip((0, 7), z_layers(dz))
        )
    )
    arrived = lax.all_to_all(chip, "space", split_axis=0, concat_axis=0, tiled=True)
    taps = kernel.reshape(3, 3, 3, channels, channels)
    flipped = jnp.flip(taps, (0, 1, 2)).transpose(0, 1, 2, 4, 3).reshape(kernel.shape)
    input_grad = backward(dz, ylo, yhi, zlo, zhi, flipped)
    owned = sum_of_arrived(arrived, input_grad)
    owned = owned + chip_swap(owned)
    weight_grad = halves_joined(owned, core_swap(owned), core, 0)
    new_moment = 0.9 * moment + 0.1 * weight_grad
    new_second = 0.999 * second + 0.001 * weight_grad * weight_grad
    first_fix = 1.0 - 0.9**10
    second_fix = 1.0 - 0.999**10
    new_weight = weight - 0.001 * (new_moment / first_fix) / (
        jnp.sqrt(new_second / second_fix) + 1e-08
    )
    return (
        output.reshape(acts.shape),
        input_grad.reshape(acts.shape),
        weight_grad,
        new_weight,
        new_moment,
        new_second,
    )


def solution(mesh):
    in_specs = (
        P("sample", "space", None, None, None, None),
        P("space", None),
        P("space", None),
        P("space", None),
        P("sample", "space", None, None, None, None),
    )
    out_specs = (
        P("sample", "space", None, None, None, None),
        P("sample", "space", None, None, None, None),
        P("space", None),
        P("space", None),
        P("space", None),
        P("space", None),
    )
    return jax.shard_map(local, mesh=mesh, in_specs=in_specs, out_specs=out_specs, check_vma=False)
```

time: 117 us -> 106 us (0.906)
  waiting for transfers between devices: 30.9 us -> 20.9 us
  other arithmetic: 5.02 us -> 1.19 us
  local copies, waits for them, and re-layouts: 7.65 us -> 10.8 us
  Pallas kernels: 19.8 us -> 21.1 us
  starting transfers between devices: 51.9 us -> 50.6 us
    all_to_all x1, waiting for transfers between devices: 9.83 us -> 0.56 us  [local(): lax.all_to_all(chip, 'space', split_axis=0, concat_axis=0, tiled=True)]
    ppermute x3, starting transfers between devices: 8.77 us -> 3.71 us  [core_swap(): return lax.ppermute(value, 'sample', flip_pairs(lax.axis_size('sample'), 1))]
    ppermute x2, waiting for transfers between devices: 14.3 us -> 10 us  [y_halo(): got = lax.ppermute(face, 'space', flip_pairs(lax.axis_size('space'), GZ))]
    ppermute x3, waiting for transfers between devices: 1.1 us -> 3.54 us  [core_swap(): return lax.ppermute(value, 'sample', flip_pairs(lax.axis_size('sample'), 1))]
    slice x9 -> x11, local copies, waits for them, and re-layouts: 0.56 us -> 2.99 us  [the longest x2 1.72 us: x_halo(): first = jnp.concatenate([field[:, :2], dy[:, :1]], 1)]
    all_to_all x1, starting transfers between devices: 8.22 us -> 10.5 us  [local(): lax.all_to_all(chip, 'space', split_axis=0, concat_axis=0, tiled=True)]
    ppermute x3, starting transfers between devices: 14.2 us -> 16.1 us  [swap_layers(): lax.ppermute(jnp.where(even, last, first), 'space', flip_pairs(devices, s...]
    select_n x4, other arithmetic: 1.58 us -> 0.23 us  [the longest x2 0.18 us: y_halo(): face = jnp.where(coord_y == 0, last, first)]
  transfers between devices with their start and end apart: 14 -> 14, of which waited for: 6 -> 8; matrix products, arithmetic and copies ran while one was open for 7% -> 7% of each run, Pallas kernels for 6% -> 7%
where the time goes in v3:
time: 106 us
  starting transfers between devices  50.6 us (48%)
  Pallas kernels  21.1 us (20%)
  waiting for transfers between devices  20.9 us (20%)
  local copies, waits for them, and re-layouts  10.8 us (10%)
  other arithmetic  1.19 us (1%)
  between operations  1.07 us (1%)
    ppermute x3, starting transfers between devices, swap_layers(): lax.ppermute(jnp.where(even, last, first), 'space', flip_pairs(devices, s...  16.1 us
    all_to_all x1, starting transfers between devices, half_kernels(): lax.all_to_all(copies, 'space', split_axis=0, concat_axis=0, tiled=True)  12.7 us
    all_to_all x1, starting transfers between devices, local(): lax.all_to_all(chip, 'space', split_axis=0, concat_axis=0, tiled=True)  10.5 us
    ppermute x2, waiting for transfers between devices, y_halo(): got = lax.ppermute(face, 'space', flip_pairs(lax.axis_size('space'), GZ))  10 us
    pallas_call x1, Pallas kernels, forward(): pl.pallas_call(forward_kernel, grid=(2,), in_specs=[pl.BlockSpec(memory_s...  9.12 us
    pallas_call x1, Pallas kernels, backward(): pl.pallas_call(backward_kernel, grid=(2,), in_specs=[crop(a.shape) for a...  6.6 us
    ppermute x3, waiting for transfers between devices, swap_layers(): lax.ppermute(jnp.where(even, last, first), 'space', flip_pairs(devices, s...  5.58 us
    pallas_call x1, Pallas kernels, weight_grad_halves(): pl.pallas_call(functools.partial(weight_grad_kernel, scale), grid=(2,), i...  4.29 us
  transfers between devices with their start and end apart: 14, of which 8 were waited for; matrix products, arithmetic and copies ran while one was open for 7% of the time, Pallas kernels for 7%

profile of v3, /device:TPU:1, one launch (start us, length us, event | category | flops | bytes accessed | tf_op | source)
XLA Modules:
  0.0 105.5 jit_solution(13367028113496579968)
XLA Ops:
  0.7 0.9 fusion.4
  3.1 9.1 %collective-permute-start.1 = (bf16[2,3,64,128]{3,2,1,0:T(8,128)(2,1)S(1)}, bf16[2,3,64,128]{3,2,1,0:T(8,128)(2,1)S(1)}, u32[]{:S(2)}, u32[]{:S(2)}) collective-permute-start(bf16[2,3,64,128]{3,2,1,0:T(8,128)(2,1)S(1)} %get-tuple-element.51), channel_id=1, source_target_pairs={{0,8},{1,9},{2,10},{3,11},{4,12},{5,13},{6,14},{7,15},{8,0},{9,1},... | collective-permute-start | bytes 294920 | tf_op jit(solution)/shard_map/ppermute | solution.py:262
  13.8 12.7 %all-to-all-start = ((bf16[64,27,128]{2,1,0:T(8,128)(2,1)}), bf16[64,27,128]{2,1,0:T(8,128)(2,1)S(1)}, u32[]{:S(2)}, u32[]{:S(2)}) async-start(bf16[64,27,128]{2,1,0:T(8,128)(2,1)} %broadcast_in_dim.14), calls=%async_computation | async-start | bytes 1048576 | tf_op jit(solution)/shard_map/all_to_all | solution.py:357
  26.5 1.1 %copy.44 = bf16[2,1,16,8,8,128]{5,3,2,0,4,1:T(8,128)(2,1)S(1)} copy(bf16[2,1,16,8,8,128]{5,4,3,2,1,0:T(8,128)(2,1)} %param.5) | data formatting | bytes 1048576 | tf_op args[0]
  29.5 3.5 %collective-permute-start.3 = (bf16[2,20,8,128]{3,2,1,0:T(8,128)(2,1)S(1)}, bf16[2,20,8,128]{3,2,1,0:T(8,128)(2,1)S(1)}, u32[]{:S(2)}, u32[]{:S(2)}) collective-permute-start(bf16[2,20,8,128]{3,2,1,0:T(8,128)(2,1)S(1)} %get-tuple-element.56), channel_id=1, source_target_pairs={{0,1},{1,0},{2,3},{3,2},{4,5},{5,4},{6,7},{7,6},{8,9},{9,8},{10,11... | collective-permute-start | bytes 245768 | tf_op jit(solution)/shard_map/ppermute | solution.py:262
  33.0 3.2 %collective-permute-done.3 = bf16[2,20,8,128]{3,2,1,0:T(8,128)(2,1)S(1)} collective-permute-done((bf16[2,20,8,128]{3,2,1,0:T(8,128)(2,1)S(1)}, bf16[2,20,8,128]{3,2,1,0:T(8,128)(2,1)S(1)}, u32[]{:S(2)}, u32[]{:S(2)}) %collective-permute-start.3) | collective-permute-done | bytes 81952 | tf_op jit(solution)/shard_map/ppermute | solution.py:262
  36.5 1.4 %collective-permute-start.4 = (bf16[2,20,10,128]{3,2,1,0:T(8,128)(2,1)S(1)}, bf16[2,20,10,128]{3,2,1,0:T(8,128)(2,1)S(1)}, u32[]{:S(2)}, u32[]{:S(2)}) collective-permute-start(bf16[2,20,10,128]{3,2,1,0:T(8,128)(2,1)S(1)} %maximum_select_fusion), channel_id=1, source_target_pairs={{0,4},{1,5},{2,6},{3,7},{4,0},{5,1},{6,2},{7,3},{8,12},{9,13},{10,... | collective-permute-start | bytes 307208 | tf_op jit(solution)/shard_map/ppermute | solution.py:294
  37.9 10.0 %collective-permute-done.4 = bf16[2,20,10,128]{3,2,1,0:T(8,128)(2,1)S(1)} collective-permute-done((bf16[2,20,10,128]{3,2,1,0:T(8,128)(2,1)S(1)}, bf16[2,20,10,128]{3,2,1,0:T(8,128)(2,1)S(1)}, u32[]{:S(2)}, u32[]{:S(2)}) %collective-permute-start.4) | collective-permute-done | bytes 102432 | tf_op jit(solution)/shard_map/ppermute | solution.py:294
  48.5 1.5 %collective-permute-done.5.other = bf16[64,27,128]{2,1,0:T(8,128)(2,1)S(1)} collective-permute-done((bf16[64,27,128]{2,1,0:T(8,128)(2,1)S(1)}, bf16[64,27,128]{2,1,0:T(8,128)(2,1)S(1)}, u32[]{:S(2)}, u32[]{:S(2)}) %collective-permute-start.5) | collective-permute-done | bytes 442400 | tf_op jit(solution)/shard_map/ppermute | solution.py:273
  50.1 1.0 copy-done.2
  51.1 9.1 %forward.1 = (bf16[2,16,64,128]{3,2,1,0:T(8,128)(2,1)}, bf16[2,18,64,128]{3,2,1,0:T(8,128)(2,1)S(1)}, bf16[2,20,64,1152]{3,2,1,0:T(8,128)(2,1)S(1)}, bf16[3,1152,128]{2,1,0:T(8,128)(2,1)S(1)}) custom-call(s32[1]{0:T(128)} %bitcast.core_ref, bf16[2,16,64,128]{3,2,1,0:T(8,128)(2,1)S(1)} %bitcast.45, bf16[2,20,8,128]{3,2,1,0:T(8,128)(2,1)S(1)} %get-tuple-element.55.zlo, ...), custom_call_target="tpu_custom_call" | custom-call | flops 4000000000 | bytes 8000000 | tf_op jit(solution)/shard_map/forward/pallas_call | solution.py:128
  60.2 4.3 %weight_grad_halves.1 = (bf16[64,27,128]{2,1,0:T(8,128)(2,1)S(1)}, bf16[64,27,128]{2,1,0:T(8,128)(2,1)S(1)}) custom-call(s32[1]{0:T(128)} %bitcast.core_ref, bf16[2,20,64,1152]{3,2,1,0:T(8,128)(2,1)S(1)} %get-tuple-element.14.windows, bf16[2,18,64,128]{3,2,1,0:T(8,128)(2,1)S(1)} %get-tuple-element.13.dz.center), custom_call_target="tpu_custom_call" | custom-call | flops 4000000000 | bytes 7000000 | tf_op jit(solution)/shard_map/weight_grad_halves/pallas_call | solution.py:179
  65.4 1.2 %collective-permute-done.7.got = bf16[64,27,128]{2,1,0:T(8,128)(2,1)S(1)} collective-permute-done((bf16[64,27,128]{2,1,0:T(8,128)(2,1)S(1)}, bf16[64,27,128]{2,1,0:T(8,128)(2,1)S(1)}, u32[]{:S(2)}, u32[]{:S(2)}) %collective-permute-start.7) | collective-permute-done | bytes 442400 | tf_op jit(solution)/shard_map/ppermute | solution.py:273
  66.5 0.9 chip_sum.1.after
  67.5 10.5 %all-to-all-start.1 = ((bf16[64,27,128]{2,1,0:T(8,128)(2,1)}), bf16[64,27,128]{2,1,0:T(8,128)(2,1)S(1)}, u32[]{:S(2)}, u32[]{:S(2)}) async-start(bf16[64,27,128]{2,1,0:T(8,128)(2,1)} %chip_sum.1.after), calls=%async_computation.1 | async-start | bytes 1048576 | tf_op jit(solution)/shard_map/all_to_all | solution.py:395
  79.0 3.5 %collective-permute-start.9 = (bf16[2,18,10,128]{3,2,1,0:T(8,128)(2,1)S(1)}, bf16[2,18,10,128]{3,2,1,0:T(8,128)(2,1)S(1)}, u32[]{:S(2)}, u32[]{:S(2)}) collective-permute-start(bf16[2,18,10,128]{3,2,1,0:T(8,128)(2,1)S(1)} %get-tuple-element.46), channel_id=1, source_target_pairs={{0,1},{1,0},{2,3},{3,2},{4,5},{5,4},{6,7},{7,6},{8,9},{9,8},{10,11... | collective-permute-start | bytes 276488 | tf_op jit(solution)/shard_map/ppermute | solution.py:262
  82.5 1.7 %copy.28 = bf16[3,3,3,128,128]{3,4,2,1,0:T(8,128)(2,1)} copy(bf16[3,3,3,128,128]{4,3,2,1,0:T(8,128)(2,1)S(1)} %bitcast.46) | data formatting | bytes 1769472 | tf_op jit(solution)/shard_map/reshape | solution.py:396
  84.2 1.2 %rev.4 = bf16[3,3,3,128,128]{3,4,2,1,0:T(8,128)(2,1)S(1)} reverse(bf16[3,3,3,128,128]{3,4,2,1,0:T(8,128)(2,1)} %copy.28), dimensions={0,1,2} | reverse | bytes 1769472 | tf_op jit(solution)/shard_map/jit(_flip)/rev | solution.py:397
  85.4 2.4 %collective-permute-done.9 = bf16[2,18,10,128]{3,2,1,0:T(8,128)(2,1)S(1)} collective-permute-done((bf16[2,18,10,128]{3,2,1,0:T(8,128)(2,1)S(1)}, bf16[2,18,10,128]{3,2,1,0:T(8,128)(2,1)S(1)}, u32[]{:S(2)}, u32[]{:S(2)}) %collective-permute-start.9) | collective-permute-done | bytes 92192 | tf_op jit(solution)/shard_map/ppermute | solution.py:262
  87.9 6.6 %backward.1.after = bf16[2,16,64,128]{3,2,1,0:T(8,128)(2,1)} custom-call(bf16[2,18,64,128]{3,2,1,0:T(8,128)(2,1)S(1)} %get-tuple-element.13.dz.center, bf16[2,18,8,128]{3,2,1,0:T(8,128)(2,1)S(1)} %get-tuple-element.71.ylo, bf16[2,18,8,128]{3,2,1,0:T(8,128)(2,1)S(1)} %get-tuple-element.70.yhi, bf16[2,18,10,128]{3,2,1,0:T(8,128)(2,1)S(1)} %get-tuple-element.45.zlo, ...), custom_call_target="tpu_custom_call" | custom-call | flops 4000000000 | bytes 3000000 | tf_op jit(solution)/shard_map/backward/pallas_call | solution.py:232
  95.1 1.0 copy-done.1
  96.2 4.0 %collective-permute-start.10 = (f32[27,128]{1,0:T(8,128)S(1)}, f32[27,128]{1,0:T(8,128)S(1)}, u32[]{:S(2)}, u32[]{:S(2)}) collective-permute-start(f32[27,128]{1,0:T(8,128)S(1)} %sum_of_arrived.1), channel_id=1, source_target_pairs={{0,128},{64,192},{128,0},{192,64},{1,129},{65,193},{129,1},{193,65... | collective-permute-start | bytes 41480 | tf_op jit(solution)/shard_map/ppermute | solution.py:277
  100.2 1.1 %collective-permute-done.10 = f32[27,128]{1,0:T(8,128)S(1)} collective-permute-done((f32[27,128]{1,0:T(8,128)S(1)}, f32[27,128]{1,0:T(8,128)S(1)}, u32[]{:S(2)}, u32[]{:S(2)}) %collective-permute-start.10) | collective-permute-done | bytes 13856 | tf_op jit(solution)/shard_map/ppermute | solution.py:277
  101.4 2.6 %collective-permute-start.11 = (f32[27,128]{1,0:T(8,128)S(1)}, f32[27,128]{1,0:T(8,128)S(1)}, u32[]{:S(2)}, u32[]{:S(2)}) collective-permute-start(f32[27,128]{1,0:T(8,128)S(1)} %add.45), channel_id=1, source_target_pairs={{0,64},{64,0},{128,192},{192,128},{1,65},{65,1},{129,193},{193,129... | collective-permute-start | bytes 41480 | tf_op jit(solution)/shard_map/ppermute | solution.py:273
  (60 shorter events, 9.6 us)
Async XLA Ops:
  0.6 49.5 %copy-start = (bf16[2,1,16,8,8,128]{5,4,3,2,1,0:T(8,128)(2,1)S(1)}, bf16[2,1,16,8,8,128]{5,4,3,2,1,0:T(8,128)(2,1)}, u32[]{:S(2)}) copy-start(bf16[2,1,16,8,8,128]{5,4,3,2,1,0:T(8,128)(2,1)} %param.5) | copy-start | bytes 1572868
  2.4 26.2 %collective-permute-start = (bf16[2,3,64,128]{3,2,1,0:T(8,128)(2,1)S(1)}, bf16[2,3,64,128]{3,2,1,0:T(8,128)(2,1)S(1)}, u32[]{:S(2)}, u32[]{:S(2)}) collective-permute-start(bf16[2,3,64,128]{3,2,1,0:T(8,128)(2,1)S(1)} %get-tuple-element.50), channel_id=1, source_target_pairs={{8,16},{9,17},{10,18},{11,19},{12,20},{13,21},{14,22},{15,23},{16,... | collective-permute-start | bytes 294920 | tf_op jit(solution)/shard_map/ppermute | solution.py:266
  3.1 25.5 %collective-permute-start.1 = (bf16[2,3,64,128]{3,2,1,0:T(8,128)(2,1)S(1)}, bf16[2,3,64,128]{3,2,1,0:T(8,128)(2,1)S(1)}, u32[]{:S(2)}, u32[]{:S(2)}) collective-permute-start(bf16[2,3,64,128]{3,2,1,0:T(8,128)(2,1)S(1)} %get-tuple-element.51), channel_id=1, source_target_pairs={{0,8},{1,9},{2,10},{3,11},{4,12},{5,13},{6,14},{7,15},{8,0},{9,1},... | collective-permute-start | bytes 294920 | tf_op jit(solution)/shard_map/ppermute | solution.py:262
  13.8 34.1 %all-to-all-start = ((bf16[64,27,128]{2,1,0:T(8,128)(2,1)}), bf16[64,27,128]{2,1,0:T(8,128)(2,1)S(1)}, u32[]{:S(2)}, u32[]{:S(2)}) async-start(bf16[64,27,128]{2,1,0:T(8,128)(2,1)} %broadcast_in_dim.14), calls=%async_computation | async-start | bytes 1048576 | tf_op jit(solution)/shard_map/all_to_all | solution.py:357
  28.8 4.2 %collective-permute-start.2 = (bf16[2,20,8,128]{3,2,1,0:T(8,128)(2,1)S(1)}, bf16[2,20,8,128]{3,2,1,0:T(8,128)(2,1)S(1)}, u32[]{:S(2)}, u32[]{:S(2)}) collective-permute-start(bf16[2,20,8,128]{3,2,1,0:T(8,128)(2,1)S(1)} %get-tuple-element.57), channel_id=1, source_target_pairs={{1,2},{2,1},{5,6},{6,5},{9,10},{10,9},{13,14},{14,13},{17,18},{18,... | collective-permute-start | bytes 245768 | tf_op jit(solution)/shard_map/ppermute | solution.py:266
  29.5 6.7 %collective-permute-start.3 = (bf16[2,20,8,128]{3,2,1,0:T(8,128)(2,1)S(1)}, bf16[2,20,8,128]{3,2,1,0:T(8,128)(2,1)S(1)}, u32[]{:S(2)}, u32[]{:S(2)}) collective-permute-start(bf16[2,20,8,128]{3,2,1,0:T(8,128)(2,1)S(1)} %get-tuple-element.56), channel_id=1, source_target_pairs={{0,1},{1,0},{2,3},{3,2},{4,5},{5,4},{6,7},{7,6},{8,9},{9,8},{10,11... | collective-permute-start | bytes 245768 | tf_op jit(solution)/shard_map/ppermute | solution.py:262
  36.5 11.4 %collective-permute-start.4 = (bf16[2,20,10,128]{3,2,1,0:T(8,128)(2,1)S(1)}, bf16[2,20,10,128]{3,2,1,0:T(8,128)(2,1)S(1)}, u32[]{:S(2)}, u32[]{:S(2)}) collective-permute-start(bf16[2,20,10,128]{3,2,1,0:T(8,128)(2,1)S(1)} %maximum_select_fusion), channel_id=1, source_target_pairs={{0,4},{1,5},{2,6},{3,7},{4,0},{5,1},{6,2},{7,3},{8,12},{9,13},{10,... | collective-permute-start | bytes 307208 | tf_op jit(solution)/shard_map/ppermute | solution.py:294
  47.9 2.1 %collective-permute-start.5 = (bf16[64,27,128]{2,1,0:T(8,128)(2,1)S(1)}, bf16[64,27,128]{2,1,0:T(8,128)(2,1)S(1)}, u32[]{:S(2)}, u32[]{:S(2)}) collective-permute-start(bf16[64,27,128]{2,1,0:T(8,128)(2,1)S(1)} %gate.2.mine), channel_id=1, source_target_pairs={{0,64},{64,0},{128,192},{192,128},{1,65},{65,1},{129,193},{193,129... | collective-permute-start | bytes 1327112 | tf_op jit(solution)/shard_map/ppermute | solution.py:273
  50.1 1.0 copy-start.2
  64.5 2.0 %collective-permute-start.7 = (bf16[64,27,128]{2,1,0:T(8,128)(2,1)S(1)}, bf16[64,27,128]{2,1,0:T(8,128)(2,1)S(1)}, u32[]{:S(2)}, u32[]{:S(2)}) collective-permute-start(bf16[64,27,128]{2,1,0:T(8,128)(2,1)S(1)} %get-tuple-element.16), channel_id=1, source_target_pairs={{0,64},{64,0},{128,192},{192,128},{1,65},{65,1},{129,193},{193,129... | collective-permute-start | bytes 1327112 | tf_op jit(solution)/shard_map/ppermute | solution.py:273
  65.0 13.0 %collective-permute-start.6 = (bf16[2,18,8,128]{3,2,1,0:T(8,128)(2,1)S(1)}, bf16[2,18,8,128]{3,2,1,0:T(8,128)(2,1)S(1)}, u32[]{:S(2)}, u32[]{:S(2)}) collective-permute-start(bf16[2,18,8,128]{3,2,1,0:T(8,128)(2,1)S(1)} %slice_select_fusion), channel_id=1, source_target_pairs={{0,4},{1,5},{2,6},{3,7},{4,0},{5,1},{6,2},{7,3},{8,12},{9,13},{10,... | collective-permute-start | bytes 221192 | tf_op jit(solution)/shard_map/ppermute | solution.py:294
  67.5 27.6 %all-to-all-start.1 = ((bf16[64,27,128]{2,1,0:T(8,128)(2,1)}), bf16[64,27,128]{2,1,0:T(8,128)(2,1)S(1)}, u32[]{:S(2)}, u32[]{:S(2)}) async-start(bf16[64,27,128]{2,1,0:T(8,128)(2,1)} %chip_sum.1.after), calls=%async_computation.1 | async-start | bytes 1048576 | tf_op jit(solution)/shard_map/all_to_all | solution.py:395
  78.3 7.1 %collective-permute-start.8 = (bf16[2,18,10,128]{3,2,1,0:T(8,128)(2,1)S(1)}, bf16[2,18,10,128]{3,2,1,0:T(8,128)(2,1)S(1)}, u32[]{:S(2)}, u32[]{:S(2)}) collective-permute-start(bf16[2,18,10,128]{3,2,1,0:T(8,128)(2,1)S(1)} %get-tuple-element.47), channel_id=1, source_target_pairs={{1,2},{2,1},{5,6},{6,5},{9,10},{10,9},{13,14},{14,13},{17,18},{18,... | collective-permute-start | bytes 276488 | tf_op jit(solution)/shard_map/ppermute | solution.py:266
  79.0 8.8 %collective-permute-start.9 = (bf16[2,18,10,128]{3,2,1,0:T(8,128)(2,1)S(1)}, bf16[2,18,10,128]{3,2,1,0:T(8,128)(2,1)S(1)}, u32[]{:S(2)}, u32[]{:S(2)}) collective-permute-start(bf16[2,18,10,128]{3,2,1,0:T(8,128)(2,1)S(1)} %get-tuple-element.46), channel_id=1, source_target_pairs={{0,1},{1,0},{2,3},{3,2},{4,5},{5,4},{6,7},{7,6},{8,9},{9,8},{10,11... | collective-permute-start | bytes 276488 | tf_op jit(solution)/shard_map/ppermute | solution.py:262
  87.9 17.0 %copy-start.3 = (f32[54,128]{1,0:T(8,128)S(1)}, f32[54,128]{1,0:T(8,128)}, u32[]{:S(2)}) copy-start(f32[54,128]{1,0:T(8,128)} %param.6) | copy-start | bytes 82948
  87.9 17.0 %copy-start.4 = (f32[54,128]{1,0:T(8,128)S(1)}, f32[54,128]{1,0:T(8,128)}, u32[]{:S(2)}) copy-start(f32[54,128]{1,0:T(8,128)} %param.7) | copy-start | bytes 82948
  87.9 17.0 %copy-start.5 = (f32[54,128]{1,0:T(8,128)S(1)}, f32[54,128]{1,0:T(8,128)}, u32[]{:S(2)}) copy-start(f32[54,128]{1,0:T(8,128)} %param.8) | copy-start | bytes 82948
  95.1 1.0 copy-start.1
  96.2 5.1 %collective-permute-start.10 = (f32[27,128]{1,0:T(8,128)S(1)}, f32[27,128]{1,0:T(8,128)S(1)}, u32[]{:S(2)}, u32[]{:S(2)}) collective-permute-start(f32[27,128]{1,0:T(8,128)S(1)} %sum_of_arrived.1), channel_id=1, source_target_pairs={{0,128},{64,192},{128,0},{192,64},{1,129},{65,193},{129,1},{193,65... | collective-permute-start | bytes 41480 | tf_op jit(solution)/shard_map/ppermute | solution.py:277
  101.4 3.5 %collective-permute-start.11 = (f32[27,128]{1,0:T(8,128)S(1)}, f32[27,128]{1,0:T(8,128)S(1)}, u32[]{:S(2)}, u32[]{:S(2)}) collective-permute-start(f32[27,128]{1,0:T(8,128)S(1)} %add.45), channel_id=1, source_target_pairs={{0,64},{64,0},{128,192},{192,128},{1,65},{65,1},{129,193},{193,129... | collective-permute-start | bytes 41480 | tf_op jit(solution)/shard_map/ppermute | solution.py:273

commit v4 on v3

v4 whole, which is shorter than its diff:
```python
import functools

import jax
import jax.numpy as jnp
from jax import lax
from jax.experimental import pallas as pl
from jax.experimental.pallas import tpu as pltpu
from jax.sharding import PartitionSpec as P

GY = 2
GZ = 4
FWD_VMEM = 20

root_coef = 0.7978845608
cubic_coef = 0.044715
bf16, f32 = jnp.bfloat16, jnp.float32


def activate(pre):
    square = pre * pre
    inner = root_coef * (pre + cubic_coef * pre * square)
    tval = jnp.tanh(inner)
    value = 0.5 * pre * (1.0 + tval)
    slope = 0.5 * (1.0 + tval) + 0.5 * pre * (1.0 - tval * tval) * root_coef * (
        1.0 + 3.0 * cubic_coef * square
    )
    return (value, slope)


def fill_windows(windows, start, layers, source):
    place = lax.broadcasted_iota(jnp.int32, (8, 128), 0)

    def one(x, _):
        at = start + x
        shifted = [[], [], []]
        for row, low, high in source(x):
            lo, hi = jnp.broadcast_to(low, (8, 128)), jnp.broadcast_to(high, (8, 128))
            shifted[0].append(jnp.where(place == 0, lo, pltpu.roll(row, 1, 0)))
            shifted[1].append(row)
            shifted[2].append(jnp.where(place == 7, hi, pltpu.roll(row, 7, 0)))
        for ky in range(3):
            for kz in range(3):
                col = (ky * 3 + kz) * 128
                tile = jnp.concatenate(shifted[kz][ky : ky + 8], axis=0).astype(bf16)
                windows[lax.div(at, 2), lax.rem(at, 2), :, col : col + 128] = tile
        return 0

    lax.fori_loop(0, layers, one, 0)


def z_first_source(b, center, zlo, zhi, ylo, yhi, ahead=0):
    def source(x):
        at = x + ahead
        wide, low, high = (ref.astype(f32) for ref in (center[b, x], zlo[b, at], zhi[b, at]))
        below, above = ylo[b, at].astype(f32), yhi[b, at].astype(f32)
        rows = [(below[0:8], below[8:9], below[9:10])]
        rows += [(wide[8 * y : 8 * y + 8], low[y : y + 1], high[y : y + 1]) for y in range(8)]
        return rows + [(above[0:8], above[8:9], above[9:10])]

    return source


def y_first_source(b, center, ylo, yhi, zlo, zhi):
    def source(x):
        wide, low, high = (ref.astype(f32) for ref in (center[b, x], zlo[b, x], zhi[b, x]))
        rows = [ylo[b, x].astype(f32)] + [wide[8 * y : 8 * y + 8] for y in range(8)]
        rows += [yhi[b, x].astype(f32)]
        return [(rows[y], low[y : y + 1], high[y : y + 1]) for y in range(10)]

    return source


def pair_kernels(kern, wide):
    none = jnp.zeros((1152, 128), bf16)
    for at in range(4):
        wide[at, :, 0:128] = kern[at] if at < 3 else none
        wide[at, :, 128:256] = kern[at - 1] if at > 0 else none


def pair_products(windows, wide, pairs):
    total = jnp.zeros((64 * pairs, 256), f32)
    for at in range(4):
        lhs = windows[at // 2 : at // 2 + pairs, at % 2].reshape(64 * pairs, 1152)
        total += jnp.dot(lhs, wide[at], preferred_element_type=f32)
    return total


def forward_kernel(core_ref, center, zlo, zhi, ylo, yhi, dy, below, above, mine, other,
                   out, dz, windows, kern, rows, wide):
    core = core_ref[0]

    def piece(s, _):
        a, b = mine[s].astype(f32), other[s].astype(f32)
        rows[pl.ds(54 * s, 27), :] = jnp.where(core == 0, a, b)
        rows[pl.ds(54 * s + 27, 27), :] = jnp.where(core == 0, b, a)
        return 0

    lax.fori_loop(0, 64, piece, 0)
    for kx in range(3):
        kern[kx] = rows[1152 * kx : 1152 * (kx + 1), :].astype(bf16)
    pair_kernels(kern, wide)
    side = (zlo, zhi, ylo, yhi)

    def crop(b, _):
        own = windows.at[b]
        fill_windows(own, 0, 2, z_first_source(b, below, *side))
        fill_windows(own, 2, 16, z_first_source(b, center, *side, 2))
        fill_windows(own, 18, 2, z_first_source(b, above, *side, 18))
        both = pair_products(own, wide, 9)
        for at in range(2):
            value, slope = activate(both[:, 128 * at : 128 * (at + 1)])
            grad = dy[b, :, at].reshape(576, 128).astype(f32) * slope
            dz[b, :, at] = grad.astype(bf16).reshape(9, 64, 128)
            value = value.astype(bf16).reshape(9, 64, 128)
            out[b, :, 1 - at] = value[1:9] if at == 0 else value[0:8]
        return 0

    lax.fori_loop(0, 2, crop, 0)


VMEM = pl.BlockSpec(memory_space=pltpu.VMEM)
SMEM = pl.BlockSpec(memory_space=pltpu.SMEM)
ANY = pl.BlockSpec(memory_space=pl.ANY)


def forward(core, center, zlo, zhi, ylo, yhi, dy, below, above, mine, other):
    ins = (center, zlo, zhi, ylo, yhi, dy.reshape(2, 9, 2, 64, 128), below, above, mine, other)
    outs = [
        jax.ShapeDtypeStruct((2, 8, 2, 64, 128), bf16),
        jax.ShapeDtypeStruct((2, 9, 2, 64, 128), bf16),
        jax.ShapeDtypeStruct((2, 10, 2, 64, 1152), bf16),
        jax.ShapeDtypeStruct((3, 1152, 128), bf16),
    ]
    out, dz, windows, kern = pl.pallas_call(
        forward_kernel,
        in_specs=[SMEM] + [VMEM] * len(ins),
        out_specs=[VMEM] * 4,
        out_shape=outs,
        scratch_shapes=[pltpu.VMEM((3488, 128), f32), pltpu.VMEM((4, 1152, 256), bf16)],
        compiler_params=pltpu.CompilerParams(vmem_limit_bytes=FWD_VMEM * 2**20),
        cost_estimate=pl.CostEstimate(flops=4 * 10**9, bytes_accessed=8 * 10**6, transcendentals=300000),
        name="forward",
    )(core, *ins)
    return out, dz.reshape(2, 18, 64, 128), windows.reshape(2, 20, 64, 1152), kern


def weight_grad_kernel(scale, core_ref, windows, dz, stays, leaves, rows, dzs, total):
    core = core_ref[0]
    dzs[...] = jnp.zeros_like(dzs)
    for b in range(2):
        own = dz[b, 1:17].reshape(1024, 128)
        for kx in range(3):
            dzs[64 * kx : 64 * kx + 1024, 128 * kx : 128 * (kx + 1)] = own
        both = windows[b, 1:19].reshape(1152, 1152)
        term = lax.dot_general(dzs[...], both, (((0,), (0,)), ((), ())), preferred_element_type=f32)
        if b == 0:
            total[...] = term
    whole = (total[...] + term) * scale
    for kx in range(3):
        for t in range(9):
            block = whole[128 * kx : 128 * (kx + 1), 128 * t : 128 * (t + 1)]
            row = (kx * 9 + t) * 128
            rows[row : row + 128, :] = block.T

    def piece(s, _):
        low, high = rows[pl.ds(54 * s, 27), :], rows[pl.ds(54 * s + 27, 27), :]
        stays[s] = jnp.where(core == 0, low, high).astype(bf16)
        leaves[s] = jnp.where(core == 0, high, low).astype(bf16)
        return 0

    lax.fori_loop(0, 64, piece, 0)


def weight_grad_halves(core, windows, dz, scale):
    half = jax.ShapeDtypeStruct((64, 27, 128), bf16)
    return pl.pallas_call(
        functools.partial(weight_grad_kernel, scale),
        in_specs=[SMEM, VMEM, VMEM],
        out_specs=[VMEM] * 2,
        out_shape=[half] * 2,
        scratch_shapes=[
            pltpu.VMEM((3488, 128), f32),
            pltpu.VMEM((1152, 384), bf16),
            pltpu.VMEM((384, 1152), f32),
        ],
        compiler_params=pltpu.CompilerParams(vmem_limit_bytes=FWD_VMEM * 2**20),
        cost_estimate=pl.CostEstimate(flops=4 * 10**9, bytes_accessed=7 * 10**6, transcendentals=0),
        name="weight_grad_halves",
    )(core, windows, dz)


def chip_kernel(stays, got, chip):
    chip[...] = (stays[...].astype(f32) + got[...].astype(f32)).astype(bf16)


def chip_sum(stays, got):
    vmem = pl.BlockSpec(memory_space=pltpu.VMEM)
    return pl.pallas_call(
        chip_kernel,
        in_specs=[vmem, vmem],
        out_specs=vmem,
        out_shape=jax.ShapeDtypeStruct(stays.shape, bf16),
        compiler_params=pltpu.CompilerParams(vmem_limit_bytes=4 * 2**20),
        name="chip_sum",
    )(stays, got)


def backward_kernel(center, ylo, yhi, zlo, zhi, kern, out, token, windows, wide):
    token[...] = jnp.zeros_like(token)
    pair_kernels(kern, wide)

    def crop(b, _):
        fill_windows(windows, 0, 18, y_first_source(b, center, ylo, yhi, zlo, zhi))
        both = pair_products(windows, wide, 8).astype(bf16)
        for at in range(2):
            out[b, :, at] = both[:, 128 * at : 128 * (at + 1)].reshape(8, 64, 128)
        return 0

    lax.fori_loop(0, 2, crop, 0)


def backward(center, ylo, yhi, zlo, zhi, kern):
    return pl.pallas_call(
        backward_kernel,
        in_specs=[VMEM] * 6,
        out_specs=[VMEM] * 2,
        out_shape=[jax.ShapeDtypeStruct((2, 8, 2, 64, 128), bf16), jax.ShapeDtypeStruct((8, 128), f32)],
        scratch_shapes=[pltpu.VMEM((9, 2, 64, 1152), bf16), pltpu.VMEM((4, 1152, 256), bf16)],
        compiler_params=pltpu.CompilerParams(vmem_limit_bytes=FWD_VMEM * 2**20),
        cost_estimate=pl.CostEstimate(flops=4 * 10**9, bytes_accessed=3 * 10**6, transcendentals=0),
        name="backward",
    )(center, ylo, yhi, zlo, zhi, kern)


def flip_pairs(count, bit):
    return [(i, i ^ bit) for i in range(count)]


def odd_pairs(count, stride, length):
    pairs = []
    for i in range(count):
        coord = i // stride % length
        other = coord + 1 if coord % 2 == 1 else coord - 1
        if 0 <= other < length:
            pairs.append((i, i + (other - coord) * stride))
    return pairs


def swapped(inner, outer, even, stride, length):
    devices = lax.axis_size("space")
    inner = lax.ppermute(inner, "space", flip_pairs(devices, stride))
    outer = lax.ppermute(outer, "space", odd_pairs(devices, stride, length))
    return jnp.where(even, outer, inner), jnp.where(even, inner, outer)


def swap_layers(first, last, coord, stride, length):
    even = coord % 2 == 0
    return swapped(jnp.where(even, last, first), jnp.where(even, first, last), even, stride, length)


def core_swap(value):
    return lax.ppermute(value, "sample", flip_pairs(lax.axis_size("sample"), 1))


def chip_swap(value):
    return lax.ppermute(value, "sample", flip_pairs(lax.axis_size("sample"), 2))


def halves_joined(mine, other, core, dim):
    low = jnp.where(core == 0, mine, other)
    high = jnp.where(core == 0, other, mine)
    return jnp.concatenate([low, high], dim)


def coords():
    place = lax.axis_index("space")
    return place // (GZ * GY), place // GZ % GY, place % GZ


def y_halo(first, last, after=None):
    coord_y = coords()[1]
    face = jnp.where(coord_y == 0, last, first)
    got = lax.ppermute(face, "space", flip_pairs(lax.axis_size("space"), GZ))
    got = got if after is None else gate(got, after)
    none = jnp.zeros_like(got)
    return jnp.where(coord_y == 0, none, got), jnp.where(coord_y == 0, got, none)


def y_layers(field):
    return field[:, :, :8], field[:, :, -8:]


def z_halo(first, last):
    return swap_layers(first, last, coords()[2], 1, GZ)


def start_kernel(even_ref, core_ref, field, dy, weight, inner, outer, copies, ends, rows, wide, sems):
    def spread(at):
        return pltpu.make_async_copy(wide, copies.at[pl.ds(8 * at, 8)], sems.at[6 + at])

    fetches = [pltpu.make_async_copy(weight, rows, sems.at[0])]
    for at, x in ((0, 0), (1, 14)):
        fetches.append(pltpu.make_async_copy(field.at[:, x : x + 2], ends.at[at, :, 0:2], sems.at[1 + 2 * at]))
        x = 15 * at
        fetches.append(pltpu.make_async_copy(dy.at[:, x : x + 1], ends.at[at, :, 2:3], sems.at[2 + 2 * at]))
    for fetch in fetches:
        fetch.start()
    even, core = even_ref[0] == 1, core_ref[0]
    fetches[0].wait()
    half = jnp.where(core == 0, rows[0:27], rows[27:54]).astype(bf16)
    for at in range(8):
        wide[at] = half
    for at in range(8):
        spread(at).start()
    for fetch in fetches[1:]:
        fetch.wait()
    inner[...] = jnp.where(even, ends[1], ends[0])
    outer[...] = jnp.where(even, ends[0], ends[1])
    for at in range(8):
        spread(at).wait()


def start(even, core, field, dy, weight):
    end = jax.ShapeDtypeStruct((2, 3, 64, 128), bf16)
    return pl.pallas_call(
        start_kernel,
        in_specs=[SMEM, SMEM, ANY, ANY, ANY],
        out_specs=[VMEM, VMEM, ANY],
        out_shape=[end, end, jax.ShapeDtypeStruct((64, 27, 128), bf16)],
        scratch_shapes=[
            pltpu.VMEM((2, 2, 3, 64, 128), bf16),
            pltpu.VMEM((54, 128), f32),
            pltpu.VMEM((8, 27, 128), bf16),
            pltpu.SemaphoreType.DMA((14,)),
        ],
        name="start",
    )(even, core, field, dy, weight)


def z_edges_kernel(field, first, last, tall):
    def one(i, _):
        b, x = lax.div(i, 16), lax.rem(i, 16)
        tall[i] = field[b, x].astype(f32)
        first[b, x] = tall[i, pl.ds(0, 8, stride=8)].astype(bf16)
        last[b, x] = tall[i, pl.ds(7, 8, stride=8)].astype(bf16)
        return 0

    lax.fori_loop(0, 32, one, 0, unroll=4)


def z_edges(field):
    edge = jax.ShapeDtypeStruct((2, 16, 8, 128), bf16)
    return pl.pallas_call(
        z_edges_kernel,
        in_specs=[VMEM],
        out_specs=[VMEM] * 2,
        out_shape=[edge] * 2,
        scratch_shapes=[pltpu.VMEM((32, 64, 128), f32)],
        compiler_params=pltpu.CompilerParams(vmem_limit_bytes=4 * 2**20),
        name="z_edges",
    )(field)


def z_layers(field):
    tall = field.reshape(*field.shape[:2], 8, 8, field.shape[3])
    return tall[:, :, :, 0], tall[:, :, :, 7]


def gate_kernel(value, after, same):
    pass


def gate(value, after):
    space = pl.BlockSpec(memory_space=pl.ANY)
    return pl.pallas_call(
        gate_kernel,
        in_specs=[space, space],
        out_specs=space,
        out_shape=jax.ShapeDtypeStruct(value.shape, value.dtype),
        input_output_aliases={0: 0},
        compiler_params=pltpu.CompilerParams(vmem_limit_bytes=2**20),
        name="gate",
    )(value, after)


def sum_kernel(arrived, after, total):
    total[...] = arrived[...].astype(f32).sum(axis=0)


def sum_of_arrived(arrived, after):
    return pl.pallas_call(
        sum_kernel,
        in_specs=[pl.BlockSpec(memory_space=pltpu.VMEM), pl.BlockSpec(memory_space=pl.ANY)],
        out_shape=jax.ShapeDtypeStruct(arrived.shape[1:], f32),
        compiler_params=pltpu.CompilerParams(vmem_limit_bytes=4 * 2**20),
        cost_estimate=pl.CostEstimate(flops=10**6, bytes_accessed=5 * 10**5, transcendentals=0),
        name="sum_of_arrived",
    )(arrived, after)


def local(acts, weight, moment, second, cotangent):
    crops, _, nx, ny, nz, channels = acts.shape
    field = acts.reshape(crops, nx, ny * nz, channels)
    grad_out = cotangent.reshape(field.shape)
    core = lax.axis_index("sample") % 2
    even = coords()[0] % 2 == 0
    groups = lax.axis_size("space") // (GY * GZ)
    which = jnp.full((1,), core, jnp.int32)
    inner, outer, copies = start(jnp.full((1,), even, jnp.int32), which, field, grad_out, weight)
    mine = lax.all_to_all(copies, "space", split_axis=0, concat_axis=0, tiled=True)
    below, above = swapped(inner, outer, even, GY * GZ, groups)

    def along(layers, own):
        pairs = zip(layers(below[:, :2]), own(field), layers(above[:, :2]))
        return [jnp.concatenate(three, 1) for three in pairs]

    zlo, zhi = z_halo(*along(z_layers, z_edges))
    ylo, yhi = y_halo(
        *(
            jnp.concatenate([face, zlo[:, :, at : at + 1], zhi[:, :, at : at + 1]], 2)
            for at, face in zip((0, 7), along(y_layers, y_layers))
        )
    )
    total = crops * lax.axis_size("sample") * lax.axis_size("space") * nx * ny * nz
    mine = gate(mine, yhi)
    dy = jnp.concatenate([below[:, 2:], grad_out, above[:, 2:]], 1)
    other = core_swap(mine)
    output, dz, windows, kernel = forward(
        which, field, zlo, zhi, ylo, yhi, dy, below, above, mine, other
    )
    stays, leaves = weight_grad_halves(which, windows, dz, float(total) ** (-0.5))
    chip = chip_sum(stays, core_swap(leaves))
    ylo, yhi = y_halo(*y_layers(dz), chip)
    zlo, zhi = z_halo(
        *(
            jnp.concatenate([ylo[:, :, at : at + 1], face, yhi[:, :, at : at + 1]], 2)
            for at, face in zip((0, 7), z_layers(dz))
        )
    )
    arrived = lax.all_to_all(chip, "space", split_axis=0, concat_axis=0, tiled=True)
    taps = kernel.reshape(3, 3, 3, channels, channels)
    flipped = jnp.flip(taps, (0, 1, 2)).transpose(0, 1, 2, 4, 3).reshape(kernel.shape)
    input_grad, token = backward(dz, ylo, yhi, zlo, zhi, flipped)
    owned = sum_of_arrived(arrived, token)
    owned = owned + chip_swap(owned)
    weight_grad = halves_joined(owned, core_swap(owned), core, 0)
    new_moment = 0.9 * moment + 0.1 * weight_grad
    new_second = 0.999 * second + 0.001 * weight_grad * weight_grad
    first_fix = 1.0 - 0.9**10
    second_fix = 1.0 - 0.999**10
    new_weight = weight - 0.001 * (new_moment / first_fix) / (
        jnp.sqrt(new_second / second_fix) + 1e-08
    )
    return (
        output.reshape(acts.shape),
        input_grad.reshape(acts.shape),
        weight_grad,
        new_weight,
        new_moment,
        new_second,
    )


def solution(mesh):
    in_specs = (
        P("sample", "space", None, None, None, None),
        P("space", None),
        P("space", None),
        P("space", None),
        P("sample", "space", None, None, None, None),
    )
    out_specs = (
        P("sample", "space", None, None, None, None),
        P("sample", "space", None, None, None, None),
        P("space", None),
        P("space", None),
        P("space", None),
        P("space", None),
    )
    return jax.shard_map(local, mesh=mesh, in_specs=in_specs, out_specs=out_specs, check_vma=False)
```

time: 106 us -> 99.8 us (0.942)
  local copies, waits for them, and re-layouts: 10.8 us -> 5.28 us
  Pallas kernels: 21.1 us -> 19.1 us
    unnamed x19 -> x18, local copies, waits for them, and re-layouts: 3.29 us -> 1.11 us
    pallas_call x3 -> x5, Pallas kernels: 20 us -> 18.1 us  [the longest x1 6.79 us: forward(): pl.pallas_call(forward_kernel, in_specs=[SMEM] + [VMEM] * len(ins), out_s...]
    slice x2, local copies, waits for them, and re-layouts: 1.72 us -> 0.01 us  [local(): dy = jnp.concatenate([below[:, 2:], grad_out, above[:, 2:]], 1)]
  transfers between devices with their start and end apart: 14 -> 14, of which waited for: 8 -> 8; matrix products, arithmetic and copies ran while one was open for 7% -> 5% of each run, Pallas kernels for 7% -> 6%
where the time goes in v4:
time: 99.8 us; the launch traced here: 99.4 us
  starting transfers between devices  50.9 us (51%)
  waiting for transfers between devices  21.8 us (22%)
  Pallas kernels  19.1 us (19%)
  local copies, waits for them, and re-layouts  5.28 us (5%)
  other arithmetic  1.25 us (1%)
  between operations  1.1 us (1%)
    ppermute x3, starting transfers between devices, swapped(): inner = lax.ppermute(inner, 'space', flip_pairs(devices, stride))  16.3 us
    all_to_all x1, starting transfers between devices, local(): lax.all_to_all(copies, 'space', split_axis=0, concat_axis=0, tiled=True)  12.7 us
    all_to_all x1, starting transfers between devices, local(): lax.all_to_all(chip, 'space', split_axis=0, concat_axis=0, tiled=True)  10.6 us
    ppermute x2, waiting for transfers between devices, y_halo(): got = lax.ppermute(face, 'space', flip_pairs(lax.axis_size('space'), GZ))  9.84 us
    pallas_call x1, Pallas kernels, forward(): pl.pallas_call(forward_kernel, in_specs=[SMEM] + [VMEM] * len(ins), out_s...  6.79 us
    ppermute x3, waiting for transfers between devices, swapped(): inner = lax.ppermute(inner, 'space', flip_pairs(devices, stride))  6 us
    pallas_call x1, Pallas kernels, backward(): pl.pallas_call(backward_kernel, in_specs=[VMEM] * 6, out_specs=[VMEM] * 2...  5.22 us
    ppermute x1, starting transfers between devices, chip_swap(): return lax.ppermute(value, 'sample', flip_pairs(lax.axis_size('sample'), 2))  3.96 us
  transfers between devices with their start and end apart: 14, of which 8 were waited for; matrix products, arithmetic and copies ran while one was open for 5% of the time, Pallas kernels for 6%

profile of v4, /device:TPU:1, one launch (start us, length us, event | category | flops | bytes accessed | tf_op | source)
XLA Modules:
  0.0 99.4 jit_solution(6140744378164096266)
XLA Ops:
  0.7 2.4 %start.1 = (bf16[2,3,64,128]{3,2,1,0:T(8,128)(2,1)}, bf16[2,3,64,128]{3,2,1,0:T(8,128)(2,1)}, bf16[64,27,128]{2,1,0:T(8,128)(2,1)}) custom-call(s32[1]{0:T(128)} %bitcast.2.even_ref, s32[1]{0:T(128)} %bitcast.core_ref, bf16[2,16,64,128]{3,2,1,0:T(8,128)(2,1)} %bitcast.40, bf16[2,16,64,128]{3,2,1,0:T(8,128)(2,1)} %bitcast.52, f32[54,128]{1,0:T(8,128)} %weight.1), custom_call_target="tpu_custom_call" | custom-call | tf_op jit(solution)/shard_map/start/pallas_call | solution.py:325
  3.8 9.1 %collective-permute-start.1 = (bf16[2,3,64,128]{3,2,1,0:T(8,128)(2,1)}, bf16[2,3,64,128]{3,2,1,0:T(8,128)(2,1)S(1)}, u32[]{:S(2)}, u32[]{:S(2)}) collective-permute-start(bf16[2,3,64,128]{3,2,1,0:T(8,128)(2,1)} %get-tuple-element.20), channel_id=1, source_target_pairs={{0,8},{1,9},{2,10},{3,11},{4,12},{5,13},{6,14},{7,15},{8,0},{9,1},... | collective-permute-start | bytes 294920 | tf_op jit(solution)/shard_map/ppermute | solution.py:251
  12.9 12.7 %all-to-all-start = ((bf16[64,27,128]{2,1,0:T(8,128)(2,1)}), bf16[64,27,128]{2,1,0:T(8,128)(2,1)S(1)}, u32[]{:S(2)}, u32[]{:S(2)}) async-start(bf16[64,27,128]{2,1,0:T(8,128)(2,1)} %get-tuple-element.23), calls=%async_computation | async-start | bytes 1048576 | tf_op jit(solution)/shard_map/all_to_all | solution.py:410
  25.6 0.9 fusion.3
  26.5 1.0 %copy-done = bf16[2,1,16,8,8,128]{5,4,3,2,1,0:T(8,128)(2,1)S(1)} copy-done((bf16[2,1,16,8,8,128]{5,4,3,2,1,0:T(8,128)(2,1)S(1)}, bf16[2,1,16,8,8,128]{5,4,3,2,1,0:T(8,128)(2,1)}, u32[]{:S(2)}) %copy-start) | copy-done | bytes 524312
  28.8 3.5 %collective-permute-start.3 = (bf16[2,20,8,128]{3,2,1,0:T(8,128)(2,1)S(1)}, bf16[2,20,8,128]{3,2,1,0:T(8,128)(2,1)S(1)}, u32[]{:S(2)}, u32[]{:S(2)}) collective-permute-start(bf16[2,20,8,128]{3,2,1,0:T(8,128)(2,1)S(1)} %get-tuple-element.62), channel_id=1, source_target_pairs={{0,1},{1,0},{2,3},{3,2},{4,5},{5,4},{6,7},{7,6},{8,9},{9,8},{10,11... | collective-permute-start | bytes 245768 | tf_op jit(solution)/shard_map/ppermute | solution.py:251
  32.3 3.2 %collective-permute-done.3 = bf16[2,20,8,128]{3,2,1,0:T(8,128)(2,1)S(1)} collective-permute-done((bf16[2,20,8,128]{3,2,1,0:T(8,128)(2,1)S(1)}, bf16[2,20,8,128]{3,2,1,0:T(8,128)(2,1)S(1)}, u32[]{:S(2)}, u32[]{:S(2)}) %collective-permute-start.3) | collective-permute-done | bytes 81952 | tf_op jit(solution)/shard_map/ppermute | solution.py:251
  35.7 1.3 %collective-permute-start.4 = (bf16[2,20,10,128]{3,2,1,0:T(8,128)(2,1)S(1)}, bf16[2,20,10,128]{3,2,1,0:T(8,128)(2,1)S(1)}, u32[]{:S(2)}, u32[]{:S(2)}) collective-permute-start(bf16[2,20,10,128]{3,2,1,0:T(8,128)(2,1)S(1)} %maximum_select_fusion), channel_id=1, source_target_pairs={{0,4},{1,5},{2,6},{3,7},{4,0},{5,1},{6,2},{7,3},{8,12},{9,13},{10,... | collective-permute-start | bytes 307208 | tf_op jit(solution)/shard_map/ppermute | solution.py:283
  37.1 9.8 %collective-permute-done.4 = bf16[2,20,10,128]{3,2,1,0:T(8,128)(2,1)S(1)} collective-permute-done((bf16[2,20,10,128]{3,2,1,0:T(8,128)(2,1)S(1)}, bf16[2,20,10,128]{3,2,1,0:T(8,128)(2,1)S(1)}, u32[]{:S(2)}, u32[]{:S(2)}) %collective-permute-start.4) | collective-permute-done | bytes 102432 | tf_op jit(solution)/shard_map/ppermute | solution.py:283
  47.7 1.4 %collective-permute-done.5.other = bf16[64,27,128]{2,1,0:T(8,128)(2,1)S(1)} collective-permute-done((bf16[64,27,128]{2,1,0:T(8,128)(2,1)S(1)}, bf16[64,27,128]{2,1,0:T(8,128)(2,1)S(1)}, u32[]{:S(2)}, u32[]{:S(2)}) %collective-permute-start.5) | collective-permute-done | bytes 442400 | tf_op jit(solution)/shard_map/ppermute | solution.py:262
  49.2 6.8 %forward.1 = (bf16[2,8,2,64,128]{4,3,2,1,0:T(8,128)(2,1)}, bf16[2,9,2,64,128]{4,3,2,1,0:T(8,128)(2,1)S(1)}, bf16[2,10,2,64,1152]{4,3,2,1,0:T(8,128)(2,1)S(1)}, bf16[3,1152,128]{2,1,0:T(8,128)(2,1)S(1)}) custom-call(s32[1]{0:T(128)} %bitcast.core_ref, bf16[2,16,64,128]{3,2,1,0:T(8,128)(2,1)S(1)} %bitcast.43, ...), custom_call_target="tpu_custom_call" | custom-call | flops 4000000000 | bytes 8000000 | tf_op jit(solution)/shard_map/forward/pallas_call | solution.py:134
  56.0 3.4 %weight_grad_halves.1 = (bf16[64,27,128]{2,1,0:T(8,128)(2,1)S(1)}, bf16[64,27,128]{2,1,0:T(8,128)(2,1)S(1)}) custom-call(s32[1]{0:T(128)} %bitcast.core_ref, bf16[2,20,64,1152]{3,2,1,0:T(8,128)(2,1)S(1)} %bitcast.51, bf16[2,18,64,128]{3,2,1,0:T(8,128)(2,1)S(1)} %bitcast.47), custom_call_target="tpu_custom_call" | custom-call | flops 4000000000 | bytes 7000000 | tf_op jit(solution)/shard_map/weight_grad_halves/pallas_call | solution.py:176
  60.2 1.2 %collective-permute-done.7.got = bf16[64,27,128]{2,1,0:T(8,128)(2,1)S(1)} collective-permute-done((bf16[64,27,128]{2,1,0:T(8,128)(2,1)S(1)}, bf16[64,27,128]{2,1,0:T(8,128)(2,1)S(1)}, u32[]{:S(2)}, u32[]{:S(2)}) %collective-permute-start.7) | collective-permute-done | bytes 442400 | tf_op jit(solution)/shard_map/ppermute | solution.py:262
  61.4 0.9 chip_sum.1.after
  62.3 10.6 %all-to-all-start.1 = ((bf16[64,27,128]{2,1,0:T(8,128)(2,1)}), bf16[64,27,128]{2,1,0:T(8,128)(2,1)S(1)}, u32[]{:S(2)}, u32[]{:S(2)}) async-start(bf16[64,27,128]{2,1,0:T(8,128)(2,1)} %chip_sum.1.after), calls=%async_computation.1 | async-start | bytes 1048576 | tf_op jit(solution)/shard_map/all_to_all | solution.py:440
  73.9 3.7 %collective-permute-start.9 = (bf16[2,18,10,128]{3,2,1,0:T(8,128)(2,1)S(1)}, bf16[2,18,10,128]{3,2,1,0:T(8,128)(2,1)S(1)}, u32[]{:S(2)}, u32[]{:S(2)}) collective-permute-start(bf16[2,18,10,128]{3,2,1,0:T(8,128)(2,1)S(1)} %get-tuple-element.54), channel_id=1, source_target_pairs={{0,1},{1,0},{2,3},{3,2},{4,5},{5,4},{6,7},{7,6},{8,9},{9,8},{10,11... | collective-permute-start | bytes 276488 | tf_op jit(solution)/shard_map/ppermute | solution.py:251
  77.6 1.7 %copy.26 = bf16[3,3,3,128,128]{3,4,2,1,0:T(8,128)(2,1)} copy(bf16[3,3,3,128,128]{4,3,2,1,0:T(8,128)(2,1)S(1)} %bitcast.44) | data formatting | bytes 1769472 | tf_op jit(solution)/shard_map/reshape | solution.py:441
  79.3 1.2 %rev.4 = bf16[3,3,3,128,128]{3,4,2,1,0:T(8,128)(2,1)S(1)} reverse(bf16[3,3,3,128,128]{3,4,2,1,0:T(8,128)(2,1)} %copy.26), dimensions={0,1,2} | reverse | bytes 1769472 | tf_op jit(solution)/shard_map/jit(_flip)/rev | solution.py:442
  80.5 2.8 %collective-permute-done.9 = bf16[2,18,10,128]{3,2,1,0:T(8,128)(2,1)S(1)} collective-permute-done((bf16[2,18,10,128]{3,2,1,0:T(8,128)(2,1)S(1)}, bf16[2,18,10,128]{3,2,1,0:T(8,128)(2,1)S(1)}, u32[]{:S(2)}, u32[]{:S(2)}) %collective-permute-start.9) | collective-permute-done | bytes 92192 | tf_op jit(solution)/shard_map/ppermute | solution.py:251
  83.4 5.2 %backward.1 = (bf16[2,8,2,64,128]{4,3,2,1,0:T(8,128)(2,1)}, f32[8,128]{1,0:T(8,128)S(1)}) custom-call(bf16[2,18,64,128]{3,2,1,0:T(8,128)(2,1)S(1)} %bitcast.50, bf16[2,18,8,128]{3,2,1,0:T(8,128)(2,1)S(1)} %get-tuple-element.77.ylo, bf16[2,18,8,128]{3,2,1,0:T(8,128)(2,1)S(1)} %get-tuple-element.76.yhi, bf16[2,18,10,128]{3,2,1,0:T(8,128)(2,1)S(1)} %get-tuple-element.53.zlo, ...), custom_call_target="tpu_custom_call" | custom-call | flops 4000000000 | bytes 3000000 | tf_op jit(solution)/shard_map/backward/pallas_call | solution.py:223
  88.6 1.3 %all-to-all-done.1.arrived = bf16[64,27,128]{2,1,0:T(8,128)(2,1)S(1)} async-done(((bf16[64,27,128]{2,1,0:T(8,128)(2,1)}), bf16[64,27,128]{2,1,0:T(8,128)(2,1)S(1)}, u32[]{:S(2)}, u32[]{:S(2)}) %all-to-all-start.1) | async-done | bytes 442400 | tf_op jit(solution)/shard_map/all_to_all | solution.py:440
  90.1 4.0 %collective-permute-start.10 = (f32[27,128]{1,0:T(8,128)S(1)}, f32[27,128]{1,0:T(8,128)S(1)}, u32[]{:S(2)}, u32[]{:S(2)}) collective-permute-start(f32[27,128]{1,0:T(8,128)S(1)} %sum_of_arrived.1), channel_id=1, source_target_pairs={{0,128},{64,192},{128,0},{192,64},{1,129},{65,193},{129,1},{193,65... | collective-permute-start | bytes 41480 | tf_op jit(solution)/shard_map/ppermute | solution.py:266
  94.1 1.1 %collective-permute-done.10 = f32[27,128]{1,0:T(8,128)S(1)} collective-permute-done((f32[27,128]{1,0:T(8,128)S(1)}, f32[27,128]{1,0:T(8,128)S(1)}, u32[]{:S(2)}, u32[]{:S(2)}) %collective-permute-start.10) | collective-permute-done | bytes 13856 | tf_op jit(solution)/shard_map/ppermute | solution.py:266
  95.2 2.7 %collective-permute-start.11 = (f32[27,128]{1,0:T(8,128)S(1)}, f32[27,128]{1,0:T(8,128)S(1)}, u32[]{:S(2)}, u32[]{:S(2)}) collective-permute-start(f32[27,128]{1,0:T(8,128)S(1)} %add.41), channel_id=1, source_target_pairs={{0,64},{64,0},{128,192},{192,128},{1,65},{65,1},{129,193},{193,129... | collective-permute-start | bytes 41480 | tf_op jit(solution)/shard_map/ppermute | solution.py:262
  (58 shorter events, 6.2 us)
Async XLA Ops:
  0.6 48.5 %copy-start.1 = (bf16[2,1,16,8,8,128]{5,4,3,2,1,0:T(8,128)(2,1)S(1)}, bf16[2,1,16,8,8,128]{5,4,3,2,1,0:T(8,128)(2,1)}, u32[]{:S(2)}) copy-start(bf16[2,1,16,8,8,128]{5,4,3,2,1,0:T(8,128)(2,1)} %param.5) | copy-start | bytes 1572868
  0.6 47.0 %copy-start.2 = (bf16[2,1,16,8,8,128]{5,4,3,2,1,0:T(8,128)(2,1)S(1)}, bf16[2,1,16,8,8,128]{5,4,3,2,1,0:T(8,128)(2,1)}, u32[]{:S(2)}) copy-start(bf16[2,1,16,8,8,128]{5,4,3,2,1,0:T(8,128)(2,1)} %param.9) | copy-start | bytes 1572868
  3.1 24.8 %collective-permute-start = (bf16[2,3,64,128]{3,2,1,0:T(8,128)(2,1)}, bf16[2,3,64,128]{3,2,1,0:T(8,128)(2,1)S(1)}, u32[]{:S(2)}, u32[]{:S(2)}) collective-permute-start(bf16[2,3,64,128]{3,2,1,0:T(8,128)(2,1)} %get-tuple-element.19), channel_id=1, source_target_pairs={{8,16},{9,17},{10,18},{11,19},{12,20},{13,21},{14,22},{15,23},{16,... | collective-permute-start | bytes 294920 | tf_op jit(solution)/shard_map/ppermute | solution.py:252
  3.8 24.1 %collective-permute-start.1 = (bf16[2,3,64,128]{3,2,1,0:T(8,128)(2,1)}, bf16[2,3,64,128]{3,2,1,0:T(8,128)(2,1)S(1)}, u32[]{:S(2)}, u32[]{:S(2)}) collective-permute-start(bf16[2,3,64,128]{3,2,1,0:T(8,128)(2,1)} %get-tuple-element.20), channel_id=1, source_target_pairs={{0,8},{1,9},{2,10},{3,11},{4,12},{5,13},{6,14},{7,15},{8,0},{9,1},... | collective-permute-start | bytes 294920 | tf_op jit(solution)/shard_map/ppermute | solution.py:251
  12.9 34.1 %all-to-all-start = ((bf16[64,27,128]{2,1,0:T(8,128)(2,1)}), bf16[64,27,128]{2,1,0:T(8,128)(2,1)S(1)}, u32[]{:S(2)}, u32[]{:S(2)}) async-start(bf16[64,27,128]{2,1,0:T(8,128)(2,1)} %get-tuple-element.23), calls=%async_computation | async-start | bytes 1048576 | tf_op jit(solution)/shard_map/all_to_all | solution.py:410
  26.5 1.0 %copy-start = (bf16[2,1,16,8,8,128]{5,4,3,2,1,0:T(8,128)(2,1)S(1)}, bf16[2,1,16,8,8,128]{5,4,3,2,1,0:T(8,128)(2,1)}, u32[]{:S(2)}) copy-start(bf16[2,1,16,8,8,128]{5,4,3,2,1,0:T(8,128)(2,1)} %param.5) | copy-start | bytes 1572868
  28.1 4.2 %collective-permute-start.2 = (bf16[2,20,8,128]{3,2,1,0:T(8,128)(2,1)S(1)}, bf16[2,20,8,128]{3,2,1,0:T(8,128)(2,1)S(1)}, u32[]{:S(2)}, u32[]{:S(2)}) collective-permute-start(bf16[2,20,8,128]{3,2,1,0:T(8,128)(2,1)S(1)} %get-tuple-element.63), channel_id=1, source_target_pairs={{1,2},{2,1},{5,6},{6,5},{9,10},{10,9},{13,14},{14,13},{17,18},{18,... | collective-permute-start | bytes 245768 | tf_op jit(solution)/shard_map/ppermute | solution.py:252
  28.8 6.7 %collective-permute-start.3 = (bf16[2,20,8,128]{3,2,1,0:T(8,128)(2,1)S(1)}, bf16[2,20,8,128]{3,2,1,0:T(8,128)(2,1)S(1)}, u32[]{:S(2)}, u32[]{:S(2)}) collective-permute-start(bf16[2,20,8,128]{3,2,1,0:T(8,128)(2,1)S(1)} %get-tuple-element.62), channel_id=1, source_target_pairs={{0,1},{1,0},{2,3},{3,2},{4,5},{5,4},{6,7},{7,6},{8,9},{9,8},{10,11... | collective-permute-start | bytes 245768 | tf_op jit(solution)/shard_map/ppermute | solution.py:251
  35.7 11.2 %collective-permute-start.4 = (bf16[2,20,10,128]{3,2,1,0:T(8,128)(2,1)S(1)}, bf16[2,20,10,128]{3,2,1,0:T(8,128)(2,1)S(1)}, u32[]{:S(2)}, u32[]{:S(2)}) collective-permute-start(bf16[2,20,10,128]{3,2,1,0:T(8,128)(2,1)S(1)} %maximum_select_fusion), channel_id=1, source_target_pairs={{0,4},{1,5},{2,6},{3,7},{4,0},{5,1},{6,2},{7,3},{8,12},{9,13},{10,... | collective-permute-start | bytes 307208 | tf_op jit(solution)/shard_map/ppermute | solution.py:283
  47.0 2.2 %collective-permute-start.5 = (bf16[64,27,128]{2,1,0:T(8,128)(2,1)S(1)}, bf16[64,27,128]{2,1,0:T(8,128)(2,1)S(1)}, u32[]{:S(2)}, u32[]{:S(2)}) collective-permute-start(bf16[64,27,128]{2,1,0:T(8,128)(2,1)S(1)} %gate.2.mine), channel_id=1, source_target_pairs={{0,64},{64,0},{128,192},{192,128},{1,65},{65,1},{129,193},{193,129... | collective-permute-start | bytes 1327112 | tf_op jit(solution)/shard_map/ppermute | solution.py:262
  59.4 2.0 %collective-permute-start.7 = (bf16[64,27,128]{2,1,0:T(8,128)(2,1)S(1)}, bf16[64,27,128]{2,1,0:T(8,128)(2,1)S(1)}, u32[]{:S(2)}, u32[]{:S(2)}) collective-permute-start(bf16[64,27,128]{2,1,0:T(8,128)(2,1)S(1)} %get-tuple-element.28), channel_id=1, source_target_pairs={{0,64},{64,0},{128,192},{192,128},{1,65},{65,1},{129,193},{193,129... | collective-permute-start | bytes 1327112 | tf_op jit(solution)/shard_map/ppermute | solution.py:262
  59.9 13.1 %collective-permute-start.6 = (bf16[2,18,8,128]{3,2,1,0:T(8,128)(2,1)S(1)}, bf16[2,18,8,128]{3,2,1,0:T(8,128)(2,1)S(1)}, u32[]{:S(2)}, u32[]{:S(2)}) collective-permute-start(bf16[2,18,8,128]{3,2,1,0:T(8,128)(2,1)S(1)} %slice_select_fusion), channel_id=1, source_target_pairs={{0,4},{1,5},{2,6},{3,7},{4,0},{5,1},{6,2},{7,3},{8,12},{9,13},{10,... | collective-permute-start | bytes 221192 | tf_op jit(solution)/shard_map/ppermute | solution.py:283
  62.3 27.6 %all-to-all-start.1 = ((bf16[64,27,128]{2,1,0:T(8,128)(2,1)}), bf16[64,27,128]{2,1,0:T(8,128)(2,1)S(1)}, u32[]{:S(2)}, u32[]{:S(2)}) async-start(bf16[64,27,128]{2,1,0:T(8,128)(2,1)} %chip_sum.1.after), calls=%async_computation.1 | async-start | bytes 1048576 | tf_op jit(solution)/shard_map/all_to_all | solution.py:440
  73.3 7.3 %collective-permute-start.8 = (bf16[2,18,10,128]{3,2,1,0:T(8,128)(2,1)S(1)}, bf16[2,18,10,128]{3,2,1,0:T(8,128)(2,1)S(1)}, u32[]{:S(2)}, u32[]{:S(2)}) collective-permute-start(bf16[2,18,10,128]{3,2,1,0:T(8,128)(2,1)S(1)} %get-tuple-element.55), channel_id=1, source_target_pairs={{1,2},{2,1},{5,6},{6,5},{9,10},{10,9},{13,14},{14,13},{17,18},{18,... | collective-permute-start | bytes 276488 | tf_op jit(solution)/shard_map/ppermute | solution.py:252
  73.9 9.4 %collective-permute-start.9 = (bf16[2,18,10,128]{3,2,1,0:T(8,128)(2,1)S(1)}, bf16[2,18,10,128]{3,2,1,0:T(8,128)(2,1)S(1)}, u32[]{:S(2)}, u32[]{:S(2)}) collective-permute-start(bf16[2,18,10,128]{3,2,1,0:T(8,128)(2,1)S(1)} %get-tuple-element.54), channel_id=1, source_target_pairs={{0,1},{1,0},{2,3},{3,2},{4,5},{5,4},{6,7},{7,6},{8,9},{9,8},{10,11... | collective-permute-start | bytes 276488 | tf_op jit(solution)/shard_map/ppermute | solution.py:251
  83.4 15.3 %copy-start.3 = (f32[54,128]{1,0:T(8,128)S(1)}, f32[54,128]{1,0:T(8,128)}, u32[]{:S(2)}) copy-start(f32[54,128]{1,0:T(8,128)} %weight.1) | copy-start | bytes 82948
  83.4 15.3 %copy-start.4 = (f32[54,128]{1,0:T(8,128)S(1)}, f32[54,128]{1,0:T(8,128)}, u32[]{:S(2)}) copy-start(f32[54,128]{1,0:T(8,128)} %param.7) | copy-start | bytes 82948
  83.4 15.3 %copy-start.5 = (f32[54,128]{1,0:T(8,128)S(1)}, f32[54,128]{1,0:T(8,128)}, u32[]{:S(2)}) copy-start(f32[54,128]{1,0:T(8,128)} %param.8) | copy-start | bytes 82948
  90.1 5.1 %collective-permute-start.10 = (f32[27,128]{1,0:T(8,128)S(1)}, f32[27,128]{1,0:T(8,128)S(1)}, u32[]{:S(2)}, u32[]{:S(2)}) collective-permute-start(f32[27,128]{1,0:T(8,128)S(1)} %sum_of_arrived.1), channel_id=1, source_target_pairs={{0,128},{64,192},{128,0},{192,64},{1,129},{65,193},{129,1},{193,65... | collective-permute-start | bytes 41480 | tf_op jit(solution)/shard_map/ppermute | solution.py:266
  95.2 3.5 %collective-permute-start.11 = (f32[27,128]{1,0:T(8,128)S(1)}, f32[27,128]{1,0:T(8,128)S(1)}, u32[]{:S(2)}, u32[]{:S(2)}) collective-permute-start(f32[27,128]{1,0:T(8,128)S(1)} %add.41), channel_id=1, source_target_pairs={{0,64},{64,0},{128,192},{192,128},{1,65},{65,1},{129,193},{193,129... | collective-permute-start | bytes 41480 | tf_op jit(solution)/shard_map/ppermute | solution.py:262

commit v5 on v4

--- a/solution.py
+++ b/solution.py
@@ -10,6 +10,7 @@
 GY = 2
 GZ = 4
 FWD_VMEM = 20
+QUARTERS = (0, 27, 13, 40)
 
 root_coef = 0.7978845608
 cubic_coef = 0.044715
@@ -85,28 +86,30 @@
     return total
 
 
-def forward_kernel(core_ref, center, zlo, zhi, ylo, yhi, dy, below, above, mine, other,
+def forward_kernel(member_ref, center, zlo, zhi, ylo, yhi, dy, below, above, own, chip, core, slant,
                    out, dz, windows, kern, rows, wide):
-    core = core_ref[0]
+    member = member_ref[0]
+    side, half = lax.div(member, 2), lax.rem(member, 2)
+    near, far = 27 * half, 27 - 27 * half
+    starts = (near + 13 * side, near + 13 - 13 * side, far + 13 * side, far + 13 - 13 * side)
 
     def piece(s, _):
-        a, b = mine[s].astype(f32), other[s].astype(f32)
-        rows[pl.ds(54 * s, 27), :] = jnp.where(core == 0, a, b)
-        rows[pl.ds(54 * s + 27, 27), :] = jnp.where(core == 0, b, a)
+        for quarter, first in zip((own, chip, core, slant), starts):
+            rows[pl.ds(54 * s + first, 14), :] = quarter[s].astype(f32)
         return 0
 
     lax.fori_loop(0, 64, piece, 0)
     for kx in range(3):
         kern[kx] = rows[1152 * kx : 1152 * (kx + 1), :].astype(bf16)
     pair_kernels(kern, wide)
-    side = (zlo, zhi, ylo, yhi)
+    halo = (zlo, zhi, ylo, yhi)
 
     def crop(b, _):
-        own = windows.at[b]
-        fill_windows(own, 0, 2, z_first_source(b, below, *side))
-        fill_windows(own, 2, 16, z_first_source(b, center, *side, 2))
-        fill_windows(own, 18, 2, z_first_source(b, above, *side, 18))
-        both = pair_products(own, wide, 9)
+        here = windows.at[b]
+        fill_windows(here, 0, 2, z_first_source(b, below, *halo))
+        fill_windows(here, 2, 16, z_first_source(b, center, *halo, 2))
+        fill_windows(here, 18, 2, z_first_source(b, above, *halo, 18))
+        both = pair_products(here, wide, 9)
         for at in range(2):
             value, slope = activate(both[:, 128 * at : 128 * (at + 1)])
             grad = dy[b, :, at].reshape(576, 128).astype(f32) * slope
@@ -123,8 +126,8 @@
 ANY = pl.BlockSpec(memory_space=pl.ANY)
 
 
-def forward(core, center, zlo, zhi, ylo, yhi, dy, below, above, mine, other):
-    ins = (center, zlo, zhi, ylo, yhi, dy.reshape(2, 9, 2, 64, 128), below, above, mine, other)
+def forward(member, center, zlo, zhi, ylo, yhi, dy, below, above, quarters):
+    ins = (center, zlo, zhi, ylo, yhi, dy.reshape(2, 9, 2, 64, 128), below, above, *quarters)
     outs = [
         jax.ShapeDtypeStruct((2, 8, 2, 64, 128), bf16),
         jax.ShapeDtypeStruct((2, 9, 2, 64, 128), bf16),
@@ -140,7 +143,7 @@
         compiler_params=pltpu.CompilerParams(vmem_limit_bytes=FWD_VMEM * 2**20),
         cost_estimate=pl.CostEstimate(flops=4 * 10**9, bytes_accessed=8 * 10**6, transcendentals=300000),
         name="forward",
-    )(core, *ins)
+    )(member, *ins)
     return out, dz.reshape(2, 18, 64, 128), windows.reshape(2, 20, 64, 1152), kern
 
 
@@ -205,15 +208,32 @@
     )(stays, got)
 
 
+def flipped_pair_kernels(kern, wide):
+    none = jnp.zeros((128, 1152), bf16)
+    for at in range(4):
+        for side, kx in ((0, 2 - at), (1, 3 - at)):
+            if not 0 <= kx <= 2:
+                wide[at, 128 * side : 128 * (side + 1), :] = none
+                continue
+            for tap in range(9):
+                col = 128 * (8 - tap)
+                block = kern[kx, 128 * tap : 128 * (tap + 1), :]
+                wide[at, 128 * side : 128 * (side + 1), col : col + 128] = block
+
+
 def backward_kernel(center, ylo, yhi, zlo, zhi, kern, out, token, windows, wide):
     token[...] = jnp.zeros_like(token)
-    pair_kernels(kern, wide)
+    flipped_pair_kernels(kern, wide)
 
     def crop(b, _):
         fill_windows(windows, 0, 18, y_first_source(b, center, ylo, yhi, zlo, zhi))
-        both = pair_products(windows, wide, 8).astype(bf16)
-        for at in range(2):
-            out[b, :, at] = both[:, 128 * at : 128 * (at + 1)].reshape(8, 64, 128)
+        both = jnp.zeros((512, 256), f32)
+        for at in range(4):
+            lhs = windows[at // 2 : at // 2 + 8, at % 2].reshape(512, 1152)
+            both += lax.dot_general(lhs, wide[at], (((1,), (1,)), ((), ())), preferred_element_type=f32)
+        for side in range(2):
+            grad = both[:, 128 * side : 128 * (side + 1)].astype(bf16)
+            out[b, :, side] = grad.reshape(8, 64, 128)
         return 0
 
     lax.fori_loop(0, 2, crop, 0)
@@ -225,7 +245,7 @@
         in_specs=[VMEM] * 6,
         out_specs=[VMEM] * 2,
         out_shape=[jax.ShapeDtypeStruct((2, 8, 2, 64, 128), bf16), jax.ShapeDtypeStruct((8, 128), f32)],
-        scratch_shapes=[pltpu.VMEM((9, 2, 64, 1152), bf16), pltpu.VMEM((4, 1152, 256), bf16)],
+        scratch_shapes=[pltpu.VMEM((9, 2, 64, 1152), bf16), pltpu.VMEM((4, 256, 1152), bf16)],
         compiler_params=pltpu.CompilerParams(vmem_limit_bytes=FWD_VMEM * 2**20),
         cost_estimate=pl.CostEstimate(flops=4 * 10**9, bytes_accessed=3 * 10**6, transcendentals=0),
         name="backward",
@@ -266,6 +286,10 @@
     return lax.ppermute(value, "sample", flip_pairs(lax.axis_size("sample"), 2))
 
 
+def diagonal_swap(value):
+    return lax.ppermute(value, "sample", flip_pairs(lax.axis_size("sample"), 3))
+
+
 def halves_joined(mine, other, core, dim):
     low = jnp.where(core == 0, mine, other)
     high = jnp.where(core == 0, other, mine)
@@ -294,7 +318,7 @@
     return swap_layers(first, last, coords()[2], 1, GZ)
 
 
-def start_kernel(even_ref, core_ref, field, dy, weight, inner, outer, copies, ends, rows, wide, sems):
+def start_kernel(even_ref, member_ref, field, dy, weight, inner, outer, copies, ends, rows, wide, sems):
     def spread(at):
         return pltpu.make_async_copy(wide, copies.at[pl.ds(8 * at, 8)], sems.at[6 + at])
 
@@ -305,11 +329,13 @@
         fetches.append(pltpu.make_async_copy(dy.at[:, x : x + 1], ends.at[at, :, 2:3], sems.at[2 + 2 * at]))
     for fetch in fetches:
         fetch.start()
-    even, core = even_ref[0] == 1, core_ref[0]
+    even, member = even_ref[0] == 1, member_ref[0]
     fetches[0].wait()
-    half = jnp.where(core == 0, rows[0:27], rows[27:54]).astype(bf16)
+    share = rows[0:14]
+    for at in range(1, 4):
+        share = jnp.where(member == at, rows[QUARTERS[at] : QUARTERS[at] + 14], share)
     for at in range(8):
-        wide[at] = half
+        wide[at] = share.astype(bf16)
     for at in range(8):
         spread(at).start()
     for fetch in fetches[1:]:
@@ -320,21 +346,21 @@
         spread(at).wait()
 
 
-def start(even, core, field, dy, weight):
+def start(even, member, field, dy, weight):
     end = jax.ShapeDtypeStruct((2, 3, 64, 128), bf16)
     return pl.pallas_call(
         start_kernel,
         in_specs=[SMEM, SMEM, ANY, ANY, ANY],
         out_specs=[VMEM, VMEM, ANY],
-        out_shape=[end, end, jax.ShapeDtypeStruct((64, 27, 128), bf16)],
+        out_shape=[end, end, jax.ShapeDtypeStruct((64, 14, 128), bf16)],
         scratch_shapes=[
             pltpu.VMEM((2, 2, 3, 64, 128), bf16),
             pltpu.VMEM((54, 128), f32),
-            pltpu.VMEM((8, 27, 128), bf16),
+            pltpu.VMEM((8, 14, 128), bf16),
             pltpu.SemaphoreType.DMA((14,)),
         ],
         name="start",
-    )(even, core, field, dy, weight)
+    )(even, member, field, dy, weight)
 
 
 def z_edges_kernel(field, first, last, tall):
@@ -406,7 +432,8 @@
     even = coords()[0] % 2 == 0
     groups = lax.axis_size("space") // (GY * GZ)
     which = jnp.full((1,), core, jnp.int32)
-    inner, outer, copies = start(jnp.full((1,), even, jnp.int32), which, field, grad_out, weight)
+    member = jnp.full((1,), lax.axis_index("sample"), jnp.int32)
+    inner, outer, copies = start(jnp.full((1,), even, jnp.int32), member, field, grad_out, weight)
     mine = lax.all_to_all(copies, "space", split_axis=0, concat_axis=0, tiled=True)
     below, above = swapped(inner, outer, even, GY * GZ, groups)
 
@@ -422,11 +449,12 @@
         )
     )
     total = crops * lax.axis_size("sample") * lax.axis_size("space") * nx * ny * nz
-    mine = gate(mine, yhi)
+    beside = chip_swap(mine)
+    quarters = (mine, beside, core_swap(mine), core_swap(beside))
     dy = jnp.concatenate([below[:, 2:], grad_out, above[:, 2:]], 1)
     other = core_swap(mine)
     output, dz, windows, kernel = forward(
-        which, field, zlo, zhi, ylo, yhi, dy, below, above, mine, other
+        member, field, zlo, zhi, ylo, yhi, dy, below, above, quarters
     )
     stays, leaves = weight_grad_halves(which, windows, dz, float(total) ** (-0.5))
     chip = chip_sum(stays, core_swap(leaves))
@@ -438,12 +466,12 @@
         )
     )
     arrived = lax.all_to_all(chip, "space", split_axis=0, concat_axis=0, tiled=True)
-    taps = kernel.reshape(3, 3, 3, channels, channels)
-    flipped = jnp.flip(taps, (0, 1, 2)).transpose(0, 1, 2, 4, 3).reshape(kernel.shape)
-    input_grad, token = backward(dz, ylo, yhi, zlo, zhi, flipped)
+    input_grad, token = backward(dz, ylo, yhi, zlo, zhi, kernel)
     owned = sum_of_arrived(arrived, token)
-    owned = owned + chip_swap(owned)
-    weight_grad = halves_joined(owned, core_swap(owned), core, 0)
+    owned, across, aslant = (
+        [owned + chip_swap(owned), core_swap(owned), diagonal_swap(owned)]
+    )
+    weight_grad = halves_joined(owned, across + aslant, core, 0)
     new_moment = 0.9 * moment + 0.1 * weight_grad
     new_second = 0.999 * second + 0.001 * weight_grad * weight_grad
     first_fix = 1.0 - 0.9**10

time: 99.8 us -> 98.4 us (0.986)
  local copies, waits for them, and re-layouts: 5.28 us -> 2.38 us
  other arithmetic: 1.25 us -> 2.29 us
    ppermute x2, waiting for transfers between devices: 9.84 us -> 0.01 us  [y_halo(): got = lax.ppermute(face, 'space', flip_pairs(lax.axis_size('space'), GZ))]
    ppermute x3 -> x4, starting transfers between devices: 3.81 us -> 9.58 us  [core_swap(): return lax.ppermute(value, 'sample', flip_pairs(lax.axis_size('sample'), 1))]
    all_to_all x1, waiting for transfers between devices: 0.01 us -> 4.24 us  [local(): lax.all_to_all(copies, 'space', split_axis=0, concat_axis=0, tiled=True)]
    all_to_all x1, waiting for transfers between devices: 1.33 us -> 5.47 us  [local(): lax.all_to_all(chip, 'space', split_axis=0, concat_axis=0, tiled=True)]
    all_to_all x1, starting transfers between devices: 10.6 us -> 7.11 us  [local(): lax.all_to_all(chip, 'space', split_axis=0, concat_axis=0, tiled=True)]
    ppermute x1 -> x2, starting transfers between devices: 3.96 us -> 0.87 us  [chip_swap(): return lax.ppermute(value, 'sample', flip_pairs(lax.axis_size('sample'), 2))]
    ppermute x0 -> x1, waiting for transfers between devices: none -> 1.7 us  [diagonal_swap(): return lax.ppermute(value, 'sample', flip_pairs(lax.axis_size('sample'), 3))]
    reshape x1 -> x0, local copies, waits for them, and re-layouts: 1.67 us -> none  [local(): taps = kernel.reshape(3, 3, 3, channels, channels)]
  transfers between devices with their start and end apart: 14 -> 17, of which waited for: 8 -> 8; matrix products, arithmetic and copies ran while one was open for 5% -> 3% of each run, Pallas kernels for 6% -> 7%
where the time goes in v5:
time: 98.4 us; the launch traced here: 98 us
  starting transfers between devices  51.5 us (52%)
  waiting for transfers between devices  21.5 us (22%)
  Pallas kernels  19.2 us (20%)
  local copies, waits for them, and re-layouts  2.38 us (2%)
  other arithmetic  2.29 us (2%)
  between operations  1.09 us (1%)
    ppermute x3, starting transfers between devices, swapped(): inner = lax.ppermute(inner, 'space', flip_pairs(devices, stride))  16.1 us
    all_to_all x1, starting transfers between devices, local(): lax.all_to_all(copies, 'space', split_axis=0, concat_axis=0, tiled=True)  12.7 us
    ppermute x4, starting transfers between devices, core_swap(): return lax.ppermute(value, 'sample', flip_pairs(lax.axis_size('sample'), 1))  9.58 us
    all_to_all x1, starting transfers between devices, local(): lax.all_to_all(chip, 'space', split_axis=0, concat_axis=0, tiled=True)  7.11 us
    pallas_call x1, Pallas kernels, forward(): pl.pallas_call(forward_kernel, in_specs=[SMEM] + [VMEM] * len(ins), out_s...  6.92 us
    ppermute x3, waiting for transfers between devices, swapped(): inner = lax.ppermute(inner, 'space', flip_pairs(devices, stride))  5.84 us
    all_to_all x1, waiting for transfers between devices, local(): lax.all_to_all(chip, 'space', split_axis=0, concat_axis=0, tiled=True)  5.47 us
    pallas_call x1, Pallas kernels, backward(): pl.pallas_call(backward_kernel, in_specs=[VMEM] * 6, out_specs=[VMEM] * 2...  5.21 us
  transfers between devices with their start and end apart: 17, of which 8 were waited for; matrix products, arithmetic and copies ran while one was open for 3% of the time, Pallas kernels for 7%

profile of v5, /device:TPU:1, one launch (start us, length us, event | category | flops | bytes accessed | tf_op | source)
XLA Modules:
  0.0 98.0 jit_solution(12371160075689509626)
XLA Ops:
  0.7 2.3 %start.1 = (bf16[2,3,64,128]{3,2,1,0:T(8,128)(2,1)}, bf16[2,3,64,128]{3,2,1,0:T(8,128)(2,1)}, bf16[64,14,128]{2,1,0:T(8,128)(2,1)}) custom-call(s32[1]{0:T(128)} %bitcast.2.even_ref, s32[1]{0:T(128)} %bitcast.member_ref, bf16[2,16,64,128]{3,2,1,0:T(8,128)(2,1)} %bitcast.37, bf16[2,16,64,128]{3,2,1,0:T(8,128)(2,1)} %bitcast.47, f32[54,128]{1,0:T(8,128)} %weight.1), custom_call_target="tpu_custom_call" | custom-call | tf_op jit(solution)/shard_map/start/pallas_call | solution.py:351
  3.6 9.1 %collective-permute-start.1 = (bf16[2,3,64,128]{3,2,1,0:T(8,128)(2,1)}, bf16[2,3,64,128]{3,2,1,0:T(8,128)(2,1)S(1)}, u32[]{:S(2)}, u32[]{:S(2)}) collective-permute-start(bf16[2,3,64,128]{3,2,1,0:T(8,128)(2,1)} %get-tuple-element.20), channel_id=1, source_target_pairs={{0,8},{1,9},{2,10},{3,11},{4,12},{5,13},{6,14},{7,15},{8,0},{9,1},... | collective-permute-start | bytes 294920 | tf_op jit(solution)/shard_map/ppermute | solution.py:271
  12.7 12.7 %all-to-all-start = ((bf16[64,14,128]{2,1,0:T(8,128)(2,1)}), bf16[64,14,128]{2,1,0:T(8,128)(2,1)S(1)}, u32[]{:S(2)}, u32[]{:S(2)}) async-start(bf16[64,14,128]{2,1,0:T(8,128)(2,1)} %get-tuple-element.23), calls=%async_computation | async-start | bytes 524288 | tf_op jit(solution)/shard_map/all_to_all | solution.py:437
  26.4 1.0 %copy-done = bf16[2,1,16,8,8,128]{5,4,3,2,1,0:T(8,128)(2,1)S(1)} copy-done((bf16[2,1,16,8,8,128]{5,4,3,2,1,0:T(8,128)(2,1)S(1)}, bf16[2,1,16,8,8,128]{5,4,3,2,1,0:T(8,128)(2,1)}, u32[]{:S(2)}) %copy-start) | copy-done | bytes 524312
  28.6 3.5 %collective-permute-start.3 = (bf16[2,20,8,128]{3,2,1,0:T(8,128)(2,1)S(1)}, bf16[2,20,8,128]{3,2,1,0:T(8,128)(2,1)S(1)}, u32[]{:S(2)}, u32[]{:S(2)}) collective-permute-start(bf16[2,20,8,128]{3,2,1,0:T(8,128)(2,1)S(1)} %get-tuple-element.62), channel_id=1, source_target_pairs={{0,1},{1,0},{2,3},{3,2},{4,5},{5,4},{6,7},{7,6},{8,9},{9,8},{10,11... | collective-permute-start | bytes 245768 | tf_op jit(solution)/shard_map/ppermute | solution.py:271
  32.2 2.3 %collective-permute-done.3 = bf16[2,20,8,128]{3,2,1,0:T(8,128)(2,1)S(1)} collective-permute-done((bf16[2,20,8,128]{3,2,1,0:T(8,128)(2,1)S(1)}, bf16[2,20,8,128]{3,2,1,0:T(8,128)(2,1)S(1)}, u32[]{:S(2)}, u32[]{:S(2)}) %collective-permute-start.3) | collective-permute-done | bytes 81952 | tf_op jit(solution)/shard_map/ppermute | solution.py:271
  34.5 4.2 %all-to-all-done.own = bf16[64,14,128]{2,1,0:T(8,128)(2,1)S(1)} async-done(((bf16[64,14,128]{2,1,0:T(8,128)(2,1)}), bf16[64,14,128]{2,1,0:T(8,128)(2,1)S(1)}, u32[]{:S(2)}, u32[]{:S(2)}) %all-to-all-start) | async-done | bytes 229408 | tf_op jit(solution)/shard_map/all_to_all | solution.py:437
  39.7 1.2 %collective-permute-start.4 = (bf16[2,20,10,128]{3,2,1,0:T(8,128)(2,1)S(1)}, bf16[2,20,10,128]{3,2,1,0:T(8,128)(2,1)S(1)}, u32[]{:S(2)}, u32[]{:S(2)}) collective-permute-start(bf16[2,20,10,128]{3,2,1,0:T(8,128)(2,1)S(1)} %maximum_select_fusion), channel_id=1, source_target_pairs={{0,4},{1,5},{2,6},{3,7},{4,0},{5,1},{6,2},{7,3},{8,12},{9,13},{10,... | collective-permute-start | bytes 307208 | tf_op jit(solution)/shard_map/ppermute | solution.py:307
  41.0 1.1 %pad_maximum_fusion = bf16[2,18,64,128]{3,2,1,0:T(8,128)(2,1)S(1)} fusion(bf16[2,1,64,128]{3,2,1,0:T(8,128)(2,1)S(1)} %slice.127, bf16[2,16,64,128]{3,2,1,0:T(8,128)(2,1)} %bitcast.48, bf16[2,1,64,128]{3,2,1,0:T(8,128)(2,1)S(1)} %slice.126), kind=kLoop, calls=%fused_computation | loop fusion | flops 589824 | bytes 1179648 | tf_op jit(solution)/shard_map/concatenate | solution.py:454
  42.1 2.4 %collective-permute-start.6 = (bf16[64,14,128]{2,1,0:T(8,128)(2,1)S(1)}, bf16[64,14,128]{2,1,0:T(8,128)(2,1)S(1)}, u32[]{:S(2)}, u32[]{:S(2)}) collective-permute-start(bf16[64,14,128]{2,1,0:T(8,128)(2,1)S(1)} %all-to-all-done.own), channel_id=1, source_target_pairs={{0,64},{64,0},{128,192},{192,128},{1,65},{65,1},{129,193},{193,129... | collective-permute-start | bytes 688136 | tf_op jit(solution)/shard_map/ppermute | solution.py:282
  44.5 2.2 %collective-permute-done.5.chip = bf16[64,14,128]{2,1,0:T(8,128)(2,1)S(1)} collective-permute-done((bf16[64,14,128]{2,1,0:T(8,128)(2,1)S(1)}, bf16[64,14,128]{2,1,0:T(8,128)(2,1)S(1)}, u32[]{:S(2)}, u32[]{:S(2)}) %collective-permute-start.5) | collective-permute-done | bytes 229408 | tf_op jit(solution)/shard_map/ppermute | solution.py:286
  46.7 4.4 %collective-permute-start.7 = (bf16[64,14,128]{2,1,0:T(8,128)(2,1)S(1)}, bf16[64,14,128]{2,1,0:T(8,128)(2,1)S(1)}, u32[]{:S(2)}, u32[]{:S(2)}) collective-permute-start(bf16[64,14,128]{2,1,0:T(8,128)(2,1)S(1)} %collective-permute-done.5.chip), channel_id=1, source_target_pairs={{0,64},{64,0},{128,192},{192,128},{1,65},{65,1},{129,193},{193,129... | collective-permute-start | bytes 688136 | tf_op jit(solution)/shard_map/ppermute | solution.py:282
  51.1 1.1 %collective-permute-done.7.slant = bf16[64,14,128]{2,1,0:T(8,128)(2,1)S(1)} collective-permute-done((bf16[64,14,128]{2,1,0:T(8,128)(2,1)S(1)}, bf16[64,14,128]{2,1,0:T(8,128)(2,1)S(1)}, u32[]{:S(2)}, u32[]{:S(2)}) %collective-permute-start.7) | collective-permute-done | bytes 229408 | tf_op jit(solution)/shard_map/ppermute | solution.py:282
  52.2 6.9 %forward.1 = (bf16[2,8,2,64,128]{4,3,2,1,0:T(8,128)(2,1)}, bf16[2,9,2,64,128]{4,3,2,1,0:T(8,128)(2,1)S(1)}, bf16[2,10,2,64,1152]{4,3,2,1,0:T(8,128)(2,1)S(1)}, bf16[3,1152,128]{2,1,0:T(8,128)(2,1)S(1)}) custom-call(s32[1]{0:T(128)} %bitcast.member_ref, bf16[2,16,64,128]{3,2,1,0:T(8,128)(2,1)S(1)} %bitcast.40, ...), custom_call_target="tpu_custom_call" | custom-call | flops 4000000000 | bytes 8000000 | tf_op jit(solution)/shard_map/forward/pallas_call | solution.py:137
  59.1 3.4 %weight_grad_halves.1 = (bf16[64,27,128]{2,1,0:T(8,128)(2,1)S(1)}, bf16[64,27,128]{2,1,0:T(8,128)(2,1)S(1)}) custom-call(s32[1]{0:T(128)} %bitcast.14.core_ref, bf16[2,20,64,1152]{3,2,1,0:T(8,128)(2,1)S(1)} %bitcast.46, bf16[2,18,64,128]{3,2,1,0:T(8,128)(2,1)S(1)} %bitcast.42), custom_call_target="tpu_custom_call" | custom-call | flops 4000000000 | bytes 7000000 | tf_op jit(solution)/shard_map/weight_grad_halves/pallas_call | solution.py:179
  63.6 1.0 collective-permute-done.9.got
  65.5 7.1 %all-to-all-start.1 = ((bf16[64,27,128]{2,1,0:T(8,128)(2,1)}), bf16[64,27,128]{2,1,0:T(8,128)(2,1)S(1)}, u32[]{:S(2)}, u32[]{:S(2)}) async-start(bf16[64,27,128]{2,1,0:T(8,128)(2,1)} %chip_sum.1.after), calls=%async_computation.1 | async-start | bytes 1048576 | tf_op jit(solution)/shard_map/all_to_all | solution.py:468
  73.6 3.5 %collective-permute-start.11 = (bf16[2,18,10,128]{3,2,1,0:T(8,128)(2,1)S(1)}, bf16[2,18,10,128]{3,2,1,0:T(8,128)(2,1)S(1)}, u32[]{:S(2)}, u32[]{:S(2)}) collective-permute-start(bf16[2,18,10,128]{3,2,1,0:T(8,128)(2,1)S(1)} %get-tuple-element.54), channel_id=1, source_target_pairs={{0,1},{1,0},{2,3},{3,2},{4,5},{5,4},{6,7},{7,6},{8,9},{9,8},{10,11... | collective-permute-start | bytes 276488 | tf_op jit(solution)/shard_map/ppermute | solution.py:271
  77.1 3.6 %collective-permute-done.11 = bf16[2,18,10,128]{3,2,1,0:T(8,128)(2,1)S(1)} collective-permute-done((bf16[2,18,10,128]{3,2,1,0:T(8,128)(2,1)S(1)}, bf16[2,18,10,128]{3,2,1,0:T(8,128)(2,1)S(1)}, u32[]{:S(2)}, u32[]{:S(2)}) %collective-permute-start.11) | collective-permute-done | bytes 92192 | tf_op jit(solution)/shard_map/ppermute | solution.py:271
  80.8 5.2 %backward.1 = (bf16[2,8,2,64,128]{4,3,2,1,0:T(8,128)(2,1)}, f32[8,128]{1,0:T(8,128)S(1)}) custom-call(bf16[2,18,64,128]{3,2,1,0:T(8,128)(2,1)S(1)} %bitcast.45, bf16[2,18,8,128]{3,2,1,0:T(8,128)(2,1)S(1)} %get-tuple-element.77.ylo, bf16[2,18,8,128]{3,2,1,0:T(8,128)(2,1)S(1)} %get-tuple-element.76.yhi, bf16[2,18,10,128]{3,2,1,0:T(8,128)(2,1)S(1)} %get-tuple-element.53.zlo, ...), custom_call_target="tpu_custom_call" | custom-call | flops 4000000000 | bytes 3000000 | tf_op jit(solution)/shard_map/backward/pallas_call | solution.py:243
  86.0 5.5 %all-to-all-done.1.arrived = bf16[64,27,128]{2,1,0:T(8,128)(2,1)S(1)} async-done(((bf16[64,27,128]{2,1,0:T(8,128)(2,1)}), bf16[64,27,128]{2,1,0:T(8,128)(2,1)S(1)}, u32[]{:S(2)}, u32[]{:S(2)}) %all-to-all-start.1) | async-done | bytes 442400 | tf_op jit(solution)/shard_map/all_to_all | solution.py:468
  91.7 2.4 %collective-permute-start.13 = (f32[27,128]{1,0:T(8,128)S(1)}, f32[27,128]{1,0:T(8,128)S(1)}, u32[]{:S(2)}, u32[]{:S(2)}) collective-permute-start(f32[27,128]{1,0:T(8,128)S(1)} %sum_of_arrived.1), channel_id=1, source_target_pairs={{0,64},{64,0},{128,192},{192,128},{1,65},{65,1},{129,193},{193,129... | collective-permute-start | bytes 41480 | tf_op jit(solution)/shard_map/ppermute | solution.py:282
  94.0 1.5 %collective-permute-start.14 = (f32[27,128]{1,0:T(8,128)S(1)}, f32[27,128]{1,0:T(8,128)S(1)}, u32[]{:S(2)}, u32[]{:S(2)}) collective-permute-start(f32[27,128]{1,0:T(8,128)S(1)} %sum_of_arrived.1), channel_id=1, source_target_pairs={{0,192},{64,128},{128,64},{192,0},{1,193},{65,129},{129,65},{193,1... | collective-permute-start | bytes 41480 | tf_op jit(solution)/shard_map/ppermute | solution.py:290
  95.6 1.7 %collective-permute-done.14 = f32[27,128]{1,0:T(8,128)S(1)} collective-permute-done((f32[27,128]{1,0:T(8,128)S(1)}, f32[27,128]{1,0:T(8,128)S(1)}, u32[]{:S(2)}, u32[]{:S(2)}) %collective-permute-start.14) | collective-permute-done | bytes 13856 | tf_op jit(solution)/shard_map/ppermute | solution.py:290
  (58 shorter events, 7.5 us)
Async XLA Ops:
  0.6 51.6 %copy-start.1 = (bf16[2,1,16,8,8,128]{5,4,3,2,1,0:T(8,128)(2,1)S(1)}, bf16[2,1,16,8,8,128]{5,4,3,2,1,0:T(8,128)(2,1)}, u32[]{:S(2)}) copy-start(bf16[2,1,16,8,8,128]{5,4,3,2,1,0:T(8,128)(2,1)} %param.5) | copy-start | bytes 1572868
  3.0 24.8 %collective-permute-start = (bf16[2,3,64,128]{3,2,1,0:T(8,128)(2,1)}, bf16[2,3,64,128]{3,2,1,0:T(8,128)(2,1)S(1)}, u32[]{:S(2)}, u32[]{:S(2)}) collective-permute-start(bf16[2,3,64,128]{3,2,1,0:T(8,128)(2,1)} %get-tuple-element.19), channel_id=1, source_target_pairs={{8,16},{9,17},{10,18},{11,19},{12,20},{13,21},{14,22},{15,23},{16,... | collective-permute-start | bytes 294920 | tf_op jit(solution)/shard_map/ppermute | solution.py:272
  3.6 24.1 %collective-permute-start.1 = (bf16[2,3,64,128]{3,2,1,0:T(8,128)(2,1)}, bf16[2,3,64,128]{3,2,1,0:T(8,128)(2,1)S(1)}, u32[]{:S(2)}, u32[]{:S(2)}) collective-permute-start(bf16[2,3,64,128]{3,2,1,0:T(8,128)(2,1)} %get-tuple-element.20), channel_id=1, source_target_pairs={{0,8},{1,9},{2,10},{3,11},{4,12},{5,13},{6,14},{7,15},{8,0},{9,1},... | collective-permute-start | bytes 294920 | tf_op jit(solution)/shard_map/ppermute | solution.py:271
  12.7 26.1 %all-to-all-start = ((bf16[64,14,128]{2,1,0:T(8,128)(2,1)}), bf16[64,14,128]{2,1,0:T(8,128)(2,1)S(1)}, u32[]{:S(2)}, u32[]{:S(2)}) async-start(bf16[64,14,128]{2,1,0:T(8,128)(2,1)} %get-tuple-element.23), calls=%async_computation | async-start | bytes 524288 | tf_op jit(solution)/shard_map/all_to_all | solution.py:437
  26.4 1.0 %copy-start = (bf16[2,1,16,8,8,128]{5,4,3,2,1,0:T(8,128)(2,1)S(1)}, bf16[2,1,16,8,8,128]{5,4,3,2,1,0:T(8,128)(2,1)}, u32[]{:S(2)}) copy-start(bf16[2,1,16,8,8,128]{5,4,3,2,1,0:T(8,128)(2,1)} %param.5) | copy-start | bytes 1572868
  27.9 4.2 %collective-permute-start.2 = (bf16[2,20,8,128]{3,2,1,0:T(8,128)(2,1)S(1)}, bf16[2,20,8,128]{3,2,1,0:T(8,128)(2,1)S(1)}, u32[]{:S(2)}, u32[]{:S(2)}) collective-permute-start(bf16[2,20,8,128]{3,2,1,0:T(8,128)(2,1)S(1)} %get-tuple-element.63), channel_id=1, source_target_pairs={{1,2},{2,1},{5,6},{6,5},{9,10},{10,9},{13,14},{14,13},{17,18},{18,... | collective-permute-start | bytes 245768 | tf_op jit(solution)/shard_map/ppermute | solution.py:272
  28.6 5.8 %collective-permute-start.3 = (bf16[2,20,8,128]{3,2,1,0:T(8,128)(2,1)S(1)}, bf16[2,20,8,128]{3,2,1,0:T(8,128)(2,1)S(1)}, u32[]{:S(2)}, u32[]{:S(2)}) collective-permute-start(bf16[2,20,8,128]{3,2,1,0:T(8,128)(2,1)S(1)} %get-tuple-element.62), channel_id=1, source_target_pairs={{0,1},{1,0},{2,3},{3,2},{4,5},{5,4},{6,7},{7,6},{8,9},{9,8},{10,11... | collective-permute-start | bytes 245768 | tf_op jit(solution)/shard_map/ppermute | solution.py:271
  38.8 7.9 %collective-permute-start.5 = (bf16[64,14,128]{2,1,0:T(8,128)(2,1)S(1)}, bf16[64,14,128]{2,1,0:T(8,128)(2,1)S(1)}, u32[]{:S(2)}, u32[]{:S(2)}) collective-permute-start(bf16[64,14,128]{2,1,0:T(8,128)(2,1)S(1)} %all-to-all-done.own), channel_id=1, source_target_pairs={{0,128},{64,192},{128,0},{192,64},{1,129},{65,193},{129,1},{193,65... | collective-permute-start | bytes 688136 | tf_op jit(solution)/shard_map/ppermute | solution.py:286
  39.7 11.3 %collective-permute-start.4 = (bf16[2,20,10,128]{3,2,1,0:T(8,128)(2,1)S(1)}, bf16[2,20,10,128]{3,2,1,0:T(8,128)(2,1)S(1)}, u32[]{:S(2)}, u32[]{:S(2)}) collective-permute-start(bf16[2,20,10,128]{3,2,1,0:T(8,128)(2,1)S(1)} %maximum_select_fusion), channel_id=1, source_target_pairs={{0,4},{1,5},{2,6},{3,7},{4,0},{5,1},{6,2},{7,3},{8,12},{9,13},{10,... | collective-permute-start | bytes 307208 | tf_op jit(solution)/shard_map/ppermute | solution.py:307
  42.1 9.0 %collective-permute-start.6 = (bf16[64,14,128]{2,1,0:T(8,128)(2,1)S(1)}, bf16[64,14,128]{2,1,0:T(8,128)(2,1)S(1)}, u32[]{:S(2)}, u32[]{:S(2)}) collective-permute-start(bf16[64,14,128]{2,1,0:T(8,128)(2,1)S(1)} %all-to-all-done.own), channel_id=1, source_target_pairs={{0,64},{64,0},{128,192},{192,128},{1,65},{65,1},{129,193},{193,129... | collective-permute-start | bytes 688136 | tf_op jit(solution)/shard_map/ppermute | solution.py:282
  46.7 5.5 %collective-permute-start.7 = (bf16[64,14,128]{2,1,0:T(8,128)(2,1)S(1)}, bf16[64,14,128]{2,1,0:T(8,128)(2,1)S(1)}, u32[]{:S(2)}, u32[]{:S(2)}) collective-permute-start(bf16[64,14,128]{2,1,0:T(8,128)(2,1)S(1)} %collective-permute-done.5.chip), channel_id=1, source_target_pairs={{0,64},{64,0},{128,192},{192,128},{1,65},{65,1},{129,193},{193,129... | collective-permute-start | bytes 688136 | tf_op jit(solution)/shard_map/ppermute | solution.py:282
  62.5 2.0 %collective-permute-start.9 = (bf16[64,27,128]{2,1,0:T(8,128)(2,1)S(1)}, bf16[64,27,128]{2,1,0:T(8,128)(2,1)S(1)}, u32[]{:S(2)}, u32[]{:S(2)}) collective-permute-start(bf16[64,27,128]{2,1,0:T(8,128)(2,1)S(1)} %get-tuple-element.28), channel_id=1, source_target_pairs={{0,64},{64,0},{128,192},{192,128},{1,65},{65,1},{129,193},{193,129... | collective-permute-start | bytes 1327112 | tf_op jit(solution)/shard_map/ppermute | solution.py:282
  63.0 9.6 %collective-permute-start.8 = (bf16[2,18,8,128]{3,2,1,0:T(8,128)(2,1)S(1)}, bf16[2,18,8,128]{3,2,1,0:T(8,128)(2,1)S(1)}, u32[]{:S(2)}, u32[]{:S(2)}) collective-permute-start(bf16[2,18,8,128]{3,2,1,0:T(8,128)(2,1)S(1)} %slice_select_fusion), channel_id=1, source_target_pairs={{0,4},{1,5},{2,6},{3,7},{4,0},{5,1},{6,2},{7,3},{8,12},{9,13},{10,... | collective-permute-start | bytes 221192 | tf_op jit(solution)/shard_map/ppermute | solution.py:307
  65.5 26.0 %all-to-all-start.1 = ((bf16[64,27,128]{2,1,0:T(8,128)(2,1)}), bf16[64,27,128]{2,1,0:T(8,128)(2,1)S(1)}, u32[]{:S(2)}, u32[]{:S(2)}) async-start(bf16[64,27,128]{2,1,0:T(8,128)(2,1)} %chip_sum.1.after), calls=%async_computation.1 | async-start | bytes 1048576 | tf_op jit(solution)/shard_map/all_to_all | solution.py:468
  72.9 4.2 %collective-permute-start.10 = (bf16[2,18,10,128]{3,2,1,0:T(8,128)(2,1)S(1)}, bf16[2,18,10,128]{3,2,1,0:T(8,128)(2,1)S(1)}, u32[]{:S(2)}, u32[]{:S(2)}) collective-permute-start(bf16[2,18,10,128]{3,2,1,0:T(8,128)(2,1)S(1)} %get-tuple-element.55), channel_id=1, source_target_pairs={{1,2},{2,1},{5,6},{6,5},{9,10},{10,9},{13,14},{14,13},{17,18},{18,... | collective-permute-start | bytes 276488 | tf_op jit(solution)/shard_map/ppermute | solution.py:272
  73.6 7.1 %collective-permute-start.11 = (bf16[2,18,10,128]{3,2,1,0:T(8,128)(2,1)S(1)}, bf16[2,18,10,128]{3,2,1,0:T(8,128)(2,1)S(1)}, u32[]{:S(2)}, u32[]{:S(2)}) collective-permute-start(bf16[2,18,10,128]{3,2,1,0:T(8,128)(2,1)S(1)} %get-tuple-element.54), channel_id=1, source_target_pairs={{0,1},{1,0},{2,3},{3,2},{4,5},{5,4},{6,7},{7,6},{8,9},{9,8},{10,11... | collective-permute-start | bytes 276488 | tf_op jit(solution)/shard_map/ppermute | solution.py:271
  80.7 16.6 %copy-start.2 = (f32[54,128]{1,0:T(8,128)S(1)}, f32[54,128]{1,0:T(8,128)}, u32[]{:S(2)}) copy-start(f32[54,128]{1,0:T(8,128)} %weight.1) | copy-start | bytes 82948
  80.7 16.6 %copy-start.3 = (f32[54,128]{1,0:T(8,128)S(1)}, f32[54,128]{1,0:T(8,128)}, u32[]{:S(2)}) copy-start(f32[54,128]{1,0:T(8,128)} %param.7) | copy-start | bytes 82948
  80.7 16.6 %copy-start.4 = (f32[54,128]{1,0:T(8,128)S(1)}, f32[54,128]{1,0:T(8,128)}, u32[]{:S(2)}) copy-start(f32[54,128]{1,0:T(8,128)} %param.8) | copy-start | bytes 82948
  91.6 4.0 %collective-permute-start.12 = (f32[27,128]{1,0:T(8,128)S(1)}, f32[27,128]{1,0:T(8,128)S(1)}, u32[]{:S(2)}, u32[]{:S(2)}) collective-permute-start(f32[27,128]{1,0:T(8,128)S(1)} %sum_of_arrived.1), channel_id=1, source_target_pairs={{0,128},{64,192},{128,0},{192,64},{1,129},{65,193},{129,1},{193,65... | collective-permute-start | bytes 41480 | tf_op jit(solution)/shard_map/ppermute | solution.py:286
  91.7 3.9 %collective-permute-start.13 = (f32[27,128]{1,0:T(8,128)S(1)}, f32[27,128]{1,0:T(8,128)S(1)}, u32[]{:S(2)}, u32[]{:S(2)}) collective-permute-start(f32[27,128]{1,0:T(8,128)S(1)} %sum_of_arrived.1), channel_id=1, source_target_pairs={{0,64},{64,0},{128,192},{192,128},{1,65},{65,1},{129,193},{193,129... | collective-permute-start | bytes 41480 | tf_op jit(solution)/shard_map/ppermute | solution.py:282
  94.0 3.2 %collective-permute-start.14 = (f32[27,128]{1,0:T(8,128)S(1)}, f32[27,128]{1,0:T(8,128)S(1)}, u32[]{:S(2)}, u32[]{:S(2)}) collective-permute-start(f32[27,128]{1,0:T(8,128)S(1)} %sum_of_arrived.1), channel_id=1, source_target_pairs={{0,192},{64,128},{128,64},{192,0},{1,193},{65,129},{129,65},{193,1... | collective-permute-start | bytes 41480 | tf_op jit(solution)/shard_map/ppermute | solution.py:290

commit v6 on v5

--- a/solution.py
+++ b/solution.py
@@ -363,27 +363,30 @@
     )(even, member, field, dy, weight)
 
 
-def z_edges_kernel(field, first, last, tall):
+def edges_kernel(field, yfirst, ylast, zfirst, zlast, tall):
     def one(i, _):
         b, x = lax.div(i, 16), lax.rem(i, 16)
-        tall[i] = field[b, x].astype(f32)
-        first[b, x] = tall[i, pl.ds(0, 8, stride=8)].astype(bf16)
-        last[b, x] = tall[i, pl.ds(7, 8, stride=8)].astype(bf16)
+        wide = field[b, x].astype(f32)
+        tall[i] = wide
+        yfirst[b, x] = wide[0:8].astype(bf16)
+        ylast[b, x] = wide[56:64].astype(bf16)
+        zfirst[b, x] = tall[i, pl.ds(0, 8, stride=8)].astype(bf16)
+        zlast[b, x] = tall[i, pl.ds(7, 8, stride=8)].astype(bf16)
         return 0
 
     lax.fori_loop(0, 32, one, 0, unroll=4)
 
 
-def z_edges(field):
+def edges(field):
     edge = jax.ShapeDtypeStruct((2, 16, 8, 128), bf16)
     return pl.pallas_call(
-        z_edges_kernel,
+        edges_kernel,
         in_specs=[VMEM],
-        out_specs=[VMEM] * 2,
-        out_shape=[edge] * 2,
+        out_specs=[VMEM] * 4,
+        out_shape=[edge] * 4,
         scratch_shapes=[pltpu.VMEM((32, 64, 128), f32)],
         compiler_params=pltpu.CompilerParams(vmem_limit_bytes=4 * 2**20),
-        name="z_edges",
+        name="edges",
     )(field)
 
 
@@ -437,15 +440,17 @@
     mine = lax.all_to_all(copies, "space", split_axis=0, concat_axis=0, tiled=True)
     below, above = swapped(inner, outer, even, GY * GZ, groups)
 
+    faces = edges(field)
+
     def along(layers, own):
-        pairs = zip(layers(below[:, :2]), own(field), layers(above[:, :2]))
+        pairs = zip(layers(below[:, :2]), own, layers(above[:, :2]))
         return [jnp.concatenate(three, 1) for three in pairs]
 
-    zlo, zhi = z_halo(*along(z_layers, z_edges))
+    zlo, zhi = z_halo(*along(z_layers, faces[2:]))
     ylo, yhi = y_halo(
         *(
             jnp.concatenate([face, zlo[:, :, at : at + 1], zhi[:, :, at : at + 1]], 2)
-            for at, face in zip((0, 7), along(y_layers, y_layers))
+            for at, face in zip((0, 7), along(y_layers, faces[:2]))
         )
     )
     total = crops * lax.axis_size("sample") * lax.axis_size("space") * nx * ny * nz

time: 98.4 us -> 97.8 us (level)
  transfers between devices with their start and end apart: 17 -> 17, of which waited for: 8 -> 8; matrix products, arithmetic and copies ran while one was open for 3% -> 2% of each run, Pallas kernels for 7% -> 7%
where the time goes in v6:
time: 97.8 us; the launch traced here: 97.3 us
  starting transfers between devices  51 us (52%)
  waiting for transfers between devices  22.2 us (23%)
  Pallas kernels  19.2 us (20%)
  other arithmetic  2.29 us (2%)
  local copies, waits for them, and re-layouts  1.5 us (2%)
  between operations  1.09 us (1%)
    ppermute x3, starting transfers between devices, swapped(): inner = lax.ppermute(inner, 'space', flip_pairs(devices, stride))  16.1 us
    all_to_all x1, starting transfers between devices, local(): lax.all_to_all(copies, 'space', split_axis=0, concat_axis=0, tiled=True)  12.7 us
    ppermute x4, starting transfers between devices, core_swap(): return lax.ppermute(value, 'sample', flip_pairs(lax.axis_size('sample'), 1))  9.58 us
    pallas_call x1, Pallas kernels, forward(): pl.pallas_call(forward_kernel, in_specs=[SMEM] + [VMEM] * len(ins), out_s...  6.92 us
    all_to_all x1, starting transfers between devices, local(): lax.all_to_all(chip, 'space', split_axis=0, concat_axis=0, tiled=True)  6.66 us
    ppermute x3, waiting for transfers between devices, swapped(): inner = lax.ppermute(inner, 'space', flip_pairs(devices, stride))  6.34 us
    all_to_all x1, waiting for transfers between devices, local(): lax.all_to_all(chip, 'space', split_axis=0, concat_axis=0, tiled=True)  5.22 us
    pallas_call x1, Pallas kernels, backward(): pl.pallas_call(backward_kernel, in_specs=[VMEM] * 6, out_specs=[VMEM] * 2...  5.21 us
  transfers between devices with their start and end apart: 17, of which 8 were waited for; matrix products, arithmetic and copies ran while one was open for 2% of the time, Pallas kernels for 7%

profile of v6, /device:TPU:1, one launch (start us, length us, event | category | flops | bytes accessed | tf_op | source)
XLA Modules:
  0.0 97.3 jit_solution(14889767795413655954)
XLA Ops:
  0.7 2.3 %start.1 = (bf16[2,3,64,128]{3,2,1,0:T(8,128)(2,1)}, bf16[2,3,64,128]{3,2,1,0:T(8,128)(2,1)}, bf16[64,14,128]{2,1,0:T(8,128)(2,1)}) custom-call(s32[1]{0:T(128)} %bitcast.2.even_ref, s32[1]{0:T(128)} %bitcast.member_ref, bf16[2,16,64,128]{3,2,1,0:T(8,128)(2,1)} %bitcast.37, bf16[2,16,64,128]{3,2,1,0:T(8,128)(2,1)} %bitcast.46, f32[54,128]{1,0:T(8,128)} %weight.1), custom_call_target="tpu_custom_call" | custom-call | tf_op jit(solution)/shard_map/start/pallas_call | solution.py:351
  3.6 9.1 %collective-permute-start.1 = (bf16[2,3,64,128]{3,2,1,0:T(8,128)(2,1)}, bf16[2,3,64,128]{3,2,1,0:T(8,128)(2,1)S(1)}, u32[]{:S(2)}, u32[]{:S(2)}) collective-permute-start(bf16[2,3,64,128]{3,2,1,0:T(8,128)(2,1)} %get-tuple-element.22), channel_id=1, source_target_pairs={{0,8},{1,9},{2,10},{3,11},{4,12},{5,13},{6,14},{7,15},{8,0},{9,1},... | collective-permute-start | bytes 294920 | tf_op jit(solution)/shard_map/ppermute | solution.py:271
  12.7 12.7 %all-to-all-start = ((bf16[64,14,128]{2,1,0:T(8,128)(2,1)}), bf16[64,14,128]{2,1,0:T(8,128)(2,1)S(1)}, u32[]{:S(2)}, u32[]{:S(2)}) async-start(bf16[64,14,128]{2,1,0:T(8,128)(2,1)} %get-tuple-element.27), calls=%async_computation | async-start | bytes 524288 | tf_op jit(solution)/shard_map/all_to_all | solution.py:440
  25.5 1.0 %copy-done = bf16[2,1,16,8,8,128]{5,4,3,2,1,0:T(8,128)(2,1)S(1)} copy-done((bf16[2,1,16,8,8,128]{5,4,3,2,1,0:T(8,128)(2,1)S(1)}, bf16[2,1,16,8,8,128]{5,4,3,2,1,0:T(8,128)(2,1)}, u32[]{:S(2)}) %copy-start) | copy-done | bytes 524312
  27.8 3.5 %collective-permute-start.3 = (bf16[2,20,8,128]{3,2,1,0:T(8,128)(2,1)S(1)}, bf16[2,20,8,128]{3,2,1,0:T(8,128)(2,1)S(1)}, u32[]{:S(2)}, u32[]{:S(2)}) collective-permute-start(bf16[2,20,8,128]{3,2,1,0:T(8,128)(2,1)S(1)} %get-tuple-element.64), channel_id=1, source_target_pairs={{0,1},{1,0},{2,3},{3,2},{4,5},{5,4},{6,7},{7,6},{8,9},{9,8},{10,11... | collective-permute-start | bytes 245768 | tf_op jit(solution)/shard_map/ppermute | solution.py:271
  31.3 2.7 %collective-permute-done.3 = bf16[2,20,8,128]{3,2,1,0:T(8,128)(2,1)S(1)} collective-permute-done((bf16[2,20,8,128]{3,2,1,0:T(8,128)(2,1)S(1)}, bf16[2,20,8,128]{3,2,1,0:T(8,128)(2,1)S(1)}, u32[]{:S(2)}, u32[]{:S(2)}) %collective-permute-start.3) | collective-permute-done | bytes 81952 | tf_op jit(solution)/shard_map/ppermute | solution.py:271
  34.1 4.7 %all-to-all-done.own = bf16[64,14,128]{2,1,0:T(8,128)(2,1)S(1)} async-done(((bf16[64,14,128]{2,1,0:T(8,128)(2,1)}), bf16[64,14,128]{2,1,0:T(8,128)(2,1)S(1)}, u32[]{:S(2)}, u32[]{:S(2)}) %all-to-all-start) | async-done | bytes 229408 | tf_op jit(solution)/shard_map/all_to_all | solution.py:440
  39.7 1.2 %collective-permute-start.4 = (bf16[2,20,10,128]{3,2,1,0:T(8,128)(2,1)S(1)}, bf16[2,20,10,128]{3,2,1,0:T(8,128)(2,1)S(1)}, u32[]{:S(2)}, u32[]{:S(2)}) collective-permute-start(bf16[2,20,10,128]{3,2,1,0:T(8,128)(2,1)S(1)} %maximum_select_fusion), channel_id=1, source_target_pairs={{0,4},{1,5},{2,6},{3,7},{4,0},{5,1},{6,2},{7,3},{8,12},{9,13},{10,... | collective-permute-start | bytes 307208 | tf_op jit(solution)/shard_map/ppermute | solution.py:307
  41.0 1.1 %pad_maximum_fusion = bf16[2,18,64,128]{3,2,1,0:T(8,128)(2,1)S(1)} fusion(bf16[2,1,64,128]{3,2,1,0:T(8,128)(2,1)S(1)} %slice.117, bf16[2,16,64,128]{3,2,1,0:T(8,128)(2,1)} %bitcast.47, bf16[2,1,64,128]{3,2,1,0:T(8,128)(2,1)S(1)} %slice.116), kind=kLoop, calls=%fused_computation | loop fusion | flops 589824 | bytes 1179648 | tf_op jit(solution)/shard_map/concatenate | solution.py:459
  42.1 2.4 %collective-permute-start.6 = (bf16[64,14,128]{2,1,0:T(8,128)(2,1)S(1)}, bf16[64,14,128]{2,1,0:T(8,128)(2,1)S(1)}, u32[]{:S(2)}, u32[]{:S(2)}) collective-permute-start(bf16[64,14,128]{2,1,0:T(8,128)(2,1)S(1)} %all-to-all-done.own), channel_id=1, source_target_pairs={{0,64},{64,0},{128,192},{192,128},{1,65},{65,1},{129,193},{193,129... | collective-permute-start | bytes 688136 | tf_op jit(solution)/shard_map/ppermute | solution.py:282
  44.5 2.2 %collective-permute-done.5.chip = bf16[64,14,128]{2,1,0:T(8,128)(2,1)S(1)} collective-permute-done((bf16[64,14,128]{2,1,0:T(8,128)(2,1)S(1)}, bf16[64,14,128]{2,1,0:T(8,128)(2,1)S(1)}, u32[]{:S(2)}, u32[]{:S(2)}) %collective-permute-start.5) | collective-permute-done | bytes 229408 | tf_op jit(solution)/shard_map/ppermute | solution.py:286
  46.7 4.4 %collective-permute-start.7 = (bf16[64,14,128]{2,1,0:T(8,128)(2,1)S(1)}, bf16[64,14,128]{2,1,0:T(8,128)(2,1)S(1)}, u32[]{:S(2)}, u32[]{:S(2)}) collective-permute-start(bf16[64,14,128]{2,1,0:T(8,128)(2,1)S(1)} %collective-permute-done.5.chip), channel_id=1, source_target_pairs={{0,64},{64,0},{128,192},{192,128},{1,65},{65,1},{129,193},{193,129... | collective-permute-start | bytes 688136 | tf_op jit(solution)/shard_map/ppermute | solution.py:282
  51.1 1.1 %collective-permute-done.7.slant = bf16[64,14,128]{2,1,0:T(8,128)(2,1)S(1)} collective-permute-done((bf16[64,14,128]{2,1,0:T(8,128)(2,1)S(1)}, bf16[64,14,128]{2,1,0:T(8,128)(2,1)S(1)}, u32[]{:S(2)}, u32[]{:S(2)}) %collective-permute-start.7) | collective-permute-done | bytes 229408 | tf_op jit(solution)/shard_map/ppermute | solution.py:282
  52.2 6.9 %forward.1 = (bf16[2,8,2,64,128]{4,3,2,1,0:T(8,128)(2,1)}, bf16[2,9,2,64,128]{4,3,2,1,0:T(8,128)(2,1)S(1)}, bf16[2,10,2,64,1152]{4,3,2,1,0:T(8,128)(2,1)S(1)}, bf16[3,1152,128]{2,1,0:T(8,128)(2,1)S(1)}) custom-call(s32[1]{0:T(128)} %bitcast.member_ref, bf16[2,16,64,128]{3,2,1,0:T(8,128)(2,1)S(1)} %bitcast.39, ...), custom_call_target="tpu_custom_call" | custom-call | flops 4000000000 | bytes 8000000 | tf_op jit(solution)/shard_map/forward/pallas_call | solution.py:137
  59.1 3.4 %weight_grad_halves.1 = (bf16[64,27,128]{2,1,0:T(8,128)(2,1)S(1)}, bf16[64,27,128]{2,1,0:T(8,128)(2,1)S(1)}) custom-call(s32[1]{0:T(128)} %bitcast.14.core_ref, bf16[2,20,64,1152]{3,2,1,0:T(8,128)(2,1)S(1)} %bitcast.45, bf16[2,18,64,128]{3,2,1,0:T(8,128)(2,1)S(1)} %bitcast.41), custom_call_target="tpu_custom_call" | custom-call | flops 4000000000 | bytes 7000000 | tf_op jit(solution)/shard_map/weight_grad_halves/pallas_call | solution.py:179
  63.6 1.0 collective-permute-done.9.got
  65.5 6.7 %all-to-all-start.1 = ((bf16[64,27,128]{2,1,0:T(8,128)(2,1)}), bf16[64,27,128]{2,1,0:T(8,128)(2,1)S(1)}, u32[]{:S(2)}, u32[]{:S(2)}) async-start(bf16[64,27,128]{2,1,0:T(8,128)(2,1)} %chip_sum.1.after), calls=%async_computation.1 | async-start | bytes 1048576 | tf_op jit(solution)/shard_map/all_to_all | solution.py:473
  73.1 3.5 %collective-permute-start.11 = (bf16[2,18,10,128]{3,2,1,0:T(8,128)(2,1)S(1)}, bf16[2,18,10,128]{3,2,1,0:T(8,128)(2,1)S(1)}, u32[]{:S(2)}, u32[]{:S(2)}) collective-permute-start(bf16[2,18,10,128]{3,2,1,0:T(8,128)(2,1)S(1)} %get-tuple-element.56), channel_id=1, source_target_pairs={{0,1},{1,0},{2,3},{3,2},{4,5},{5,4},{6,7},{7,6},{8,9},{9,8},{10,11... | collective-permute-start | bytes 276488 | tf_op jit(solution)/shard_map/ppermute | solution.py:271
  76.7 3.7 %collective-permute-done.11 = bf16[2,18,10,128]{3,2,1,0:T(8,128)(2,1)S(1)} collective-permute-done((bf16[2,18,10,128]{3,2,1,0:T(8,128)(2,1)S(1)}, bf16[2,18,10,128]{3,2,1,0:T(8,128)(2,1)S(1)}, u32[]{:S(2)}, u32[]{:S(2)}) %collective-permute-start.11) | collective-permute-done | bytes 92192 | tf_op jit(solution)/shard_map/ppermute | solution.py:271
  80.4 5.2 %backward.1 = (bf16[2,8,2,64,128]{4,3,2,1,0:T(8,128)(2,1)}, f32[8,128]{1,0:T(8,128)S(1)}) custom-call(bf16[2,18,64,128]{3,2,1,0:T(8,128)(2,1)S(1)} %bitcast.44, bf16[2,18,8,128]{3,2,1,0:T(8,128)(2,1)S(1)} %get-tuple-element.79.ylo, bf16[2,18,8,128]{3,2,1,0:T(8,128)(2,1)S(1)} %get-tuple-element.78.yhi, bf16[2,18,10,128]{3,2,1,0:T(8,128)(2,1)S(1)} %get-tuple-element.55.zlo, ...), custom_call_target="tpu_custom_call" | custom-call | flops 4000000000 | bytes 3000000 | tf_op jit(solution)/shard_map/backward/pallas_call | solution.py:243
  85.6 5.2 %all-to-all-done.1.arrived = bf16[64,27,128]{2,1,0:T(8,128)(2,1)S(1)} async-done(((bf16[64,27,128]{2,1,0:T(8,128)(2,1)}), bf16[64,27,128]{2,1,0:T(8,128)(2,1)S(1)}, u32[]{:S(2)}, u32[]{:S(2)}) %all-to-all-start.1) | async-done | bytes 442400 | tf_op jit(solution)/shard_map/all_to_all | solution.py:473
  91.1 2.4 %collective-permute-start.13 = (f32[27,128]{1,0:T(8,128)S(1)}, f32[27,128]{1,0:T(8,128)S(1)}, u32[]{:S(2)}, u32[]{:S(2)}) collective-permute-start(f32[27,128]{1,0:T(8,128)S(1)} %sum_of_arrived.1), channel_id=1, source_target_pairs={{0,64},{64,0},{128,192},{192,128},{1,65},{65,1},{129,193},{193,129... | collective-permute-start | bytes 41480 | tf_op jit(solution)/shard_map/ppermute | solution.py:282
  93.4 1.5 %collective-permute-start.14 = (f32[27,128]{1,0:T(8,128)S(1)}, f32[27,128]{1,0:T(8,128)S(1)}, u32[]{:S(2)}, u32[]{:S(2)}) collective-permute-start(f32[27,128]{1,0:T(8,128)S(1)} %sum_of_arrived.1), channel_id=1, source_target_pairs={{0,192},{64,128},{128,64},{192,0},{1,193},{65,129},{129,65},{193,1... | collective-permute-start | bytes 41480 | tf_op jit(solution)/shard_map/ppermute | solution.py:290
  94.9 1.7 %collective-permute-done.14 = f32[27,128]{1,0:T(8,128)S(1)} collective-permute-done((f32[27,128]{1,0:T(8,128)S(1)}, f32[27,128]{1,0:T(8,128)S(1)}, u32[]{:S(2)}, u32[]{:S(2)}) %collective-permute-start.14) | collective-permute-done | bytes 13856 | tf_op jit(solution)/shard_map/ppermute | solution.py:290
  (57 shorter events, 6.6 us)
Async XLA Ops:
  0.6 51.6 %copy-start.1 = (bf16[2,1,16,8,8,128]{5,4,3,2,1,0:T(8,128)(2,1)S(1)}, bf16[2,1,16,8,8,128]{5,4,3,2,1,0:T(8,128)(2,1)}, u32[]{:S(2)}) copy-start(bf16[2,1,16,8,8,128]{5,4,3,2,1,0:T(8,128)(2,1)} %param.5) | copy-start | bytes 1572868
  3.0 23.9 %collective-permute-start = (bf16[2,3,64,128]{3,2,1,0:T(8,128)(2,1)}, bf16[2,3,64,128]{3,2,1,0:T(8,128)(2,1)S(1)}, u32[]{:S(2)}, u32[]{:S(2)}) collective-permute-start(bf16[2,3,64,128]{3,2,1,0:T(8,128)(2,1)} %get-tuple-element.21), channel_id=1, source_target_pairs={{8,16},{9,17},{10,18},{11,19},{12,20},{13,21},{14,22},{15,23},{16,... | collective-permute-start | bytes 294920 | tf_op jit(solution)/shard_map/ppermute | solution.py:272
  3.6 23.2 %collective-permute-start.1 = (bf16[2,3,64,128]{3,2,1,0:T(8,128)(2,1)}, bf16[2,3,64,128]{3,2,1,0:T(8,128)(2,1)S(1)}, u32[]{:S(2)}, u32[]{:S(2)}) collective-permute-start(bf16[2,3,64,128]{3,2,1,0:T(8,128)(2,1)} %get-tuple-element.22), channel_id=1, source_target_pairs={{0,8},{1,9},{2,10},{3,11},{4,12},{5,13},{6,14},{7,15},{8,0},{9,1},... | collective-permute-start | bytes 294920 | tf_op jit(solution)/shard_map/ppermute | solution.py:271
  12.7 26.1 %all-to-all-start = ((bf16[64,14,128]{2,1,0:T(8,128)(2,1)}), bf16[64,14,128]{2,1,0:T(8,128)(2,1)S(1)}, u32[]{:S(2)}, u32[]{:S(2)}) async-start(bf16[64,14,128]{2,1,0:T(8,128)(2,1)} %get-tuple-element.27), calls=%async_computation | async-start | bytes 524288 | tf_op jit(solution)/shard_map/all_to_all | solution.py:440
  25.5 1.0 %copy-start = (bf16[2,1,16,8,8,128]{5,4,3,2,1,0:T(8,128)(2,1)S(1)}, bf16[2,1,16,8,8,128]{5,4,3,2,1,0:T(8,128)(2,1)}, u32[]{:S(2)}) copy-start(bf16[2,1,16,8,8,128]{5,4,3,2,1,0:T(8,128)(2,1)} %param.5) | copy-start | bytes 1572868
  27.1 4.2 %collective-permute-start.2 = (bf16[2,20,8,128]{3,2,1,0:T(8,128)(2,1)S(1)}, bf16[2,20,8,128]{3,2,1,0:T(8,128)(2,1)S(1)}, u32[]{:S(2)}, u32[]{:S(2)}) collective-permute-start(bf16[2,20,8,128]{3,2,1,0:T(8,128)(2,1)S(1)} %get-tuple-element.65), channel_id=1, source_target_pairs={{1,2},{2,1},{5,6},{6,5},{9,10},{10,9},{13,14},{14,13},{17,18},{18,... | collective-permute-start | bytes 245768 | tf_op jit(solution)/shard_map/ppermute | solution.py:272
  27.8 6.2 %collective-permute-start.3 = (bf16[2,20,8,128]{3,2,1,0:T(8,128)(2,1)S(1)}, bf16[2,20,8,128]{3,2,1,0:T(8,128)(2,1)S(1)}, u32[]{:S(2)}, u32[]{:S(2)}) collective-permute-start(bf16[2,20,8,128]{3,2,1,0:T(8,128)(2,1)S(1)} %get-tuple-element.64), channel_id=1, source_target_pairs={{0,1},{1,0},{2,3},{3,2},{4,5},{5,4},{6,7},{7,6},{8,9},{9,8},{10,11... | collective-permute-start | bytes 245768 | tf_op jit(solution)/shard_map/ppermute | solution.py:271
  38.8 7.9 %collective-permute-start.5 = (bf16[64,14,128]{2,1,0:T(8,128)(2,1)S(1)}, bf16[64,14,128]{2,1,0:T(8,128)(2,1)S(1)}, u32[]{:S(2)}, u32[]{:S(2)}) collective-permute-start(bf16[64,14,128]{2,1,0:T(8,128)(2,1)S(1)} %all-to-all-done.own), channel_id=1, source_target_pairs={{0,128},{64,192},{128,0},{192,64},{1,129},{65,193},{129,1},{193,65... | collective-permute-start | bytes 688136 | tf_op jit(solution)/shard_map/ppermute | solution.py:286
  39.7 11.3 %collective-permute-start.4 = (bf16[2,20,10,128]{3,2,1,0:T(8,128)(2,1)S(1)}, bf16[2,20,10,128]{3,2,1,0:T(8,128)(2,1)S(1)}, u32[]{:S(2)}, u32[]{:S(2)}) collective-permute-start(bf16[2,20,10,128]{3,2,1,0:T(8,128)(2,1)S(1)} %maximum_select_fusion), channel_id=1, source_target_pairs={{0,4},{1,5},{2,6},{3,7},{4,0},{5,1},{6,2},{7,3},{8,12},{9,13},{10,... | collective-permute-start | bytes 307208 | tf_op jit(solution)/shard_map/ppermute | solution.py:307
  42.1 9.0 %collective-permute-start.6 = (bf16[64,14,128]{2,1,0:T(8,128)(2,1)S(1)}, bf16[64,14,128]{2,1,0:T(8,128)(2,1)S(1)}, u32[]{:S(2)}, u32[]{:S(2)}) collective-permute-start(bf16[64,14,128]{2,1,0:T(8,128)(2,1)S(1)} %all-to-all-done.own), channel_id=1, source_target_pairs={{0,64},{64,0},{128,192},{192,128},{1,65},{65,1},{129,193},{193,129... | collective-permute-start | bytes 688136 | tf_op jit(solution)/shard_map/ppermute | solution.py:282
  46.7 5.5 %collective-permute-start.7 = (bf16[64,14,128]{2,1,0:T(8,128)(2,1)S(1)}, bf16[64,14,128]{2,1,0:T(8,128)(2,1)S(1)}, u32[]{:S(2)}, u32[]{:S(2)}) collective-permute-start(bf16[64,14,128]{2,1,0:T(8,128)(2,1)S(1)} %collective-permute-done.5.chip), channel_id=1, source_target_pairs={{0,64},{64,0},{128,192},{192,128},{1,65},{65,1},{129,193},{193,129... | collective-permute-start | bytes 688136 | tf_op jit(solution)/shard_map/ppermute | solution.py:282
  62.5 2.0 %collective-permute-start.9 = (bf16[64,27,128]{2,1,0:T(8,128)(2,1)S(1)}, bf16[64,27,128]{2,1,0:T(8,128)(2,1)S(1)}, u32[]{:S(2)}, u32[]{:S(2)}) collective-permute-start(bf16[64,27,128]{2,1,0:T(8,128)(2,1)S(1)} %get-tuple-element.32), channel_id=1, source_target_pairs={{0,64},{64,0},{128,192},{192,128},{1,65},{65,1},{129,193},{193,129... | collective-permute-start | bytes 1327112 | tf_op jit(solution)/shard_map/ppermute | solution.py:282
  63.0 9.1 %collective-permute-start.8 = (bf16[2,18,8,128]{3,2,1,0:T(8,128)(2,1)S(1)}, bf16[2,18,8,128]{3,2,1,0:T(8,128)(2,1)S(1)}, u32[]{:S(2)}, u32[]{:S(2)}) collective-permute-start(bf16[2,18,8,128]{3,2,1,0:T(8,128)(2,1)S(1)} %slice_select_fusion), channel_id=1, source_target_pairs={{0,4},{1,5},{2,6},{3,7},{4,0},{5,1},{6,2},{7,3},{8,12},{9,13},{10,... | collective-permute-start | bytes 221192 | tf_op jit(solution)/shard_map/ppermute | solution.py:307
  65.5 25.4 %all-to-all-start.1 = ((bf16[64,27,128]{2,1,0:T(8,128)(2,1)}), bf16[64,27,128]{2,1,0:T(8,128)(2,1)S(1)}, u32[]{:S(2)}, u32[]{:S(2)}) async-start(bf16[64,27,128]{2,1,0:T(8,128)(2,1)} %chip_sum.1.after), calls=%async_computation.1 | async-start | bytes 1048576 | tf_op jit(solution)/shard_map/all_to_all | solution.py:473
  72.5 4.2 %collective-permute-start.10 = (bf16[2,18,10,128]{3,2,1,0:T(8,128)(2,1)S(1)}, bf16[2,18,10,128]{3,2,1,0:T(8,128)(2,1)S(1)}, u32[]{:S(2)}, u32[]{:S(2)}) collective-permute-start(bf16[2,18,10,128]{3,2,1,0:T(8,128)(2,1)S(1)} %get-tuple-element.57), channel_id=1, source_target_pairs={{1,2},{2,1},{5,6},{6,5},{9,10},{10,9},{13,14},{14,13},{17,18},{18,... | collective-permute-start | bytes 276488 | tf_op jit(solution)/shard_map/ppermute | solution.py:272
  73.1 7.2 %collective-permute-start.11 = (bf16[2,18,10,128]{3,2,1,0:T(8,128)(2,1)S(1)}, bf16[2,18,10,128]{3,2,1,0:T(8,128)(2,1)S(1)}, u32[]{:S(2)}, u32[]{:S(2)}) collective-permute-start(bf16[2,18,10,128]{3,2,1,0:T(8,128)(2,1)S(1)} %get-tuple-element.56), channel_id=1, source_target_pairs={{0,1},{1,0},{2,3},{3,2},{4,5},{5,4},{6,7},{7,6},{8,9},{9,8},{10,11... | collective-permute-start | bytes 276488 | tf_op jit(solution)/shard_map/ppermute | solution.py:271
  80.4 16.3 %copy-start.2 = (f32[54,128]{1,0:T(8,128)S(1)}, f32[54,128]{1,0:T(8,128)}, u32[]{:S(2)}) copy-start(f32[54,128]{1,0:T(8,128)} %weight.1) | copy-start | bytes 82948
  80.4 16.3 %copy-start.3 = (f32[54,128]{1,0:T(8,128)S(1)}, f32[54,128]{1,0:T(8,128)}, u32[]{:S(2)}) copy-start(f32[54,128]{1,0:T(8,128)} %param.7) | copy-start | bytes 82948
  80.4 16.3 %copy-start.4 = (f32[54,128]{1,0:T(8,128)S(1)}, f32[54,128]{1,0:T(8,128)}, u32[]{:S(2)}) copy-start(f32[54,128]{1,0:T(8,128)} %param.8) | copy-start | bytes 82948
  91.0 4.0 %collective-permute-start.12 = (f32[27,128]{1,0:T(8,128)S(1)}, f32[27,128]{1,0:T(8,128)S(1)}, u32[]{:S(2)}, u32[]{:S(2)}) collective-permute-start(f32[27,128]{1,0:T(8,128)S(1)} %sum_of_arrived.1), channel_id=1, source_target_pairs={{0,128},{64,192},{128,0},{192,64},{1,129},{65,193},{129,1},{193,65... | collective-permute-start | bytes 41480 | tf_op jit(solution)/shard_map/ppermute | solution.py:286
  91.1 3.9 %collective-permute-start.13 = (f32[27,128]{1,0:T(8,128)S(1)}, f32[27,128]{1,0:T(8,128)S(1)}, u32[]{:S(2)}, u32[]{:S(2)}) collective-permute-start(f32[27,128]{1,0:T(8,128)S(1)} %sum_of_arrived.1), channel_id=1, source_target_pairs={{0,64},{64,0},{128,192},{192,128},{1,65},{65,1},{129,193},{193,129... | collective-permute-start | bytes 41480 | tf_op jit(solution)/shard_map/ppermute | solution.py:282
  93.4 3.2 %collective-permute-start.14 = (f32[27,128]{1,0:T(8,128)S(1)}, f32[27,128]{1,0:T(8,128)S(1)}, u32[]{:S(2)}, u32[]{:S(2)}) collective-permute-start(f32[27,128]{1,0:T(8,128)S(1)} %sum_of_arrived.1), channel_id=1, source_target_pairs={{0,192},{64,128},{128,64},{192,0},{1,193},{65,129},{129,65},{193,1... | collective-permute-start | bytes 41480 | tf_op jit(solution)/shard_map/ppermute | solution.py:290

commit v7 on v6

--- a/solution.py
+++ b/solution.py
@@ -46,7 +46,7 @@
                 windows[lax.div(at, 2), lax.rem(at, 2), :, col : col + 128] = tile
         return 0
 
-    lax.fori_loop(0, layers, one, 0)
+    lax.fori_loop(0, layers, one, 0, unroll=2)
 
 
 def z_first_source(b, center, zlo, zhi, ylo, yhi, ahead=0):
@@ -98,7 +98,7 @@
             rows[pl.ds(54 * s + first, 14), :] = quarter[s].astype(f32)
         return 0
 
-    lax.fori_loop(0, 64, piece, 0)
+    lax.fori_loop(0, 64, piece, 0, unroll=4)
     for kx in range(3):
         kern[kx] = rows[1152 * kx : 1152 * (kx + 1), :].astype(bf16)
     pair_kernels(kern, wide)
@@ -171,7 +171,7 @@
         leaves[s] = jnp.where(core == 0, high, low).astype(bf16)
         return 0
 
-    lax.fori_loop(0, 64, piece, 0)
+    lax.fori_loop(0, 64, piece, 0, unroll=4)
 
 
 def weight_grad_halves(core, windows, dz, scale):

time: 97.8 us -> 97 us (level)
  no operation moved by 1% of the time
where the time goes in v7:
time: 97 us; the launch traced here: 96.6 us
  starting transfers between devices  51 us (53%)
  waiting for transfers between devices  22.3 us (23%)
  Pallas kernels  18.4 us (19%)
  other arithmetic  2.29 us (2%)
  local copies, waits for them, and re-layouts  1.5 us (2%)
  between operations  1.09 us (1%)
    ppermute x3, starting transfers between devices, swapped(): inner = lax.ppermute(inner, 'space', flip_pairs(devices, stride))  16.1 us
    all_to_all x1, starting transfers between devices, local(): lax.all_to_all(copies, 'space', split_axis=0, concat_axis=0, tiled=True)  12.7 us
    ppermute x4, starting transfers between devices, core_swap(): return lax.ppermute(value, 'sample', flip_pairs(lax.axis_size('sample'), 1))  9.57 us
    all_to_all x1, starting transfers between devices, local(): lax.all_to_all(chip, 'space', split_axis=0, concat_axis=0, tiled=True)  6.66 us
    pallas_call x1, Pallas kernels, forward(): pl.pallas_call(forward_kernel, in_specs=[SMEM] + [VMEM] * len(ins), out_s...  6.42 us
    ppermute x3, waiting for transfers between devices, swapped(): inner = lax.ppermute(inner, 'space', flip_pairs(devices, stride))  6.36 us
    all_to_all x1, waiting for transfers between devices, local(): lax.all_to_all(chip, 'space', split_axis=0, concat_axis=0, tiled=True)  5.21 us
    pallas_call x1, Pallas kernels, backward(): pl.pallas_call(backward_kernel, in_specs=[VMEM] * 6, out_specs=[VMEM] * 2...  5.2 us
  transfers between devices with their start and end apart: 17, of which 8 were waited for; matrix products, arithmetic and copies ran while one was open for 2% of the time, Pallas kernels for 7%

profile of v7, /device:TPU:1, one launch (start us, length us, event | category | flops | bytes accessed | tf_op | source)
XLA Modules:
  0.0 96.6 jit_solution(6986430475031212429)
XLA Ops:
  0.7 2.3 %start.1 = (bf16[2,3,64,128]{3,2,1,0:T(8,128)(2,1)}, bf16[2,3,64,128]{3,2,1,0:T(8,128)(2,1)}, bf16[64,14,128]{2,1,0:T(8,128)(2,1)}) custom-call(s32[1]{0:T(128)} %bitcast.2.even_ref, s32[1]{0:T(128)} %bitcast.member_ref, bf16[2,16,64,128]{3,2,1,0:T(8,128)(2,1)} %bitcast.37, bf16[2,16,64,128]{3,2,1,0:T(8,128)(2,1)} %bitcast.46, f32[54,128]{1,0:T(8,128)} %weight.1), custom_call_target="tpu_custom_call" | custom-call | tf_op jit(solution)/shard_map/start/pallas_call | solution.py:351
  3.6 9.1 %collective-permute-start.1 = (bf16[2,3,64,128]{3,2,1,0:T(8,128)(2,1)}, bf16[2,3,64,128]{3,2,1,0:T(8,128)(2,1)S(1)}, u32[]{:S(2)}, u32[]{:S(2)}) collective-permute-start(bf16[2,3,64,128]{3,2,1,0:T(8,128)(2,1)} %get-tuple-element.22), channel_id=1, source_target_pairs={{0,8},{1,9},{2,10},{3,11},{4,12},{5,13},{6,14},{7,15},{8,0},{9,1},... | collective-permute-start | bytes 294920 | tf_op jit(solution)/shard_map/ppermute | solution.py:271
  12.7 12.7 %all-to-all-start = ((bf16[64,14,128]{2,1,0:T(8,128)(2,1)}), bf16[64,14,128]{2,1,0:T(8,128)(2,1)S(1)}, u32[]{:S(2)}, u32[]{:S(2)}) async-start(bf16[64,14,128]{2,1,0:T(8,128)(2,1)} %get-tuple-element.27), calls=%async_computation | async-start | bytes 524288 | tf_op jit(solution)/shard_map/all_to_all | solution.py:440
  25.5 1.0 %copy-done = bf16[2,1,16,8,8,128]{5,4,3,2,1,0:T(8,128)(2,1)S(1)} copy-done((bf16[2,1,16,8,8,128]{5,4,3,2,1,0:T(8,128)(2,1)S(1)}, bf16[2,1,16,8,8,128]{5,4,3,2,1,0:T(8,128)(2,1)}, u32[]{:S(2)}) %copy-start) | copy-done | bytes 524312
  27.8 3.5 %collective-permute-start.3 = (bf16[2,20,8,128]{3,2,1,0:T(8,128)(2,1)S(1)}, bf16[2,20,8,128]{3,2,1,0:T(8,128)(2,1)S(1)}, u32[]{:S(2)}, u32[]{:S(2)}) collective-permute-start(bf16[2,20,8,128]{3,2,1,0:T(8,128)(2,1)S(1)} %get-tuple-element.64), channel_id=1, source_target_pairs={{0,1},{1,0},{2,3},{3,2},{4,5},{5,4},{6,7},{7,6},{8,9},{9,8},{10,11... | collective-permute-start | bytes 245768 | tf_op jit(solution)/shard_map/ppermute | solution.py:271
  31.3 2.7 %collective-permute-done.3 = bf16[2,20,8,128]{3,2,1,0:T(8,128)(2,1)S(1)} collective-permute-done((bf16[2,20,8,128]{3,2,1,0:T(8,128)(2,1)S(1)}, bf16[2,20,8,128]{3,2,1,0:T(8,128)(2,1)S(1)}, u32[]{:S(2)}, u32[]{:S(2)}) %collective-permute-start.3) | collective-permute-done | bytes 81952 | tf_op jit(solution)/shard_map/ppermute | solution.py:271
  34.1 4.7 %all-to-all-done.own = bf16[64,14,128]{2,1,0:T(8,128)(2,1)S(1)} async-done(((bf16[64,14,128]{2,1,0:T(8,128)(2,1)}), bf16[64,14,128]{2,1,0:T(8,128)(2,1)S(1)}, u32[]{:S(2)}, u32[]{:S(2)}) %all-to-all-start) | async-done | bytes 229408 | tf_op jit(solution)/shard_map/all_to_all | solution.py:440
  39.7 1.2 %collective-permute-start.4 = (bf16[2,20,10,128]{3,2,1,0:T(8,128)(2,1)S(1)}, bf16[2,20,10,128]{3,2,1,0:T(8,128)(2,1)S(1)}, u32[]{:S(2)}, u32[]{:S(2)}) collective-permute-start(bf16[2,20,10,128]{3,2,1,0:T(8,128)(2,1)S(1)} %maximum_select_fusion), channel_id=1, source_target_pairs={{0,4},{1,5},{2,6},{3,7},{4,0},{5,1},{6,2},{7,3},{8,12},{9,13},{10,... | collective-permute-start | bytes 307208 | tf_op jit(solution)/shard_map/ppermute | solution.py:307
  41.0 1.1 %pad_maximum_fusion = bf16[2,18,64,128]{3,2,1,0:T(8,128)(2,1)S(1)} fusion(bf16[2,1,64,128]{3,2,1,0:T(8,128)(2,1)S(1)} %slice.117, bf16[2,16,64,128]{3,2,1,0:T(8,128)(2,1)} %bitcast.47, bf16[2,1,64,128]{3,2,1,0:T(8,128)(2,1)S(1)} %slice.116), kind=kLoop, calls=%fused_computation | loop fusion | flops 589824 | bytes 1179648 | tf_op jit(solution)/shard_map/concatenate | solution.py:459
  42.1 2.4 %collective-permute-start.6 = (bf16[64,14,128]{2,1,0:T(8,128)(2,1)S(1)}, bf16[64,14,128]{2,1,0:T(8,128)(2,1)S(1)}, u32[]{:S(2)}, u32[]{:S(2)}) collective-permute-start(bf16[64,14,128]{2,1,0:T(8,128)(2,1)S(1)} %all-to-all-done.own), channel_id=1, source_target_pairs={{0,64},{64,0},{128,192},{192,128},{1,65},{65,1},{129,193},{193,129... | collective-permute-start | bytes 688136 | tf_op jit(solution)/shard_map/ppermute | solution.py:282
  44.5 2.2 %collective-permute-done.5.chip = bf16[64,14,128]{2,1,0:T(8,128)(2,1)S(1)} collective-permute-done((bf16[64,14,128]{2,1,0:T(8,128)(2,1)S(1)}, bf16[64,14,128]{2,1,0:T(8,128)(2,1)S(1)}, u32[]{:S(2)}, u32[]{:S(2)}) %collective-permute-start.5) | collective-permute-done | bytes 229408 | tf_op jit(solution)/shard_map/ppermute | solution.py:286
  46.7 4.4 %collective-permute-start.7 = (bf16[64,14,128]{2,1,0:T(8,128)(2,1)S(1)}, bf16[64,14,128]{2,1,0:T(8,128)(2,1)S(1)}, u32[]{:S(2)}, u32[]{:S(2)}) collective-permute-start(bf16[64,14,128]{2,1,0:T(8,128)(2,1)S(1)} %collective-permute-done.5.chip), channel_id=1, source_target_pairs={{0,64},{64,0},{128,192},{192,128},{1,65},{65,1},{129,193},{193,129... | collective-permute-start | bytes 688136 | tf_op jit(solution)/shard_map/ppermute | solution.py:282
  51.1 1.1 %collective-permute-done.7.slant = bf16[64,14,128]{2,1,0:T(8,128)(2,1)S(1)} collective-permute-done((bf16[64,14,128]{2,1,0:T(8,128)(2,1)S(1)}, bf16[64,14,128]{2,1,0:T(8,128)(2,1)S(1)}, u32[]{:S(2)}, u32[]{:S(2)}) %collective-permute-start.7) | collective-permute-done | bytes 229408 | tf_op jit(solution)/shard_map/ppermute | solution.py:282
  52.2 6.4 %forward.1 = (bf16[2,8,2,64,128]{4,3,2,1,0:T(8,128)(2,1)}, bf16[2,9,2,64,128]{4,3,2,1,0:T(8,128)(2,1)S(1)}, bf16[2,10,2,64,1152]{4,3,2,1,0:T(8,128)(2,1)S(1)}, bf16[3,1152,128]{2,1,0:T(8,128)(2,1)S(1)}) custom-call(s32[1]{0:T(128)} %bitcast.member_ref, bf16[2,16,64,128]{3,2,1,0:T(8,128)(2,1)S(1)} %bitcast.39, ...), custom_call_target="tpu_custom_call" | custom-call | flops 4000000000 | bytes 8000000 | tf_op jit(solution)/shard_map/forward/pallas_call | solution.py:137
  58.6 3.2 %weight_grad_halves.1 = (bf16[64,27,128]{2,1,0:T(8,128)(2,1)S(1)}, bf16[64,27,128]{2,1,0:T(8,128)(2,1)S(1)}) custom-call(s32[1]{0:T(128)} %bitcast.14.core_ref, bf16[2,20,64,1152]{3,2,1,0:T(8,128)(2,1)S(1)} %bitcast.45, bf16[2,18,64,128]{3,2,1,0:T(8,128)(2,1)S(1)} %bitcast.41), custom_call_target="tpu_custom_call" | custom-call | flops 4000000000 | bytes 7000000 | tf_op jit(solution)/shard_map/weight_grad_halves/pallas_call | solution.py:179
  62.8 1.0 collective-permute-done.9.got
  64.7 6.7 %all-to-all-start.1 = ((bf16[64,27,128]{2,1,0:T(8,128)(2,1)}), bf16[64,27,128]{2,1,0:T(8,128)(2,1)S(1)}, u32[]{:S(2)}, u32[]{:S(2)}) async-start(bf16[64,27,128]{2,1,0:T(8,128)(2,1)} %chip_sum.1.after), calls=%async_computation.1 | async-start | bytes 1048576 | tf_op jit(solution)/shard_map/all_to_all | solution.py:473
  72.4 3.5 %collective-permute-start.11 = (bf16[2,18,10,128]{3,2,1,0:T(8,128)(2,1)S(1)}, bf16[2,18,10,128]{3,2,1,0:T(8,128)(2,1)S(1)}, u32[]{:S(2)}, u32[]{:S(2)}) collective-permute-start(bf16[2,18,10,128]{3,2,1,0:T(8,128)(2,1)S(1)} %get-tuple-element.56), channel_id=1, source_target_pairs={{0,1},{1,0},{2,3},{3,2},{4,5},{5,4},{6,7},{7,6},{8,9},{9,8},{10,11... | collective-permute-start | bytes 276488 | tf_op jit(solution)/shard_map/ppermute | solution.py:271
  75.9 3.7 %collective-permute-done.11 = bf16[2,18,10,128]{3,2,1,0:T(8,128)(2,1)S(1)} collective-permute-done((bf16[2,18,10,128]{3,2,1,0:T(8,128)(2,1)S(1)}, bf16[2,18,10,128]{3,2,1,0:T(8,128)(2,1)S(1)}, u32[]{:S(2)}, u32[]{:S(2)}) %collective-permute-start.11) | collective-permute-done | bytes 92192 | tf_op jit(solution)/shard_map/ppermute | solution.py:271
  79.7 5.2 %backward.1 = (bf16[2,8,2,64,128]{4,3,2,1,0:T(8,128)(2,1)}, f32[8,128]{1,0:T(8,128)S(1)}) custom-call(bf16[2,18,64,128]{3,2,1,0:T(8,128)(2,1)S(1)} %bitcast.44, bf16[2,18,8,128]{3,2,1,0:T(8,128)(2,1)S(1)} %get-tuple-element.79.ylo, bf16[2,18,8,128]{3,2,1,0:T(8,128)(2,1)S(1)} %get-tuple-element.78.yhi, bf16[2,18,10,128]{3,2,1,0:T(8,128)(2,1)S(1)} %get-tuple-element.55.zlo, ...), custom_call_target="tpu_custom_call" | custom-call | flops 4000000000 | bytes 3000000 | tf_op jit(solution)/shard_map/backward/pallas_call | solution.py:243
  84.9 5.2 %all-to-all-done.1.arrived = bf16[64,27,128]{2,1,0:T(8,128)(2,1)S(1)} async-done(((bf16[64,27,128]{2,1,0:T(8,128)(2,1)}), bf16[64,27,128]{2,1,0:T(8,128)(2,1)S(1)}, u32[]{:S(2)}, u32[]{:S(2)}) %all-to-all-start.1) | async-done | bytes 442400 | tf_op jit(solution)/shard_map/all_to_all | solution.py:473
  90.3 2.4 %collective-permute-start.13 = (f32[27,128]{1,0:T(8,128)S(1)}, f32[27,128]{1,0:T(8,128)S(1)}, u32[]{:S(2)}, u32[]{:S(2)}) collective-permute-start(f32[27,128]{1,0:T(8,128)S(1)} %sum_of_arrived.1), channel_id=1, source_target_pairs={{0,64},{64,0},{128,192},{192,128},{1,65},{65,1},{129,193},{193,129... | collective-permute-start | bytes 41480 | tf_op jit(solution)/shard_map/ppermute | solution.py:282
  92.6 1.5 %collective-permute-start.14 = (f32[27,128]{1,0:T(8,128)S(1)}, f32[27,128]{1,0:T(8,128)S(1)}, u32[]{:S(2)}, u32[]{:S(2)}) collective-permute-start(f32[27,128]{1,0:T(8,128)S(1)} %sum_of_arrived.1), channel_id=1, source_target_pairs={{0,192},{64,128},{128,64},{192,0},{1,193},{65,129},{129,65},{193,1... | collective-permute-start | bytes 41480 | tf_op jit(solution)/shard_map/ppermute | solution.py:290
  94.2 1.7 %collective-permute-done.14 = f32[27,128]{1,0:T(8,128)S(1)} collective-permute-done((f32[27,128]{1,0:T(8,128)S(1)}, f32[27,128]{1,0:T(8,128)S(1)}, u32[]{:S(2)}, u32[]{:S(2)}) %collective-permute-start.14) | collective-permute-done | bytes 13856 | tf_op jit(solution)/shard_map/ppermute | solution.py:290
  (57 shorter events, 6.6 us)
Async XLA Ops:
  0.6 51.6 %copy-start.1 = (bf16[2,1,16,8,8,128]{5,4,3,2,1,0:T(8,128)(2,1)S(1)}, bf16[2,1,16,8,8,128]{5,4,3,2,1,0:T(8,128)(2,1)}, u32[]{:S(2)}) copy-start(bf16[2,1,16,8,8,128]{5,4,3,2,1,0:T(8,128)(2,1)} %param.5) | copy-start | bytes 1572868
  3.0 23.9 %collective-permute-start = (bf16[2,3,64,128]{3,2,1,0:T(8,128)(2,1)}, bf16[2,3,64,128]{3,2,1,0:T(8,128)(2,1)S(1)}, u32[]{:S(2)}, u32[]{:S(2)}) collective-permute-start(bf16[2,3,64,128]{3,2,1,0:T(8,128)(2,1)} %get-tuple-element.21), channel_id=1, source_target_pairs={{8,16},{9,17},{10,18},{11,19},{12,20},{13,21},{14,22},{15,23},{16,... | collective-permute-start | bytes 294920 | tf_op jit(solution)/shard_map/ppermute | solution.py:272
  3.6 23.2 %collective-permute-start.1 = (bf16[2,3,64,128]{3,2,1,0:T(8,128)(2,1)}, bf16[2,3,64,128]{3,2,1,0:T(8,128)(2,1)S(1)}, u32[]{:S(2)}, u32[]{:S(2)}) collective-permute-start(bf16[2,3,64,128]{3,2,1,0:T(8,128)(2,1)} %get-tuple-element.22), channel_id=1, source_target_pairs={{0,8},{1,9},{2,10},{3,11},{4,12},{5,13},{6,14},{7,15},{8,0},{9,1},... | collective-permute-start | bytes 294920 | tf_op jit(solution)/shard_map/ppermute | solution.py:271
  12.7 26.1 %all-to-all-start = ((bf16[64,14,128]{2,1,0:T(8,128)(2,1)}), bf16[64,14,128]{2,1,0:T(8,128)(2,1)S(1)}, u32[]{:S(2)}, u32[]{:S(2)}) async-start(bf16[64,14,128]{2,1,0:T(8,128)(2,1)} %get-tuple-element.27), calls=%async_computation | async-start | bytes 524288 | tf_op jit(solution)/shard_map/all_to_all | solution.py:440
  25.5 1.0 %copy-start = (bf16[2,1,16,8,8,128]{5,4,3,2,1,0:T(8,128)(2,1)S(1)}, bf16[2,1,16,8,8,128]{5,4,3,2,1,0:T(8,128)(2,1)}, u32[]{:S(2)}) copy-start(bf16[2,1,16,8,8,128]{5,4,3,2,1,0:T(8,128)(2,1)} %param.5) | copy-start | bytes 1572868
  27.1 4.2 %collective-permute-start.2 = (bf16[2,20,8,128]{3,2,1,0:T(8,128)(2,1)S(1)}, bf16[2,20,8,128]{3,2,1,0:T(8,128)(2,1)S(1)}, u32[]{:S(2)}, u32[]{:S(2)}) collective-permute-start(bf16[2,20,8,128]{3,2,1,0:T(8,128)(2,1)S(1)} %get-tuple-element.65), channel_id=1, source_target_pairs={{1,2},{2,1},{5,6},{6,5},{9,10},{10,9},{13,14},{14,13},{17,18},{18,... | collective-permute-start | bytes 245768 | tf_op jit(solution)/shard_map/ppermute | solution.py:272
  27.8 6.2 %collective-permute-start.3 = (bf16[2,20,8,128]{3,2,1,0:T(8,128)(2,1)S(1)}, bf16[2,20,8,128]{3,2,1,0:T(8,128)(2,1)S(1)}, u32[]{:S(2)}, u32[]{:S(2)}) collective-permute-start(bf16[2,20,8,128]{3,2,1,0:T(8,128)(2,1)S(1)} %get-tuple-element.64), channel_id=1, source_target_pairs={{0,1},{1,0},{2,3},{3,2},{4,5},{5,4},{6,7},{7,6},{8,9},{9,8},{10,11... | collective-permute-start | bytes 245768 | tf_op jit(solution)/shard_map/ppermute | solution.py:271
  38.8 7.9 %collective-permute-start.5 = (bf16[64,14,128]{2,1,0:T(8,128)(2,1)S(1)}, bf16[64,14,128]{2,1,0:T(8,128)(2,1)S(1)}, u32[]{:S(2)}, u32[]{:S(2)}) collective-permute-start(bf16[64,14,128]{2,1,0:T(8,128)(2,1)S(1)} %all-to-all-done.own), channel_id=1, source_target_pairs={{0,128},{64,192},{128,0},{192,64},{1,129},{65,193},{129,1},{193,65... | collective-permute-start | bytes 688136 | tf_op jit(solution)/shard_map/ppermute | solution.py:286
  39.7 11.3 %collective-permute-start.4 = (bf16[2,20,10,128]{3,2,1,0:T(8,128)(2,1)S(1)}, bf16[2,20,10,128]{3,2,1,0:T(8,128)(2,1)S(1)}, u32[]{:S(2)}, u32[]{:S(2)}) collective-permute-start(bf16[2,20,10,128]{3,2,1,0:T(8,128)(2,1)S(1)} %maximum_select_fusion), channel_id=1, source_target_pairs={{0,4},{1,5},{2,6},{3,7},{4,0},{5,1},{6,2},{7,3},{8,12},{9,13},{10,... | collective-permute-start | bytes 307208 | tf_op jit(solution)/shard_map/ppermute | solution.py:307
  42.1 9.0 %collective-permute-start.6 = (bf16[64,14,128]{2,1,0:T(8,128)(2,1)S(1)}, bf16[64,14,128]{2,1,0:T(8,128)(2,1)S(1)}, u32[]{:S(2)}, u32[]{:S(2)}) collective-permute-start(bf16[64,14,128]{2,1,0:T(8,128)(2,1)S(1)} %all-to-all-done.own), channel_id=1, source_target_pairs={{0,64},{64,0},{128,192},{192,128},{1,65},{65,1},{129,193},{193,129... | collective-permute-start | bytes 688136 | tf_op jit(solution)/shard_map/ppermute | solution.py:282
  46.7 5.5 %collective-permute-start.7 = (bf16[64,14,128]{2,1,0:T(8,128)(2,1)S(1)}, bf16[64,14,128]{2,1,0:T(8,128)(2,1)S(1)}, u32[]{:S(2)}, u32[]{:S(2)}) collective-permute-start(bf16[64,14,128]{2,1,0:T(8,128)(2,1)S(1)} %collective-permute-done.5.chip), channel_id=1, source_target_pairs={{0,64},{64,0},{128,192},{192,128},{1,65},{65,1},{129,193},{193,129... | collective-permute-start | bytes 688136 | tf_op jit(solution)/shard_map/ppermute | solution.py:282
  61.8 2.0 %collective-permute-start.9 = (bf16[64,27,128]{2,1,0:T(8,128)(2,1)S(1)}, bf16[64,27,128]{2,1,0:T(8,128)(2,1)S(1)}, u32[]{:S(2)}, u32[]{:S(2)}) collective-permute-start(bf16[64,27,128]{2,1,0:T(8,128)(2,1)S(1)} %get-tuple-element.32), channel_id=1, source_target_pairs={{0,64},{64,0},{128,192},{192,128},{1,65},{65,1},{129,193},{193,129... | collective-permute-start | bytes 1327112 | tf_op jit(solution)/shard_map/ppermute | solution.py:282
  62.3 9.1 %collective-permute-start.8 = (bf16[2,18,8,128]{3,2,1,0:T(8,128)(2,1)S(1)}, bf16[2,18,8,128]{3,2,1,0:T(8,128)(2,1)S(1)}, u32[]{:S(2)}, u32[]{:S(2)}) collective-permute-start(bf16[2,18,8,128]{3,2,1,0:T(8,128)(2,1)S(1)} %slice_select_fusion), channel_id=1, source_target_pairs={{0,4},{1,5},{2,6},{3,7},{4,0},{5,1},{6,2},{7,3},{8,12},{9,13},{10,... | collective-permute-start | bytes 221192 | tf_op jit(solution)/shard_map/ppermute | solution.py:307
  64.7 25.4 %all-to-all-start.1 = ((bf16[64,27,128]{2,1,0:T(8,128)(2,1)}), bf16[64,27,128]{2,1,0:T(8,128)(2,1)S(1)}, u32[]{:S(2)}, u32[]{:S(2)}) async-start(bf16[64,27,128]{2,1,0:T(8,128)(2,1)} %chip_sum.1.after), calls=%async_computation.1 | async-start | bytes 1048576 | tf_op jit(solution)/shard_map/all_to_all | solution.py:473
  71.7 4.2 %collective-permute-start.10 = (bf16[2,18,10,128]{3,2,1,0:T(8,128)(2,1)S(1)}, bf16[2,18,10,128]{3,2,1,0:T(8,128)(2,1)S(1)}, u32[]{:S(2)}, u32[]{:S(2)}) collective-permute-start(bf16[2,18,10,128]{3,2,1,0:T(8,128)(2,1)S(1)} %get-tuple-element.57), channel_id=1, source_target_pairs={{1,2},{2,1},{5,6},{6,5},{9,10},{10,9},{13,14},{14,13},{17,18},{18,... | collective-permute-start | bytes 276488 | tf_op jit(solution)/shard_map/ppermute | solution.py:272
  72.4 7.2 %collective-permute-start.11 = (bf16[2,18,10,128]{3,2,1,0:T(8,128)(2,1)S(1)}, bf16[2,18,10,128]{3,2,1,0:T(8,128)(2,1)S(1)}, u32[]{:S(2)}, u32[]{:S(2)}) collective-permute-start(bf16[2,18,10,128]{3,2,1,0:T(8,128)(2,1)S(1)} %get-tuple-element.56), channel_id=1, source_target_pairs={{0,1},{1,0},{2,3},{3,2},{4,5},{5,4},{6,7},{7,6},{8,9},{9,8},{10,11... | collective-permute-start | bytes 276488 | tf_op jit(solution)/shard_map/ppermute | solution.py:271
  79.6 16.3 %copy-start.2 = (f32[54,128]{1,0:T(8,128)S(1)}, f32[54,128]{1,0:T(8,128)}, u32[]{:S(2)}) copy-start(f32[54,128]{1,0:T(8,128)} %weight.1) | copy-start | bytes 82948
  79.6 16.3 %copy-start.3 = (f32[54,128]{1,0:T(8,128)S(1)}, f32[54,128]{1,0:T(8,128)}, u32[]{:S(2)}) copy-start(f32[54,128]{1,0:T(8,128)} %param.7) | copy-start | bytes 82948
  79.6 16.3 %copy-start.4 = (f32[54,128]{1,0:T(8,128)S(1)}, f32[54,128]{1,0:T(8,128)}, u32[]{:S(2)}) copy-start(f32[54,128]{1,0:T(8,128)} %param.8) | copy-start | bytes 82948
  90.2 4.0 %collective-permute-start.12 = (f32[27,128]{1,0:T(8,128)S(1)}, f32[27,128]{1,0:T(8,128)S(1)}, u32[]{:S(2)}, u32[]{:S(2)}) collective-permute-start(f32[27,128]{1,0:T(8,128)S(1)} %sum_of_arrived.1), channel_id=1, source_target_pairs={{0,128},{64,192},{128,0},{192,64},{1,129},{65,193},{129,1},{193,65... | collective-permute-start | bytes 41480 | tf_op jit(solution)/shard_map/ppermute | solution.py:286
  90.3 3.9 %collective-permute-start.13 = (f32[27,128]{1,0:T(8,128)S(1)}, f32[27,128]{1,0:T(8,128)S(1)}, u32[]{:S(2)}, u32[]{:S(2)}) collective-permute-start(f32[27,128]{1,0:T(8,128)S(1)} %sum_of_arrived.1), channel_id=1, source_target_pairs={{0,64},{64,0},{128,192},{192,128},{1,65},{65,1},{129,193},{193,129... | collective-permute-start | bytes 41480 | tf_op jit(solution)/shard_map/ppermute | solution.py:282
  92.6 3.2 %collective-permute-start.14 = (f32[27,128]{1,0:T(8,128)S(1)}, f32[27,128]{1,0:T(8,128)S(1)}, u32[]{:S(2)}, u32[]{:S(2)}) collective-permute-start(f32[27,128]{1,0:T(8,128)S(1)} %sum_of_arrived.1), channel_id=1, source_target_pairs={{0,192},{64,128},{128,64},{192,0},{1,193},{65,129},{129,65},{193,1... | collective-permute-start | bytes 41480 | tf_op jit(solution)/shard_map/ppermute | solution.py:290
